TPU v7x, 32 devices: a whole 2x2x4 slice. The times are simulated.
32 devices in a mesh: grp: 4 (over y, x), band: 8 (over z, core).
Axes of the slice: x: 2, y: 2, z: 4, core: 2. Of those that a mesh axis runs over, the one named last changes fastest.
Arguments:
- probes: bfloat16 [32, 1, 4320, 128], P(('grp', 'band')), may hold values from -6 to 6
- kernel: bfloat16 [32, 5, 1, 289], P(('grp', 'band')), may hold values from -0.375 to 0.375
- pair_station: int32 [32, 5], P(('grp', 'band')), may hold values from 0 to 7, as said below
- pair_count: int32 [32], P(('grp', 'band')), may hold values from 1 to 5, as said below
Outputs:
- basis: float32 [32, 4320, 128], P('grp', 'band')
Inputs may be any that keep to these rules, and one draw needn't show every extreme that they name: `pair_station`: slot 0 of source row r names the station row r mod 8; every other slot names a station row within 3 of it, counted cyclically within the super-band. `pair_count`: rows nearer either end of the latitude range tend to use more pair slots.
All inputs are finite; a program needn't handle non-finite values.
Results may differ from a plain program's by a relative error of at most 0.003.
Values may be sent and summed in bfloat16 or wider, within the bound.
No kernel may reach another device: no remote copies, remote signals or barrier semaphores. Data moves between devices by JAX's collectives and lax.ppermute only.
A program may use at most 128 MiB of HBM per device.

v0:
```python
import jax
import jax.numpy as jnp
from jax import lax
from jax.sharding import PartitionSpec as P


def swapped(value, axis, distance):
    mask = 2**distance
    pairs = [(source, source ^ mask) for source in range(lax.axis_size(axis))]
    return lax.ppermute(value, axis, pairs)


def lag_matrix(pair_taps, row_count, col_count, half_width):
    row_ids = lax.broadcasted_iota(jnp.int32, (row_count, col_count), 0)
    col_ids = lax.broadcasted_iota(jnp.int32, (row_count, col_count), 1)
    offset = col_ids - row_ids
    inside = jnp.logical_and(offset >= 0, offset <= 2 * half_width)
    picked = jnp.take(pair_taps, jnp.clip(offset, 0, 2 * half_width), axis=-1)
    return jnp.where(inside, picked, jnp.zeros_like(picked))


def merge_factors(factor_low, partner):
    dims = (((1,), (1,)), ((), ()))
    own_gram = lax.dot_general(
        factor_low,
        factor_low,
        dims,
        precision=lax.Precision.HIGHEST,
        preferred_element_type=jnp.float32,
    )
    other_gram = lax.dot_general(
        partner, partner, dims, precision=lax.Precision.HIGHEST, preferred_element_type=jnp.float32
    )
    return jnp.linalg.cholesky(own_gram + other_gram)


def local(probes, kernel, pair_station, pair_count):
    source = probes[0]
    layers, length, probe_count = source.shape
    band_size = lax.axis_size("band")
    segment = length // band_size
    taps_all = kernel[0]
    slots = taps_all.shape[0]
    half_width = (taps_all.shape[2] - 1) // 2
    live_pairs = pair_count[0]
    blocks = source.reshape(layers, length // half_width, half_width, probe_count)
    shifted = jnp.concatenate(
        [jnp.roll(blocks, 1, axis=1), blocks, jnp.roll(blocks, -1, axis=1)], axis=2
    )
    slot_ids = lax.broadcasted_iota(jnp.int32, (slots, 1, 1), 0)
    live_taps = jnp.where(slot_ids < live_pairs, taps_all, jnp.zeros_like(taps_all))
    lag_tables = lag_matrix(live_taps, half_width, 3 * half_width, half_width)
    product = jnp.einsum("flak,lnkp->fnap", lag_tables, shifted, preferred_element_type=jnp.float32)
    outgoing = product.reshape(slots, length, probe_count).astype(jnp.bfloat16)
    arrived = lax.all_to_all(
        outgoing.reshape(slots, band_size, segment, probe_count),
        "band",
        split_axis=1,
        concat_axis=0,
        tiled=True,
    )
    arrived = arrived.reshape(band_size * slots, segment, probe_count)
    stations = lax.all_gather(pair_station, "band", axis=0, tiled=True).reshape(band_size * slots)
    targets = lax.broadcasted_iota(jnp.int32, (band_size, band_size * slots), 0)
    picker = (stations[None, :] == targets).astype(jnp.bfloat16)
    station_field = jnp.einsum("tq,qap->tap", picker, arrived, preferred_element_type=jnp.float32)
    flat_field = station_field.reshape(band_size * segment, probe_count)
    gram_local = lax.dot_general(
        flat_field,
        flat_field,
        (((0,), (0,)), ((), ())),
        precision=lax.Precision.HIGHEST,
        preferred_element_type=jnp.float32,
    )
    factor_low = jnp.linalg.cholesky(gram_local)
    for level_bit in range(band_size.bit_length() - 1):
        partner = swapped(factor_low.astype(jnp.bfloat16), "band", level_bit).astype(
            factor_low.dtype
        )
        factor_low = merge_factors(factor_low, partner)
    for level_bit in range(lax.axis_size("grp").bit_length() - 1):
        partner = swapped(factor_low, "grp", level_bit)
        factor_low = merge_factors(factor_low, partner)
    identity = jnp.eye(probe_count, dtype=jnp.float32)
    inverse = lax.linalg.triangular_solve(factor_low, identity, left_side=True, lower=True)
    basis = lax.dot_general(
        flat_field,
        inverse,
        (((1,), (1,)), ((), ())),
        precision=lax.Precision.HIGHEST,
        preferred_element_type=jnp.float32,
    )
    total_cells = lax.axis_size("grp") * band_size * length
    basis = basis * jnp.sqrt(jnp.float32(total_cells))
    return basis.reshape(band_size, segment, probe_count)


def solution(mesh):
    placed = (
        P(("grp", "band"), None, None, None),
        P(("grp", "band"), None, None, None),
        P(("grp", "band"), None),
        P(("grp", "band")),
    )
    return jax.shard_map(
        local, mesh=mesh, in_specs=placed, out_specs=P("grp", "band", None), check_vma=False
    )
```

profile of v0, /device:TPU:0, one launch (start us, length us, event | category | flops | bytes accessed | tf_op | source)
XLA Modules:
  0.0 430.1 jit_solution(14490880258628814619)
XLA Ops:
  3.9 124.1 %gather_fusion = bf16[62208,5]{1,0:T(8,128)(2,1)} fusion(bf16[5,289]{0,1:T(8,128)(2,1)S(1)} %fusion.24, s32[62464]{0:T(1024)S(1)} %pad_clamp_fusion), kind=kCustom, calls=%fused_computation | custom fusion | bytes 1492992 | tf_op jit(solution)/shard_map/jit(_take)/gather | solution.py:18
  127.9 15.4 %copy.52 = bf16[144,432,5]{1,0,2:T(8,128)(2,1)} copy(bf16[144,432,5]{2,1,0:T(8,128)(2,1)} %bitcast.95) | data formatting | bytes 1244160 | tf_op jit(solution)/shard_map/jit(_take)/gather | solution.py:18
  143.4 5.2 %convert_bitcast_fusion = bf16[5,30,144,128]{3,2,0,1:T(8,128)(2,1)S(1)} fusion(bf16[1,1,144,128]{3,2,1,0:T(8,128)(2,1)S(1)} %get-tuple-element.7, bf16[1,29,144,128]{3,2,1,0:T(8,128)(2,1)S(1)} %get-tuple-element.9, bf16[1,30,144,128]{3,2,1,0:T(8,128)(2,1)S(1)} %bitcast.98, bf16[1,29,144,128]{3,2,1,0:T(8,128)(2,1)S(1)} %get-tuple-element.8, ...), kind=kOutput, calls=%fused_computation.4 | convolution fusion | flops 2408762880 | bytes 9593856 | tf_op jit(solution)/shard_map/flak,lnkp->fnap/dot_general | solution.py:53
  148.6 3.4 copy.53
  152.0 8.3 %convert_element_type.26 = bf16[5,8,540,128]{3,2,1,0:T(8,128)(2,1)} reshape(bf16[5,30,144,128]{3,2,1,0:T(8,128)(2,1)} %copy.53) | data formatting | bytes 11059200 | tf_op jit(solution)/shard_map/convert_element_type | solution.py:54
  160.3 5.4 %copy.54 = bf16[5,8,540,128]{3,2,0,1:T(8,128)(2,1)} copy(bf16[5,8,540,128]{3,2,1,0:T(8,128)(2,1)} %convert_element_type.26) | data formatting | bytes 11059200 | tf_op jit(solution)/shard_map/convert_element_type | solution.py:54
  165.7 6.5 %all-to-all-start = ((bf16[5,8,540,128]{3,2,0,1:T(8,128)(2,1)}), bf16[5,8,540,128]{3,2,0,1:T(8,128)(2,1)}, u32[]{:S(2)}, u32[]{:S(2)}) async-start(bf16[5,8,540,128]{3,2,0,1:T(8,128)(2,1)} %copy.54), calls=%async_computation | async-start | bytes 11141120 | tf_op jit(solution)/shard_map/all_to_all | solution.py:55
  172.2 97.3 %all-gather = s32[8,1,5]{2,1,0:T(1,128)S(1)} all-gather(s32[1,1,5]{2,1,0:T(1,128)S(1)} %bitcast.99), channel_id=1, replica_groups=mesh['grp'=4,'band'=8] {'band'}, dimensions={0}, use_global_device_ids=true | all-gather | bytes 180 | tf_op jit(solution)/shard_map/all_gather | solution.py:63
  270.8 25.1 %all-to-all-done = bf16[5,8,540,128]{3,2,0,1:T(8,128)(2,1)} async-done(((bf16[5,8,540,128]{3,2,0,1:T(8,128)(2,1)}), bf16[5,8,540,128]{3,2,0,1:T(8,128)(2,1)}, u32[]{:S(2)}, u32[]{:S(2)}) %all-to-all-start) | async-done | bytes 5529632 | tf_op jit(solution)/shard_map/all_to_all | solution.py:55
  295.8 4.6 %fusion = f32[8,540,128]{2,0,1:T(8,128)S(1)} fusion(bf16[40,540,128]{2,1,0:T(8,128)(2,1)} %bitcast.17, s32[40]{0:T(128)S(1)} %eq.13), kind=kOutput, calls=%fused_computation.2 | convolution fusion | flops 44237120 | bytes 7741600 | tf_op jit(solution)/shard_map/tq,qap->tap/dot_general | solution.py:66
  301.8 3.8 convolution_bitcast_fusion
  305.7 11.7 %cholesky.104 = f32[128,128]{1,0:T(8,128)S(1)} custom-call(f32[128,128]{1,0:T(8,128)S(1)} %fusion.33), custom_call_target="Cholesky" | custom-call | tf_op jit(solution)/shard_map/jit(cholesky)/cholesky | solution.py:75
  324.1 11.7 %cholesky.115 = f32[128,128]{1,0:T(8,128)S(1)} custom-call(f32[128,128]{1,0:T(8,128)S(1)} %fusion.32), custom_call_target="Cholesky" | custom-call | tf_op jit(solution)/shard_map/jit(cholesky)/cholesky | solution.py:34
  337.3 3.7 collective-permute-start.1
  343.2 11.7 %cholesky.126 = f32[128,128]{1,0:T(8,128)S(1)} custom-call(f32[128,128]{1,0:T(8,128)S(1)} %fusion.31), custom_call_target="Cholesky" | custom-call | tf_op jit(solution)/shard_map/jit(cholesky)/cholesky | solution.py:34
  356.4 4.2 collective-permute-start.2
  363.1 11.9 %cholesky.137 = f32[128,128]{1,0:T(8,128)S(1)} custom-call(f32[128,128]{1,0:T(8,128)S(1)} %fusion.30), custom_call_target="Cholesky" | custom-call | tf_op jit(solution)/shard_map/jit(cholesky)/cholesky | solution.py:34
  378.3 2.5 collective-permute-done.3
  381.2 11.7 %cholesky.148 = f32[128,128]{1,0:T(8,128)S(1)} custom-call(f32[128,128]{1,0:T(8,128)S(1)} %fusion.29), custom_call_target="Cholesky" | custom-call | tf_op jit(solution)/shard_map/jit(cholesky)/cholesky | solution.py:34
  396.2 2.5 collective-permute-done.4
  399.1 11.7 %cholesky.159 = f32[128,128]{1,0:T(8,128)S(1)} custom-call(f32[128,128]{1,0:T(8,128)S(1)} %fusion.28), custom_call_target="Cholesky" | custom-call | tf_op jit(solution)/shard_map/jit(cholesky)/cholesky | solution.py:34
  412.2 9.8 %custom-call.5 = f32[1,128,128]{1,2,0:T(8,128)S(1)} custom-call(f32[1,128,128]{2,1,0:T(8,128)S(1)} %fusion.25), custom_call_target="InvertDiagBlocksLowerTriangular" | custom-call | tf_op jit(solution)/shard_map/triangular_solve | solution.py:85
  422.3 3.2 convolution_multiply_fusion
  427.2 2.6 copy.73
  (72 shorter events, 30.8 us)
Async XLA Ops:
  0.8 1.9 copy-start.3
  127.9 15.4 %copy-start.2 = (bf16[1,1,4320,128]{3,2,1,0:T(8,128)(2,1)S(1)}, bf16[1,1,4320,128]{3,2,1,0:T(8,128)(2,1)}, u32[]{:S(2)}) copy-start(bf16[1,1,4320,128]{3,2,1,0:T(8,128)(2,1)} %param.5) | copy-start | bytes 3317764
  165.7 6.5 %copy-start.4 = (s32[1,5]{1,0:T(1,128)S(1)}, s32[1,5]{1,0:T(1,128)}, u32[]{:S(2)}) copy-start(s32[1,5]{1,0:T(1,128)} %param.7) | copy-start | bytes 64
  165.7 130.1 %all-to-all-start = ((bf16[5,8,540,128]{3,2,0,1:T(8,128)(2,1)}), bf16[5,8,540,128]{3,2,0,1:T(8,128)(2,1)}, u32[]{:S(2)}, u32[]{:S(2)}) async-start(bf16[5,8,540,128]{3,2,0,1:T(8,128)(2,1)} %copy.54), calls=%async_computation | async-start | bytes 11141120 | tf_op jit(solution)/shard_map/all_to_all | solution.py:55
  300.5 1.4 copy-start
  318.9 4.9 %collective-permute-start = (bf16[128,128]{1,0:T(8,128)(2,1)S(1)}, bf16[128,128]{1,0:T(8,128)(2,1)S(1)}, u32[]{:S(2)}, u32[]{:S(2)}) collective-permute-start(bf16[128,128]{1,0:T(8,128)(2,1)S(1)} %fusion.44), channel_id=1, source_target_pairs={{0,1},{1,0},{2,3},{3,2},{4,5},{5,4},{6,7},{7,6},{8,9},{9,8},{10,11... | collective-permute-start | bytes 98312 | tf_op jit(solution)/shard_map/ppermute | solution.py:10
  323.8 98.5 %copy-start.1 = (f32[4320,128]{1,0:T(8,128)S(1)}, f32[4320,128]{1,0:T(8,128)}, u32[]{:S(2)}) copy-start(f32[4320,128]{1,0:T(8,128)} %reshape.116) | copy-start | bytes 6635524
  337.3 5.6 %collective-permute-start.1 = (bf16[128,128]{1,0:T(8,128)(2,1)S(1)}, bf16[128,128]{1,0:T(8,128)(2,1)S(1)}, u32[]{:S(2)}, u32[]{:S(2)}) collective-permute-start(bf16[128,128]{1,0:T(8,128)(2,1)S(1)} %fusion.46), channel_id=1, source_target_pairs={{0,2},{1,3},{2,0},{3,1},{4,6},{5,7},{6,4},{7,5},{8,10},{9,11},{10,... | collective-permute-start | bytes 98312 | tf_op jit(solution)/shard_map/ppermute | solution.py:10
  356.4 6.5 %collective-permute-start.2 = (bf16[128,128]{1,0:T(8,128)(2,1)S(1)}, bf16[128,128]{1,0:T(8,128)(2,1)S(1)}, u32[]{:S(2)}, u32[]{:S(2)}) collective-permute-start(bf16[128,128]{1,0:T(8,128)(2,1)S(1)} %fusion.48), channel_id=1, source_target_pairs={{0,4},{1,5},{2,6},{3,7},{4,0},{5,1},{6,2},{7,3},{8,12},{9,13},{10,... | collective-permute-start | bytes 98312 | tf_op jit(solution)/shard_map/ppermute | solution.py:10
  376.4 4.3 %collective-permute-start.3 = (f32[128,128]{1,0:T(8,128)S(1)}, f32[128,128]{1,0:T(8,128)S(1)}, u32[]{:S(2)}, u32[]{:S(2)}) collective-permute-start(f32[128,128]{1,0:T(8,128)S(1)} %select_select_fusion.2), channel_id=1, source_target_pairs={{0,8},{8,0},{16,24},{24,16},{1,9},{9,1},{17,25},{25,17},{2,10},{10... | collective-permute-start | bytes 196616 | tf_op jit(solution)/shard_map/ppermute | solution.py:10
  394.3 4.3 %collective-permute-start.4 = (f32[128,128]{1,0:T(8,128)S(1)}, f32[128,128]{1,0:T(8,128)S(1)}, u32[]{:S(2)}, u32[]{:S(2)}) collective-permute-start(f32[128,128]{1,0:T(8,128)S(1)} %select_select_fusion.1), channel_id=1, source_target_pairs={{0,16},{8,24},{16,0},{24,8},{1,17},{9,25},{17,1},{25,9},{2,18},{10... | collective-permute-start | bytes 196616 | tf_op jit(solution)/shard_map/ppermute | solution.py:10
where the time goes:
time: 435 us; the launch traced here: 430 us
  local copies, waits for them, and re-layouts  170 us (39%)
  blocking collectives  97.3 us (22%)
  other arithmetic  89.9 us (21%)
  waiting for transfers between devices  32.3 us (7%)
  matrix products  21.4 us (5%)
  starting transfers between devices  17.6 us (4%)
    gather x2, local copies, waits for them, and re-layouts, lag_matrix(): picked = jnp.take(pair_taps, jnp.clip(offset, 0, 2 * half_width), axis=-1)  140 us
    all_gather x1, blocking collectives, local(): lax.all_gather(pair_station, 'band', axis=0, tiled=True)  97.3 us
    another operation x15, other arithmetic, merge_factors(): return jnp.linalg.cholesky(own_gram + other_gram)  62.5 us
    all_to_all x1, waiting for transfers between devices, local(): lax.all_to_all(outgoing.reshape(slots, band_size, segment, probe_count),...  25.1 us
    convert_element_type x3, local copies, waits for them, and re-layouts, local(): outgoing = product.reshape(slots, length, probe_count).astype(jnp.bfloat16)  17.2 us
    another operation x3, other arithmetic, local(): factor_low = jnp.linalg.cholesky(gram_local)  12.5 us
    ppermute x5, starting transfers between devices, swapped(): return lax.ppermute(value, axis, pairs)  11.2 us
    another operation x2, other arithmetic, local(): lax.linalg.triangular_solve(factor_low, identity, left_side=True, lower=T...  10.5 us
  transfers between devices with their start and end apart: 6, of which 5 were waited for; matrix products, arithmetic and copies ran while one was open for 2% of the time, Pallas kernels for 0%

commit v1 on v0

v1 whole, which is shorter than its diff:
```python
import functools

import jax
import jax.numpy as jnp
from jax import lax
from jax.experimental import pallas as pl
from jax.experimental.pallas import tpu as pltpu
from jax.sharding import PartitionSpec as P

LANES = 128
TILE = 16
BLOCK = 144


def up(value, step):
    return -(-value // step) * step


def swapped(value, axis, mask):
    pairs = [(source, source ^ mask) for source in range(lax.axis_size(axis))]
    return lax.ppermute(value, axis, pairs)


class Plan:
    def __init__(self, length, taps, slots, band_size):
        self.length, self.taps, self.slots, self.band = length, taps, slots, band_size
        self.half = (taps - 1) // 2
        self.segment = length // band_size
        starts = [b * self.segment - self.half for b in range(band_size)]
        self.aligned = [s // TILE * TILE for s in starts]
        self.shifts = [s - a for s, a in zip(starts, self.aligned)]
        self.rows = up(self.segment, TILE)
        blocks = -(-self.segment // BLOCK)
        self.block_starts = [min(i * BLOCK, self.rows - BLOCK) for i in range(blocks)]
        self.depth = up(BLOCK + taps - 1 + max(self.shifts), TILE)
        self.sub = self.block_starts[-1] + self.depth
        self.chip_starts = [self.aligned[b // 2 * 2] for b in range(band_size)]
        self.offsets = [a - c for a, c in zip(self.aligned, self.chip_starts)]
        self.window = up(max(o + self.sub for o in self.offsets), TILE)
        self.left = -min(self.chip_starts)
        self.right = up(max(max(self.chip_starts) + self.window - length, TILE), TILE)
        self.tap_rows = -(-taps // LANES)
        self.extra = up(slots * self.tap_rows + 1, TILE)
        self.message = self.window + self.extra


def pack_kernel(plan, starts_ref, station_ref, count_ref, taps_ref, probes_ref, *rest):
    peers = len(rest) - 5
    messages = rest[:peers]
    held, rows_f32, rows_bf, in_sems, out_sems = rest[peers:]
    length, left, right = plan.length, plan.left, plan.right
    loads = [
        pltpu.make_async_copy(
            probes_ref.at[pl.ds(0, length)], held.at[pl.ds(left, length)], in_sems.at[0]
        ),
        pltpu.make_async_copy(
            probes_ref.at[pl.ds(length - left, left)], held.at[pl.ds(0, left)], in_sems.at[1]
        ),
        pltpu.make_async_copy(
            probes_ref.at[pl.ds(0, right)], held.at[pl.ds(left + length, right)], in_sems.at[2]
        ),
    ]
    for copy in loads:
        copy.start()
    rows_f32[...] = jnp.zeros_like(rows_f32)
    live = count_ref[0]
    for slot in range(plan.slots):
        keep = (slot < live).astype(jnp.float32)
        for part in range(plan.tap_rows):
            low = part * LANES
            width = min(LANES, plan.taps - low)
            piece = taps_ref[pl.ds(slot, 1), pl.ds(low, width)].astype(jnp.float32)
            rows_f32[pl.ds(slot * plan.tap_rows + part, 1), pl.ds(0, width)] = piece * keep
    lane = lax.broadcasted_iota(jnp.int32, (1, LANES), 1)
    names = jnp.zeros((1, LANES), jnp.float32)
    for slot in range(plan.slots):
        names = jnp.where(lane == slot, station_ref[0, slot].astype(jnp.float32), names)
    rows_f32[pl.ds(plan.slots * plan.tap_rows, 1), :] = names
    rows_bf[...] = rows_f32[...].astype(jnp.bfloat16)
    for copy in loads:
        copy.wait()
    stores = []
    for peer in range(peers):
        start = pl.multiple_of(starts_ref[peer], TILE)
        stores.append(
            pltpu.make_async_copy(
                held.at[pl.ds(start, plan.window)],
                messages[peer].at[pl.ds(0, plan.window)],
                out_sems.at[2 * peer],
            )
        )
        stores.append(
            pltpu.make_async_copy(
                rows_bf, messages[peer].at[pl.ds(plan.window, plan.extra)], out_sems.at[2 * peer + 1]
            )
        )
    for copy in stores:
        copy.start()
    for copy in stores:
        copy.wait()


def pack(plan, probes, taps, station, count, peer_starts):
    peers = plan.band // 2
    smem = pl.BlockSpec(memory_space=pltpu.SMEM)
    return pl.pallas_call(
        functools.partial(pack_kernel, plan),
        out_shape=[jax.ShapeDtypeStruct((plan.message, LANES), jnp.bfloat16)] * peers,
        in_specs=[smem, smem, smem, pl.BlockSpec(memory_space=pltpu.VMEM), pl.BlockSpec(memory_space=pl.ANY)],
        out_specs=[pl.BlockSpec(memory_space=pl.ANY)] * peers,
        scratch_shapes=[
            pltpu.VMEM((plan.left + plan.length + plan.right, LANES), jnp.bfloat16),
            pltpu.VMEM((plan.extra, LANES), jnp.float32),
            pltpu.VMEM((plan.extra, LANES), jnp.bfloat16),
            pltpu.SemaphoreType.DMA((3,)),
            pltpu.SemaphoreType.DMA((2 * peers,)),
        ],
        compiler_params=pltpu.CompilerParams(vmem_limit_bytes=32 << 20),
        cost_estimate=pl.CostEstimate(flops=0, bytes_accessed=4 << 20, transcendentals=0),
        name="pack_windows",
    )(peer_starts, station, count, taps, probes)


def field_kernel(plan, place_ref, *rest):
    messages = rest[: plan.band]
    split_ref, gram_ref, held, field, table, sems = rest[plan.band :]
    offset = pl.multiple_of(place_ref[0], TILE)
    shift = place_ref[1]
    copies = []
    for source in range(plan.band):
        copies.append(
            pltpu.make_async_copy(
                messages[source].at[pl.ds(offset, plan.sub)],
                held.at[source, pl.ds(0, plan.sub)],
                sems.at[source, 0],
            )
        )
        copies.append(
            pltpu.make_async_copy(
                messages[source].at[pl.ds(plan.window, plan.extra)],
                held.at[source, pl.ds(plan.sub, plan.extra)],
                sems.at[source, 1],
            )
        )
    for copy in copies:
        copy.start()
    field[...] = jnp.zeros_like(field)
    lanes = up(plan.depth, LANES)
    for copy in copies:
        copy.wait()

    @pl.loop(0, plan.band)
    def _(source):
        rows = held[source, pl.ds(plan.sub, plan.extra), :].astype(jnp.float32)
        names = rows[plan.slots * plan.tap_rows : plan.slots * plan.tap_rows + 1, :]
        for slot in range(plan.slots):
            pieces = [
                rows[slot * plan.tap_rows + part : slot * plan.tap_rows + part + 1, :]
                for part in range(plan.tap_rows)
            ]
            pieces += [jnp.zeros((1, LANES), jnp.float32)] * (lanes // LANES - plan.tap_rows)
            moved = pltpu.roll(jnp.concatenate(pieces, axis=1), shift, 1)
            spread = jnp.broadcast_to(moved, (BLOCK, lanes))
            rolled = pltpu.roll(spread, 0, 1, stride=1, stride_axis=0)
            table[pl.ds(slot * BLOCK, BLOCK), :] = rolled[:, : plan.depth].astype(jnp.bfloat16)
        right = jnp.concatenate(
            [held[source, pl.ds(start, plan.depth), :] for start in plan.block_starts], axis=1
        )
        for slot in range(plan.slots):
            product = jnp.dot(
                table[pl.ds(slot * BLOCK, BLOCK), :], right, preferred_element_type=jnp.float32
            )
            station = names[0, slot].astype(jnp.int32)
            done = 0
            for i, start in enumerate(plan.block_starts):
                skip = done - start
                field[station, pl.ds(done, BLOCK - skip), :] += product[
                    skip:, i * LANES : (i + 1) * LANES
                ]
                done = start + BLOCK

    gram_ref[...] = jnp.zeros_like(gram_ref)
    inside = lax.broadcasted_iota(jnp.int32, (plan.rows, LANES), 0) < plan.segment

    @pl.loop(0, plan.band)
    def _(station):
        values = jnp.where(inside, field[station], 0.0)
        high = values.astype(jnp.bfloat16)
        low = (values - high.astype(jnp.float32)).astype(jnp.bfloat16)
        both = jnp.concatenate([high, low], axis=1)
        split_ref[station] = both
        square = lax.dot_general(
            both, both, (((0,), (0,)), ((), ())), preferred_element_type=jnp.float32
        )
        gram_ref[...] += (
            square[:LANES, :LANES]
            + square[:LANES, LANES:]
            + square[LANES:, :LANES]
            + square[LANES:, LANES:]
        )


def make_field(plan, place, messages):
    return pl.pallas_call(
        functools.partial(field_kernel, plan),
        out_shape=[
            jax.ShapeDtypeStruct((plan.band, plan.rows, 2 * LANES), jnp.bfloat16),
            jax.ShapeDtypeStruct((LANES, LANES), jnp.float32),
        ],
        in_specs=[pl.BlockSpec(memory_space=pltpu.SMEM)] + [pl.BlockSpec(memory_space=pl.ANY)] * plan.band,
        out_specs=[pl.BlockSpec(memory_space=pltpu.VMEM)] * 2,
        scratch_shapes=[
            pltpu.VMEM((plan.band, plan.sub + plan.extra, LANES), jnp.bfloat16),
            pltpu.VMEM((plan.band, plan.rows, LANES), jnp.float32),
            pltpu.VMEM((plan.slots * BLOCK, plan.depth), jnp.bfloat16),
            pltpu.SemaphoreType.DMA((plan.band, 2)),
        ],
        compiler_params=pltpu.CompilerParams(vmem_limit_bytes=40 << 20),
        cost_estimate=pl.CostEstimate(flops=3 << 30, bytes_accessed=6 << 20, transcendentals=0),
        name="field_and_gram",
    )(place, *messages)


def basis_kernel(segment, weight_ref, split_ref, out_ref):
    weight = weight_ref[...]
    high = weight.astype(jnp.bfloat16)
    low = (weight - high.astype(jnp.float32)).astype(jnp.bfloat16)
    both = jnp.concatenate([high, low], axis=1)
    right = jnp.concatenate([both, both], axis=0)
    product = jnp.dot(split_ref[0], right, preferred_element_type=jnp.float32)
    out_ref[0] = (product[:, :LANES] + product[:, LANES:])[:segment]


def make_basis(plan, weight, split):
    return pl.pallas_call(
        functools.partial(basis_kernel, plan.segment),
        grid=(plan.band,),
        out_shape=jax.ShapeDtypeStruct((plan.band, plan.segment, LANES), jnp.float32),
        in_specs=[
            pl.BlockSpec((LANES, LANES), lambda t: (0, 0)),
            pl.BlockSpec((1, plan.rows, 2 * LANES), lambda t: (t, 0, 0)),
        ],
        out_specs=pl.BlockSpec((1, plan.segment, LANES), lambda t: (t, 0, 0)),
        compiler_params=pltpu.CompilerParams(vmem_limit_bytes=32 << 20),
        name="basis",
    )(weight, split)


def sum_over(value, axis, first_bit=0):
    bits = lax.axis_size(axis).bit_length() - 1
    for bit in range(first_bit, bits):
        value = value + swapped(value, axis, 1 << bit)
    return value


def local(probes, kernel, pair_station, pair_count):
    length, probe_count = probes.shape[2:]
    slots, taps = kernel.shape[1], kernel.shape[3]
    band_size = lax.axis_size("band")
    plan = Plan(length, taps, slots, band_size)
    band = lax.axis_index("band")
    chip_starts = jnp.array(plan.chip_starts, jnp.int32)
    peers = band_size // 2
    peer_starts = jnp.stack([chip_starts[band ^ (2 * k)] for k in range(peers)]) + plan.left
    place = jnp.stack(
        [jnp.array(plan.offsets, jnp.int32)[band], jnp.array(plan.shifts, jnp.int32)[band]]
    )
    messages = pack(
        plan, probes.reshape(length, probe_count), kernel.reshape(slots, taps), pair_station, pair_count, peer_starts
    )
    held = [messages[0]] + [swapped(messages[k], "band", 2 * k) for k in range(1, peers)]
    held = held + [swapped(value, "band", 1) for value in held]
    split, gram = make_field(plan, place, held)
    gram = sum_over(gram, "band")
    gram = sum_over(gram, "grp")
    factor_low = jnp.linalg.cholesky(gram)
    identity = jnp.eye(probe_count, dtype=jnp.float32)
    inverse = lax.linalg.triangular_solve(factor_low, identity, left_side=True, lower=True)
    total_cells = lax.axis_size("grp") * band_size * length
    weight = inverse.T * jnp.sqrt(jnp.float32(total_cells))
    return make_basis(plan, weight, split)


def solution(mesh):
    placed = (
        P(("grp", "band"), None, None, None),
        P(("grp", "band"), None, None, None),
        P(("grp", "band"), None),
        P(("grp", "band")),
    )
    return jax.shard_map(
        local, mesh=mesh, in_specs=placed, out_specs=P("grp", "band", None), check_vma=False
    )
```

time: 435 us -> 110 us (0.25); the launches traced: 430 us -> 110 us
  local copies, waits for them, and re-layouts: 170 us -> 9.35 us
  blocking collectives: 97.3 us -> 0 us
  other arithmetic: 89.9 us -> 26.8 us
  matrix products: 21.4 us -> 0.25 us
  Pallas kernels: 0 us -> 16.3 us
  waiting for transfers between devices: 32.3 us -> 37.4 us
    gather x2 -> x0, local copies, waits for them, and re-layouts: 140 us -> none  [lag_matrix(): picked = jnp.take(pair_taps, jnp.clip(offset, 0, 2 * half_width), axis=-1)]
    all_gather x1 -> x0, blocking collectives: 97.3 us -> none  [local(): lax.all_gather(pair_station, 'band', axis=0, tiled=True)]
    another operation x18 -> x4, other arithmetic: 75 us -> 13.7 us  [the longest x3 12.4 us: local(): factor_low = jnp.linalg.cholesky(gram)]
    ppermute x5 -> x12, waiting for transfers between devices: 7.23 us -> 37.4 us  [swapped(): return lax.ppermute(value, axis, pairs)]
    all_to_all x1 -> x0, waiting for transfers between devices: 25.1 us -> none  [local(): lax.all_to_all(outgoing.reshape(slots, band_size, segment, probe_count),...]
    dot_general x14 -> x0, matrix products: 21.2 us -> none  [the longest x1 5.19 us: local(): jnp.einsum('flak,lnkp->fnap', lag_tables, shifted, preferred_element_type...]
    convert_element_type x3 -> x0, local copies, waits for them, and re-layouts: 17.2 us -> none  [local(): outgoing = product.reshape(slots, length, probe_count).astype(jnp.bfloat16)]
    pallas_call x0 -> x3, Pallas kernels: none -> 16.3 us  [the longest x1 12.9 us: make_field(): pl.pallas_call(functools.partial(field_kernel, plan), out_shape=[jax.Shap...]
  transfers between devices with their start and end apart: 6 -> 12, of which waited for: 5 -> 7; matrix products, arithmetic and copies ran while one was open for 2% -> 4% of each run, Pallas kernels for 0% -> 0%
where the time goes in v1:
time: 110 us
  waiting for transfers between devices  37.4 us (34%)
  other arithmetic  26.8 us (24%)
  starting transfers between devices  18.8 us (17%)
  Pallas kernels  16.3 us (15%)
  local copies, waits for them, and re-layouts  9.35 us (8%)
    ppermute x12, waiting for transfers between devices, swapped(): return lax.ppermute(value, axis, pairs)  37.4 us
    ppermute x12, starting transfers between devices, swapped(): return lax.ppermute(value, axis, pairs)  18.8 us
    pallas_call x1, Pallas kernels, make_field(): pl.pallas_call(functools.partial(field_kernel, plan), out_shape=[jax.Shap...  12.9 us
    another operation x3, other arithmetic, local(): factor_low = jnp.linalg.cholesky(gram)  12.4 us
    another operation x2, other arithmetic, local(): lax.linalg.triangular_solve(factor_low, identity, left_side=True, lower=T...  10.5 us
    pallas_call x1, local copies, waits for them, and re-layouts, make_basis(): pl.pallas_call(functools.partial(basis_kernel, plan.segment), grid=(plan....  2.64 us
    unnamed x6, local copies, waits for them, and re-layouts  2.59 us
    add x1, other arithmetic, local(): jnp.stack([chip_starts[band ^ 2 * k] for k in range(peers)]) + plan.left  2.55 us
  transfers between devices with their start and end apart: 12, of which 7 were waited for; matrix products, arithmetic and copies ran while one was open for 4% of the time, Pallas kernels for 0%

profile of v1, /device:TPU:0, one launch (start us, length us, event | category | flops | bytes accessed | tf_op | source)
XLA Modules:
  0.0 109.7 jit_solution(5003817276751362563)
XLA Ops:
  0.7 1.4 %fusion.3 = (s32[1]{0:T(128)}, s32[1]{0:T(128)}, s32[1]{0:T(128)}, s32[1]{0:T(128)}) fusion(s32[8]{0:T(128)} %constant.65.clone, s32[]{:T(128)S(6)} %select_n.18, s32[]{:T(128)S(6)} %select_n.19, s32[]{:T(128)S(6)} %select_n.21, s32[]{:T(128)S(6)} %select_n.20), kind=kLoop, calls=%fused_computation.12 | loop fusion | bytes 48 | tf_op jit(solution)/shard_map/dynamic_slice | solution.py:264
  2.1 2.5 %add_add_fusion.starts_ref = s32[4]{0:T(128)S(1)} fusion(s32[1]{0:T(128)} %get-tuple-element.19, s32[1]{0:T(128)} %get-tuple-element.20, s32[1]{0:T(128)} %get-tuple-element.18, s32[1]{0:T(128)} %get-tuple-element.17), kind=kLoop, calls=%fused_computation.11 | loop fusion | flops 16 | bytes 32 | tf_op jit(solution)/shard_map/add | solution.py:264
  4.6 1.2 %copy-done = bf16[1,1,4320,128]{3,2,1,0:T(8,128)(2,1)S(1)} copy-done((bf16[1,1,4320,128]{3,2,1,0:T(8,128)(2,1)S(1)}, bf16[1,1,4320,128]{3,2,1,0:T(8,128)(2,1)}, u32[]{:S(2)}) %copy-start) | copy-done | bytes 1105944
  7.2 1.5 %pack_windows.1 = (bf16[1408,128]{1,0:T(8,128)(2,1)S(1)}, bf16[1408,128]{1,0:T(8,128)(2,1)S(1)}, bf16[1408,128]{1,0:T(8,128)(2,1)S(1)}, bf16[1408,128]{1,0:T(8,128)(2,1)S(1)}) custom-call(s32[4]{0:T(128)S(1)} %add_add_fusion.starts_ref, s32[1,5]{1,0:T(1,128)S(1)} %copy-done.2, s32[1]{0:T(128)S(6)} %copy.12.count_ref, bf16[5,289]{1,0:T(8,128)(2,1)S(1)} %bitcast.12, ...), custom_call_target="tpu_custom_call" | custom-call | bytes 4194304 | tf_op jit(solution)/shard_map/pack_windows/pallas_call | solution.py:106
  8.8 3.1 %collective-permute-start = (bf16[1408,128]{1,0:T(8,128)(2,1)S(1)}, bf16[1408,128]{1,0:T(8,128)(2,1)S(1)}, u32[]{:S(2)}, u32[]{:S(2)}) collective-permute-start(bf16[1408,128]{1,0:T(8,128)(2,1)S(1)} %get-tuple-element.12), channel_id=1, source_target_pairs={{0,2},{1,3},{2,0},{3,1},{4,6},{5,7},{6,4},{7,5},{8,10},{9,11},{10,... | collective-permute-start | bytes 1081352 | tf_op jit(solution)/shard_map/ppermute | solution.py:21
  11.8 2.6 %collective-permute-start.1 = (bf16[1408,128]{1,0:T(8,128)(2,1)S(1)}, bf16[1408,128]{1,0:T(8,128)(2,1)S(1)}, u32[]{:S(2)}, u32[]{:S(2)}) collective-permute-start(bf16[1408,128]{1,0:T(8,128)(2,1)S(1)} %get-tuple-element.13), channel_id=1, source_target_pairs={{0,4},{1,5},{2,6},{3,7},{4,0},{5,1},{6,2},{7,3},{8,12},{9,13},{10,... | collective-permute-start | bytes 1081352 | tf_op jit(solution)/shard_map/ppermute | solution.py:21
  14.4 12.8 %collective-permute-done.rest_1_ = bf16[1408,128]{1,0:T(8,128)(2,1)S(1)} collective-permute-done((bf16[1408,128]{1,0:T(8,128)(2,1)S(1)}, bf16[1408,128]{1,0:T(8,128)(2,1)S(1)}, u32[]{:S(2)}, u32[]{:S(2)}) %collective-permute-start) | collective-permute-done | bytes 360480 | tf_op jit(solution)/shard_map/ppermute | solution.py:21
  27.2 12.3 %collective-permute-done.1.rest_2_ = bf16[1408,128]{1,0:T(8,128)(2,1)S(1)} collective-permute-done((bf16[1408,128]{1,0:T(8,128)(2,1)S(1)}, bf16[1408,128]{1,0:T(8,128)(2,1)S(1)}, u32[]{:S(2)}, u32[]{:S(2)}) %collective-permute-start.1) | collective-permute-done | bytes 360480 | tf_op jit(solution)/shard_map/ppermute | solution.py:21
  41.3 1.3 %dynamic_slice.18 = s32[1]{0:T(128)} dynamic-slice(s32[8]{0:T(128)} %constant.66.clone, s32[]{:T(128)S(6)} %select_n.18), dynamic_slice_sizes={1} | dynamic-slice | bytes 12 | tf_op jit(solution)/shard_map/dynamic_slice | solution.py:266
  42.5 1.4 %pad_add_fusion.place_ref = s32[2]{0:T(128)S(1)} fusion(s32[1]{0:T(128)} %dynamic_slice.19, s32[1]{0:T(128)} %dynamic_slice.18), kind=kLoop, calls=%fused_computation.10 | loop fusion | flops 2 | bytes 16 | tf_op jit(solution)/shard_map/stack | solution.py:265
  43.9 12.9 %field_and_gram.1 = (bf16[8,544,256]{2,1,0:T(8,128)(2,1)S(1)}, f32[128,128]{1,0:T(8,128)S(1)}) custom-call(s32[2]{0:T(128)S(1)} %pad_add_fusion.place_ref, bf16[1408,128]{1,0:T(8,128)(2,1)S(1)} %get-tuple-element.11.rest_0_, bf16[1408,128]{1,0:T(8,128)(2,1)S(1)} %collective-permute-done.rest_1_, bf16[1408,128]{1,0:T(8,128)(2,1)S(1)} %collective-permute-done.1.rest_2_, ...), custom_call_target="tpu_custom_call" | custom-call | flops 3221225472 | bytes 6291456 | tf_op jit(solution)/shard_map/field_and_gram/pallas_call | solution.py:204
  57.0 1.2 %collective-permute-done.7 = f32[128,128]{0,1:T(8,128)S(1)} collective-permute-done((f32[128,128]{0,1:T(8,128)S(1)}, f32[128,128]{0,1:T(8,128)S(1)}, u32[]{:S(2)}, u32[]{:S(2)}) %collective-permute-start.7) | collective-permute-done | bytes 65568 | tf_op jit(solution)/shard_map/ppermute | solution.py:21
  58.2 6.6 %collective-permute-start.8 = (f32[128,128]{0,1:T(8,128)S(1)}, f32[128,128]{0,1:T(8,128)S(1)}, u32[]{:S(2)}, u32[]{:S(2)}) collective-permute-start(f32[128,128]{0,1:T(8,128)S(1)} %add.48), channel_id=1, source_target_pairs={{0,2},{1,3},{2,0},{3,1},{4,6},{5,7},{6,4},{7,5},{8,10},{9,11},{10,... | collective-permute-start | bytes 196616 | tf_op jit(solution)/shard_map/ppermute | solution.py:21
  64.8 2.6 %collective-permute-done.8 = f32[128,128]{0,1:T(8,128)S(1)} collective-permute-done((f32[128,128]{0,1:T(8,128)S(1)}, f32[128,128]{0,1:T(8,128)S(1)}, u32[]{:S(2)}, u32[]{:S(2)}) %collective-permute-start.8) | collective-permute-done | bytes 65568 | tf_op jit(solution)/shard_map/ppermute | solution.py:21
  67.5 2.8 %collective-permute-start.9 = (f32[128,128]{0,1:T(8,128)S(1)}, f32[128,128]{0,1:T(8,128)S(1)}, u32[]{:S(2)}, u32[]{:S(2)}) collective-permute-start(f32[128,128]{0,1:T(8,128)S(1)} %add.49), channel_id=1, source_target_pairs={{0,4},{1,5},{2,6},{3,7},{4,0},{5,1},{6,2},{7,3},{8,12},{9,13},{10,... | collective-permute-start | bytes 196616 | tf_op jit(solution)/shard_map/ppermute | solution.py:21
  70.3 2.9 %collective-permute-done.9 = f32[128,128]{0,1:T(8,128)S(1)} collective-permute-done((f32[128,128]{0,1:T(8,128)S(1)}, f32[128,128]{0,1:T(8,128)S(1)}, u32[]{:S(2)}, u32[]{:S(2)}) %collective-permute-start.9) | collective-permute-done | bytes 65568 | tf_op jit(solution)/shard_map/ppermute | solution.py:21
  73.2 1.5 %collective-permute-start.10 = (f32[128,128]{0,1:T(8,128)S(1)}, f32[128,128]{0,1:T(8,128)S(1)}, u32[]{:S(2)}, u32[]{:S(2)}) collective-permute-start(f32[128,128]{0,1:T(8,128)S(1)} %add.50), channel_id=1, source_target_pairs={{0,8},{8,0},{16,24},{24,16},{1,9},{9,1},{17,25},{25,17},{2,10},{10... | collective-permute-start | bytes 196616 | tf_op jit(solution)/shard_map/ppermute | solution.py:21
  74.7 2.8 %collective-permute-done.10 = f32[128,128]{0,1:T(8,128)S(1)} collective-permute-done((f32[128,128]{0,1:T(8,128)S(1)}, f32[128,128]{0,1:T(8,128)S(1)}, u32[]{:S(2)}, u32[]{:S(2)}) %collective-permute-start.10) | collective-permute-done | bytes 65568 | tf_op jit(solution)/shard_map/ppermute | solution.py:21
  77.5 1.6 %collective-permute-start.11 = (f32[128,128]{0,1:T(8,128)S(1)}, f32[128,128]{0,1:T(8,128)S(1)}, u32[]{:S(2)}, u32[]{:S(2)}) collective-permute-start(f32[128,128]{0,1:T(8,128)S(1)} %add.51), channel_id=1, source_target_pairs={{0,16},{8,24},{16,0},{24,8},{1,17},{9,25},{17,1},{25,9},{2,18},{10... | collective-permute-start | bytes 196616 | tf_op jit(solution)/shard_map/ppermute | solution.py:21
  79.1 2.7 %collective-permute-done.11 = f32[128,128]{0,1:T(8,128)S(1)} collective-permute-done((f32[128,128]{0,1:T(8,128)S(1)}, f32[128,128]{0,1:T(8,128)S(1)}, u32[]{:S(2)}, u32[]{:S(2)}) %collective-permute-start.11) | collective-permute-done | bytes 65568 | tf_op jit(solution)/shard_map/ppermute | solution.py:21
  82.0 11.7 %cholesky.14 = f32[128,128]{1,0:T(8,128)S(1)} custom-call(f32[128,128]{1,0:T(8,128)S(1)} %fusion.2), custom_call_target="Cholesky" | custom-call | tf_op jit(solution)/shard_map/jit(cholesky)/cholesky | solution.py:276
  95.0 9.8 %custom-call.6 = f32[1,128,128]{1,2,0:T(8,128)S(1)} custom-call(f32[1,128,128]{2,1,0:T(8,128)S(1)} %fusion), custom_call_target="InvertDiagBlocksLowerTriangular" | custom-call | tf_op jit(solution)/shard_map/triangular_solve | solution.py:278
  105.1 1.9 %basis.1 = f32[8,540,128]{2,1,0:T(8,128)S(1)} custom-call(f32[128,128]{1,0:T(8,128)S(1)} %convolution_multiply_fusion.weight_ref, bf16[8,544,256]{2,1,0:T(8,128)(2,1)S(1)} %get-tuple-element.16.split_ref), custom_call_target="tpu_custom_call" | custom-call | tf_op jit(solution)/shard_map/basis/pallas_call | solution.py:235
  107.0 2.6 %copy.11 = f32[8,540,128]{2,0,1:T(8,128)} copy(f32[8,540,128]{2,1,0:T(8,128)S(1)} %basis.1) | data formatting | bytes 4423680 | tf_op jit(solution)/shard_map/basis/pallas_call | solution.py:235
  (29 shorter events, 5.0 us)
Async XLA Ops:
  4.6 1.2 %copy-start = (bf16[1,1,4320,128]{3,2,1,0:T(8,128)(2,1)S(1)}, bf16[1,1,4320,128]{3,2,1,0:T(8,128)(2,1)}, u32[]{:S(2)}) copy-start(bf16[1,1,4320,128]{3,2,1,0:T(8,128)(2,1)} %param.7) | copy-start | bytes 3317764
  5.9 0.7 copy-start.1
  6.6 0.7 copy-start.2
  8.8 18.5 %collective-permute-start = (bf16[1408,128]{1,0:T(8,128)(2,1)S(1)}, bf16[1408,128]{1,0:T(8,128)(2,1)S(1)}, u32[]{:S(2)}, u32[]{:S(2)}) collective-permute-start(bf16[1408,128]{1,0:T(8,128)(2,1)S(1)} %get-tuple-element.12), channel_id=1, source_target_pairs={{0,2},{1,3},{2,0},{3,1},{4,6},{5,7},{6,4},{7,5},{8,10},{9,11},{10,... | collective-permute-start | bytes 1081352 | tf_op jit(solution)/shard_map/ppermute | solution.py:21
  11.8 27.7 %collective-permute-start.1 = (bf16[1408,128]{1,0:T(8,128)(2,1)S(1)}, bf16[1408,128]{1,0:T(8,128)(2,1)S(1)}, u32[]{:S(2)}, u32[]{:S(2)}) collective-permute-start(bf16[1408,128]{1,0:T(8,128)(2,1)S(1)} %get-tuple-element.13), channel_id=1, source_target_pairs={{0,4},{1,5},{2,6},{3,7},{4,0},{5,1},{6,2},{7,3},{8,12},{9,13},{10,... | collective-permute-start | bytes 1081352 | tf_op jit(solution)/shard_map/ppermute | solution.py:21
  14.4 25.1 %collective-permute-start.2 = (bf16[1408,128]{1,0:T(8,128)(2,1)S(1)}, bf16[1408,128]{1,0:T(8,128)(2,1)S(1)}, u32[]{:S(2)}, u32[]{:S(2)}) collective-permute-start(bf16[1408,128]{1,0:T(8,128)(2,1)S(1)} %get-tuple-element.14), channel_id=1, source_target_pairs={{0,6},{1,7},{2,4},{3,5},{4,2},{5,3},{6,0},{7,1},{8,14},{9,15},{10,... | collective-permute-start | bytes 1081352 | tf_op jit(solution)/shard_map/ppermute | solution.py:21
  14.4 29.5 %collective-permute-start.3 = (bf16[1408,128]{1,0:T(8,128)(2,1)S(1)}, bf16[1408,128]{1,0:T(8,128)(2,1)S(1)}, u32[]{:S(2)}, u32[]{:S(2)}) collective-permute-start(bf16[1408,128]{1,0:T(8,128)(2,1)S(1)} %get-tuple-element.11.rest_0_), channel_id=1, source_target_pairs={{0,1},{1,0},{2,3},{3,2},{4,5},{5,4},{6,7},{7,6},{8,9},{9,8},{10,11... | collective-permute-start | bytes 1081352 | tf_op jit(solution)/shard_map/ppermute | solution.py:21
  27.2 16.7 %collective-permute-start.4 = (bf16[1408,128]{1,0:T(8,128)(2,1)S(1)}, bf16[1408,128]{1,0:T(8,128)(2,1)S(1)}, u32[]{:S(2)}, u32[]{:S(2)}) collective-permute-start(bf16[1408,128]{1,0:T(8,128)(2,1)S(1)} %collective-permute-done.rest_1_), channel_id=1, source_target_pairs={{0,1},{1,0},{2,3},{3,2},{4,5},{5,4},{6,7},{7,6},{8,9},{9,8},{10,11... | collective-permute-start | bytes 1081352 | tf_op jit(solution)/shard_map/ppermute | solution.py:21
  39.5 4.4 %collective-permute-start.5 = (bf16[1408,128]{1,0:T(8,128)(2,1)S(1)}, bf16[1408,128]{1,0:T(8,128)(2,1)S(1)}, u32[]{:S(2)}, u32[]{:S(2)}) collective-permute-start(bf16[1408,128]{1,0:T(8,128)(2,1)S(1)} %collective-permute-done.1.rest_2_), channel_id=1, source_target_pairs={{0,1},{1,0},{2,3},{3,2},{4,5},{5,4},{6,7},{7,6},{8,9},{9,8},{10,11... | collective-permute-start | bytes 1081352 | tf_op jit(solution)/shard_map/ppermute | solution.py:21
  39.5 4.4 %collective-permute-start.6 = (bf16[1408,128]{1,0:T(8,128)(2,1)S(1)}, bf16[1408,128]{1,0:T(8,128)(2,1)S(1)}, u32[]{:S(2)}, u32[]{:S(2)}) collective-permute-start(bf16[1408,128]{1,0:T(8,128)(2,1)S(1)} %collective-permute-done.2.rest_3_), channel_id=1, source_target_pairs={{0,1},{1,0},{2,3},{3,2},{4,5},{5,4},{6,7},{7,6},{8,9},{9,8},{10,11... | collective-permute-start | bytes 1081352 | tf_op jit(solution)/shard_map/ppermute | solution.py:21
  56.9 1.3 %collective-permute-start.7 = (f32[128,128]{0,1:T(8,128)S(1)}, f32[128,128]{0,1:T(8,128)S(1)}, u32[]{:S(2)}, u32[]{:S(2)}) collective-permute-start(f32[128,128]{0,1:T(8,128)S(1)} %copy.9), channel_id=1, source_target_pairs={{0,1},{1,0},{2,3},{3,2},{4,5},{5,4},{6,7},{7,6},{8,9},{9,8},{10,11... | collective-permute-start | bytes 196616 | tf_op jit(solution)/shard_map/ppermute | solution.py:21
  58.2 9.2 %collective-permute-start.8 = (f32[128,128]{0,1:T(8,128)S(1)}, f32[128,128]{0,1:T(8,128)S(1)}, u32[]{:S(2)}, u32[]{:S(2)}) collective-permute-start(f32[128,128]{0,1:T(8,128)S(1)} %add.48), channel_id=1, source_target_pairs={{0,2},{1,3},{2,0},{3,1},{4,6},{5,7},{6,4},{7,5},{8,10},{9,11},{10,... | collective-permute-start | bytes 196616 | tf_op jit(solution)/shard_map/ppermute | solution.py:21
  67.5 5.7 %collective-permute-start.9 = (f32[128,128]{0,1:T(8,128)S(1)}, f32[128,128]{0,1:T(8,128)S(1)}, u32[]{:S(2)}, u32[]{:S(2)}) collective-permute-start(f32[128,128]{0,1:T(8,128)S(1)} %add.49), channel_id=1, source_target_pairs={{0,4},{1,5},{2,6},{3,7},{4,0},{5,1},{6,2},{7,3},{8,12},{9,13},{10,... | collective-permute-start | bytes 196616 | tf_op jit(solution)/shard_map/ppermute | solution.py:21
  73.2 4.3 %collective-permute-start.10 = (f32[128,128]{0,1:T(8,128)S(1)}, f32[128,128]{0,1:T(8,128)S(1)}, u32[]{:S(2)}, u32[]{:S(2)}) collective-permute-start(f32[128,128]{0,1:T(8,128)S(1)} %add.50), channel_id=1, source_target_pairs={{0,8},{8,0},{16,24},{24,16},{1,9},{9,1},{17,25},{25,17},{2,10},{10... | collective-permute-start | bytes 196616 | tf_op jit(solution)/shard_map/ppermute | solution.py:21
  77.5 4.3 %collective-permute-start.11 = (f32[128,128]{0,1:T(8,128)S(1)}, f32[128,128]{0,1:T(8,128)S(1)}, u32[]{:S(2)}, u32[]{:S(2)}) collective-permute-start(f32[128,128]{0,1:T(8,128)S(1)} %add.51), channel_id=1, source_target_pairs={{0,16},{8,24},{16,0},{24,8},{1,17},{9,25},{17,1},{25,9},{2,18},{10... | collective-permute-start | bytes 196616 | tf_op jit(solution)/shard_map/ppermute | solution.py:21

commit v2 on v1

v2 whole, which is shorter than its diff:
```python
import functools

import jax
import jax.numpy as jnp
from jax import lax
from jax.experimental import pallas as pl
from jax.experimental.pallas import tpu as pltpu
from jax.sharding import PartitionSpec as P

LANES = 128
TILE = 16
BLOCK = 144


def up(value, step):
    return -(-value // step) * step


def swapped(value, axis, mask):
    pairs = [(source, source ^ mask) for source in range(lax.axis_size(axis))]
    return lax.ppermute(value, axis, pairs)


class Plan:
    def __init__(self, length, taps, slots, band_size):
        self.length, self.taps, self.slots, self.band = length, taps, slots, band_size
        self.half = (taps - 1) // 2
        self.segment = length // band_size
        starts = [b * self.segment - self.half for b in range(band_size)]
        self.aligned = [s // TILE * TILE for s in starts]
        self.shifts = [s - a for s, a in zip(starts, self.aligned)]
        self.rows = up(self.segment, TILE)
        blocks = -(-self.segment // BLOCK)
        self.block_starts = [min(i * BLOCK, self.rows - BLOCK) for i in range(blocks)]
        self.depth = up(BLOCK + taps - 1 + max(self.shifts), TILE)
        self.sub = self.block_starts[-1] + self.depth
        self.chip_starts = [self.aligned[b // 2 * 2] for b in range(band_size)]
        self.offsets = [a - c for a, c in zip(self.aligned, self.chip_starts)]
        self.window = up(max(o + self.sub for o in self.offsets), TILE)
        self.left = -min(self.chip_starts)
        self.right = up(max(max(self.chip_starts) + self.window - length, TILE), TILE)
        self.tap_rows = -(-taps // LANES)
        self.extra = up(slots * self.tap_rows + 1, TILE)
        self.message = self.window + self.extra


def pack_kernel(plan, band_hbm, station_hbm, count_hbm, taps_hbm, probes_hbm, *rest):
    peers = plan.band // 2
    messages = rest[:peers]
    band_ref, station_ref, count_ref, taps_ref, held, rows_f32, rows_bf, in_sems, out_sems = rest[peers:]
    length, left, right = plan.length, plan.left, plan.right
    loads = [
        (probes_hbm.at[pl.ds(0, length)], held.at[pl.ds(left, length)]),
        (probes_hbm.at[pl.ds(length - left, left)], held.at[pl.ds(0, left)]),
        (probes_hbm.at[pl.ds(0, right)], held.at[pl.ds(left + length, right)]),
        (band_hbm, band_ref),
        (station_hbm, station_ref),
        (count_hbm, count_ref),
        (taps_hbm, taps_ref),
    ]
    loads = [pltpu.make_async_copy(a, b, in_sems.at[i]) for i, (a, b) in enumerate(loads)]
    for copy in loads:
        copy.start()
    rows_f32[...] = jnp.zeros_like(rows_f32)
    for copy in loads[3:]:
        copy.wait()
    live = count_ref[0]
    for slot in range(plan.slots):
        keep = (slot < live).astype(jnp.float32)
        for part in range(plan.tap_rows):
            low = part * LANES
            width = min(LANES, plan.taps - low)
            piece = taps_ref[pl.ds(slot, 1), pl.ds(low, width)].astype(jnp.float32)
            rows_f32[pl.ds(slot * plan.tap_rows + part, 1), pl.ds(0, width)] = piece * keep
    lane = lax.broadcasted_iota(jnp.int32, (1, LANES), 1)
    names = jnp.zeros((1, LANES), jnp.float32)
    for slot in range(plan.slots):
        names = jnp.where(lane == slot, station_ref[0, slot].astype(jnp.float32), names)
    rows_f32[pl.ds(plan.slots * plan.tap_rows, 1), :] = names
    rows_bf[...] = rows_f32[...].astype(jnp.bfloat16)
    for copy in loads[:3]:
        copy.wait()
    band = band_ref[0]
    stores = []
    for peer in range(peers):
        chip = (band ^ (2 * peer)) // 2
        start = pl.multiple_of((chip * (2 * plan.segment) + left - plan.half) // TILE * TILE, TILE)
        stores.append(
            pltpu.make_async_copy(
                held.at[pl.ds(start, plan.window)],
                messages[peer].at[pl.ds(0, plan.window)],
                out_sems.at[2 * peer],
            )
        )
        stores.append(
            pltpu.make_async_copy(
                rows_bf, messages[peer].at[pl.ds(plan.window, plan.extra)], out_sems.at[2 * peer + 1]
            )
        )
    for copy in stores:
        copy.start()
    for copy in stores:
        copy.wait()


def pack(plan, band, probes, taps, station, count):
    peers = plan.band // 2
    hbm = pl.BlockSpec(memory_space=pltpu.HBM)
    return pl.pallas_call(
        functools.partial(pack_kernel, plan),
        out_shape=[jax.ShapeDtypeStruct((plan.message, LANES), jnp.bfloat16)] * peers,
        in_specs=[hbm] * 5,
        out_specs=[pl.BlockSpec(memory_space=pl.ANY)] * peers,
        scratch_shapes=[
            pltpu.SMEM((1,), jnp.int32),
            pltpu.SMEM(station.shape, jnp.int32),
            pltpu.SMEM((1,), jnp.int32),
            pltpu.VMEM(taps.shape, jnp.bfloat16),
            pltpu.VMEM((plan.left + plan.length + plan.right, LANES), jnp.bfloat16),
            pltpu.VMEM((plan.extra, LANES), jnp.float32),
            pltpu.VMEM((plan.extra, LANES), jnp.bfloat16),
            pltpu.SemaphoreType.DMA((7,)),
            pltpu.SemaphoreType.DMA((2 * peers,)),
        ],
        compiler_params=pltpu.CompilerParams(vmem_limit_bytes=60 << 20),
        cost_estimate=pl.CostEstimate(flops=0, bytes_accessed=4 << 20, transcendentals=0),
        name="pack_windows",
    )(band, station, count, taps, probes)


def add_products(plan, place, messages, field, table):
    offset, shift = place
    lanes = up(plan.depth, LANES)
    for source, message in enumerate(messages):
        rows = message[pl.ds(plan.window, plan.extra), :].astype(jnp.float32)
        names = rows[plan.slots * plan.tap_rows : plan.slots * plan.tap_rows + 1, :]
        for slot in range(plan.slots):
            pieces = [
                rows[slot * plan.tap_rows + part : slot * plan.tap_rows + part + 1, :]
                for part in range(plan.tap_rows)
            ]
            pieces += [jnp.zeros((1, LANES), jnp.float32)] * (lanes // LANES - plan.tap_rows)
            moved = pltpu.roll(jnp.concatenate(pieces, axis=1), shift, 1)
            spread = jnp.broadcast_to(moved, (BLOCK, lanes))
            rolled = pltpu.roll(spread, 0, 1, stride=1, stride_axis=0)
            table[source, pl.ds(slot * BLOCK, BLOCK), :] = rolled[:, : plan.depth].astype(jnp.bfloat16)
        right = jnp.concatenate(
            [
                message[pl.ds(pl.multiple_of(offset + start, TILE), plan.depth), :]
                for start in plan.block_starts
            ],
            axis=1,
        )
        for slot in range(plan.slots):
            product = jnp.dot(
                table[source, pl.ds(slot * BLOCK, BLOCK), :], right, preferred_element_type=jnp.float32
            )
            station = names[0, slot].astype(jnp.int32)
            done = 0
            for i, start in enumerate(plan.block_starts):
                skip = done - start
                field[station, pl.ds(done, BLOCK - skip), :] += product[
                    skip:, i * LANES : (i + 1) * LANES
                ]
                done = start + BLOCK


def split_and_gram(plan, field, split_ref, gram_ref):
    gram_ref[...] = jnp.zeros_like(gram_ref)
    inside = lax.broadcasted_iota(jnp.int32, (plan.rows, LANES), 0) < plan.segment

    @pl.loop(0, plan.band)
    def _(station):
        values = jnp.where(inside, field[station], 0.0)
        high = values.astype(jnp.bfloat16)
        low = (values - high.astype(jnp.float32)).astype(jnp.bfloat16)
        both = jnp.concatenate([high, low], axis=1)
        split_ref[station] = both
        square = lax.dot_general(
            both, both, (((0,), (0,)), ((), ())), preferred_element_type=jnp.float32
        )
        gram_ref[...] += (
            square[:LANES, :LANES]
            + square[:LANES, LANES:]
            + square[LANES:, :LANES]
            + square[LANES:, LANES:]
        )


def field_kernel(plan, first, last, count, band_ref, *rest):
    messages, rest = rest[:count], rest[count:]
    if not first:
        field, rest = rest[0], rest[1:]
    base = band_ref[0] * plan.segment + plan.left - plan.half
    chip = band_ref[0] // 2 * (2 * plan.segment) + plan.left - plan.half
    aligned = base // TILE * TILE
    place = (aligned - chip // TILE * TILE, base - aligned)
    if last:
        split_ref, gram_ref, table = rest
        add_products(plan, place, messages, field, table)
        split_and_gram(plan, field, split_ref, gram_ref)
    else:
        out_ref, table = rest
        if first:
            out_ref[...] = jnp.zeros_like(out_ref)
        add_products(plan, place, messages, out_ref, table)


def add_rows(plan, band, messages, field, last):
    count, first = len(messages), field is None
    vmem = pl.BlockSpec(memory_space=pltpu.VMEM)
    field_shape = jax.ShapeDtypeStruct((plan.band, plan.rows, LANES), jnp.float32)
    if last:
        out_shape = [
            jax.ShapeDtypeStruct((plan.band, plan.rows, 2 * LANES), jnp.bfloat16),
            jax.ShapeDtypeStruct((LANES, LANES), jnp.float32),
        ]
    else:
        out_shape = field_shape
    operands = [band, *messages] + ([] if first else [field])
    return pl.pallas_call(
        functools.partial(field_kernel, plan, first, last, count),
        out_shape=out_shape,
        in_specs=[pl.BlockSpec(memory_space=pltpu.SMEM)] + [vmem] * (len(operands) - 1),
        out_specs=[vmem] * 2 if last else vmem,
        input_output_aliases={} if first or last else {len(operands) - 1: 0},
        scratch_shapes=[pltpu.VMEM((count, plan.slots * BLOCK, plan.depth), jnp.bfloat16)],
        compiler_params=pltpu.CompilerParams(vmem_limit_bytes=24 << 20),
        cost_estimate=pl.CostEstimate(flops=3 << 30, bytes_accessed=6 << 20, transcendentals=0),
        name="field_and_gram" if last else "field",
    )(*operands)


def basis_kernel(plan, weight_ref, split_ref, out_ref):
    weight = weight_ref[...]
    high = weight.astype(jnp.bfloat16)
    low = (weight - high.astype(jnp.float32)).astype(jnp.bfloat16)
    both = jnp.concatenate([high, low], axis=1)
    right = jnp.concatenate([both, both], axis=0)
    for station in range(plan.band):
        product = jnp.dot(split_ref[station], right, preferred_element_type=jnp.float32)
        total = product[:, :LANES] + product[:, LANES:]
        out_ref[pl.ds(station, plan.segment, stride=plan.band), :] = total[: plan.segment]


def make_basis(plan, weight, split):
    vmem = pl.BlockSpec(memory_space=pltpu.VMEM)
    rows = pl.pallas_call(
        functools.partial(basis_kernel, plan),
        out_shape=jax.ShapeDtypeStruct((plan.segment * plan.band, LANES), jnp.float32),
        in_specs=[vmem, vmem],
        out_specs=vmem,
        compiler_params=pltpu.CompilerParams(vmem_limit_bytes=24 << 20),
        name="basis",
    )(weight, split)
    return rows.reshape(plan.segment, plan.band, LANES).transpose(1, 0, 2)


def sum_four(value, axis, bit):
    return value + sum(swapped(value, axis, k << bit) for k in (1, 2, 3))


def sum_over(value, axis, bits):
    while bits:
        if axis == "grp" and len(bits) > 1:
            value = sum_four(value, axis, bits[0])
            bits = bits[2:]
        else:
            value = value + swapped(value, axis, 1 << bits[0])
            bits = bits[1:]
    return value


def local(probes, kernel, pair_station, pair_count):
    length, probe_count = probes.shape[2:]
    slots, taps = kernel.shape[1], kernel.shape[3]
    band_size, grp_size = lax.axis_size("band"), lax.axis_size("grp")
    plan = Plan(length, taps, slots, band_size)
    band = lax.axis_index("band").astype(jnp.int32).reshape(1)
    messages = pack(
        plan, band, probes.reshape(length, probe_count), kernel.reshape(slots, taps), pair_station, pair_count
    )
    peers = band_size // 2
    arrived = [messages[0]] + [swapped(messages[k], "band", 2 * k) for k in range(1, peers)]
    field = None
    for k, value in enumerate(arrived):
        field = add_rows(plan, band, [value, swapped(value, "band", 1)], field, k == peers - 1)
    split, gram = field
    band_bits, grp_bits = (list(range(n.bit_length() - 1)) for n in (band_size, grp_size))
    gram = sum_over(gram, "band", band_bits[:1])
    gram = sum_over(gram, "grp", grp_bits)
    gram = sum_over(gram, "band", band_bits[1:])
    factor_low = jnp.linalg.cholesky(gram)
    identity = jnp.eye(probe_count, dtype=jnp.float32)
    inverse = lax.linalg.triangular_solve(factor_low, identity, left_side=True, lower=True)
    total_cells = grp_size * band_size * length
    weight = inverse.T * jnp.sqrt(jnp.float32(total_cells))
    return make_basis(plan, weight, split)


def solution(mesh):
    placed = (
        P(("grp", "band"), None, None, None),
        P(("grp", "band"), None, None, None),
        P(("grp", "band"), None),
        P(("grp", "band")),
    )
    return jax.shard_map(
        local, mesh=mesh, in_specs=placed, out_specs=P("grp", "band", None), check_vma=False
    )
```

time: 110 us -> 91.3 us (0.83)
  local copies, waits for them, and re-layouts: 9.35 us -> 1.16 us
  other arithmetic: 26.8 us -> 22.9 us
  waiting for transfers between devices: 37.4 us -> 34.8 us
  starting transfers between devices: 18.8 us -> 16.6 us
  Pallas kernels: 16.3 us -> 14.6 us
    dynamic_slice x3 -> x0, local copies, waits for them, and re-layouts: 3.94 us -> none  [the longest x1 1.44 us: local(): chip_starts[band ^ 2 * k]]
    pallas_call x2 -> x5, Pallas kernels: 14.8 us -> 12.1 us  [the longest x4 10 us: add_rows(): pl.pallas_call(functools.partial(field_kernel, plan, first, last, count),...]
    pallas_call x2 -> x1, local copies, waits for them, and re-layouts: 2.73 us -> 0.09 us  [add_rows(): pl.pallas_call(functools.partial(field_kernel, plan, first, last, count),...]
    ppermute x12 -> x13, waiting for transfers between devices: 37.4 us -> 34.8 us  [swapped(): return lax.ppermute(value, axis, pairs)]
    add x6 -> x4, other arithmetic: 2.59 us -> 0.04 us  [the longest x3 0.03 us: sum_over(): value = value + swapped(value, axis, 1 << bits[0])]
    ppermute x12 -> x13, starting transfers between devices: 18.8 us -> 16.6 us  [swapped(): return lax.ppermute(value, axis, pairs)]
    unnamed x6 -> x2, local copies, waits for them, and re-layouts: 2.59 us -> 0.98 us
    another operation x1 -> x0, other arithmetic: 1.35 us -> none  [local(): jnp.stack([jnp.array(plan.offsets, jnp.int32)[band], jnp.array(plan.shift...]
  transfers between devices with their start and end apart: 12 -> 13, of which waited for: 7 -> 8; matrix products, arithmetic and copies ran while one was open for 4% -> 0% of each run, Pallas kernels for 0% -> 6%
where the time goes in v2:
time: 91.3 us; the launch traced here: 91.1 us
  waiting for transfers between devices  34.8 us (38%)
  other arithmetic  22.9 us (25%)
  starting transfers between devices  16.6 us (18%)
  Pallas kernels  14.6 us (16%)
  local copies, waits for them, and re-layouts  1.16 us (1%)
    ppermute x13, waiting for transfers between devices, swapped(): return lax.ppermute(value, axis, pairs)  34.8 us
    ppermute x13, starting transfers between devices, swapped(): return lax.ppermute(value, axis, pairs)  16.6 us
    another operation x3, other arithmetic, local(): factor_low = jnp.linalg.cholesky(gram)  12.4 us
    another operation x2, other arithmetic, local(): lax.linalg.triangular_solve(factor_low, identity, left_side=True, lower=T...  10.5 us
    pallas_call x4, Pallas kernels, add_rows(): pl.pallas_call(functools.partial(field_kernel, plan, first, last, count),...  10 us
    pallas_call x1, Pallas kernels, pack(): pl.pallas_call(functools.partial(pack_kernel, plan), out_shape=[jax.Shape...  2.49 us
    pallas_call x1, Pallas kernels, make_basis(): pl.pallas_call(functools.partial(basis_kernel, plan), out_shape=jax.Shape...  2.11 us
  transfers between devices with their start and end apart: 13, of which 8 were waited for; matrix products, arithmetic and copies ran while one was open for 0% of the time, Pallas kernels for 6%

profile of v2, /device:TPU:0, one launch (start us, length us, event | category | flops | bytes accessed | tf_op | source)
XLA Modules:
  0.0 91.1 jit_solution(5849354875803299716)
XLA Ops:
  0.7 2.5 %pack_windows.1 = (bf16[1408,128]{1,0:T(8,128)(2,1)}, bf16[1408,128]{1,0:T(8,128)(2,1)}, bf16[1408,128]{1,0:T(8,128)(2,1)}, bf16[1408,128]{1,0:T(8,128)(2,1)}) custom-call(s32[1]{0:T(128)} %bitcast.band_hbm.band_ref, s32[1,5]{1,0:T(1,128)} %station_hbm.1, s32[1]{0:T(128)S(6)} %copy.12.count_hbm, bf16[5,289]{1,0:T(8,128)(2,1)} %bitcast.16, ...), custom_call_target="tpu_custom_call" | custom-call | bytes 4194304 | tf_op jit(solution)/shard_map/pack_windows/pallas_call | solution.py:109
  3.1 3.1 %collective-permute-start.4 = (bf16[1408,128]{1,0:T(8,128)(2,1)}, bf16[1408,128]{1,0:T(8,128)(2,1)S(1)}, u32[]{:S(2)}, u32[]{:S(2)}) collective-permute-start(bf16[1408,128]{1,0:T(8,128)(2,1)} %get-tuple-element.13), channel_id=1, source_target_pairs={{0,2},{1,3},{2,0},{3,1},{4,6},{5,7},{6,4},{7,5},{8,10},{9,11},{10,... | collective-permute-start | bytes 1081352 | tf_op jit(solution)/shard_map/ppermute | solution.py:21
  6.2 2.6 %collective-permute-start.2 = (bf16[1408,128]{1,0:T(8,128)(2,1)}, bf16[1408,128]{1,0:T(8,128)(2,1)S(1)}, u32[]{:S(2)}, u32[]{:S(2)}) collective-permute-start(bf16[1408,128]{1,0:T(8,128)(2,1)} %get-tuple-element.12), channel_id=1, source_target_pairs={{0,4},{1,5},{2,6},{3,7},{4,0},{5,1},{6,2},{7,3},{8,12},{9,13},{10,... | collective-permute-start | bytes 1081352 | tf_op jit(solution)/shard_map/ppermute | solution.py:21
  8.8 13.0 %collective-permute-done.4.rest_0_ = bf16[1408,128]{1,0:T(8,128)(2,1)S(1)} collective-permute-done((bf16[1408,128]{1,0:T(8,128)(2,1)}, bf16[1408,128]{1,0:T(8,128)(2,1)S(1)}, u32[]{:S(2)}, u32[]{:S(2)}) %collective-permute-start.4) | collective-permute-done | bytes 360480 | tf_op jit(solution)/shard_map/ppermute | solution.py:21
  21.8 12.3 %collective-permute-done.2.rest_0_ = bf16[1408,128]{1,0:T(8,128)(2,1)S(1)} collective-permute-done((bf16[1408,128]{1,0:T(8,128)(2,1)}, bf16[1408,128]{1,0:T(8,128)(2,1)S(1)}, u32[]{:S(2)}, u32[]{:S(2)}) %collective-permute-start.2) | collective-permute-done | bytes 360480 | tf_op jit(solution)/shard_map/ppermute | solution.py:21
  34.1 1.0 %copy-done = bf16[1408,128]{1,0:T(8,128)(2,1)S(1)} copy-done((bf16[1408,128]{1,0:T(8,128)(2,1)S(1)}, bf16[1408,128]{1,0:T(8,128)(2,1)}, u32[]{:S(2)}) %copy-start) | copy-done | bytes 360472
  35.1 1.9 %field.3.rest_2_ = f32[8,544,128]{2,1,0:T(8,128)S(1)} custom-call(s32[1]{0:T(128)} %bitcast.band_hbm.band_ref, bf16[1408,128]{1,0:T(8,128)(2,1)S(1)} %copy-done, bf16[1408,128]{1,0:T(8,128)(2,1)S(1)} %collective-permute-done.6.rest_1_), custom_call_target="tpu_custom_call" | custom-call | flops 3221225472 | bytes 6291456 | tf_op jit(solution)/shard_map/field/pallas_call | solution.py:221
  37.0 0.6 collective-permute-start.1
  37.6 1.8 %field.4.rest_2_ = f32[8,544,128]{2,1,0:T(8,128)S(1)} custom-call(s32[1]{0:T(128)} %bitcast.band_hbm.band_ref, bf16[1408,128]{1,0:T(8,128)(2,1)S(1)} %collective-permute-done.4.rest_0_, bf16[1408,128]{1,0:T(8,128)(2,1)S(1)} %collective-permute-done.5.rest_1_, f32[8,544,128]{2,1,0:T(8,128)S(1)} %field.3.rest_2_), custom_call_target="tpu_custom_call", output_to_operand_aliasing={{}: (3, {})} | custom-call | flops 3221225472 | bytes 6291456 | tf_op jit(solution)/shard_map/field/pallas_call | solution.py:221
  39.4 1.8 %field.5.rest_2_ = f32[8,544,128]{2,1,0:T(8,128)S(1)} custom-call(s32[1]{0:T(128)} %bitcast.band_hbm.band_ref, bf16[1408,128]{1,0:T(8,128)(2,1)S(1)} %collective-permute-done.2.rest_0_, bf16[1408,128]{1,0:T(8,128)(2,1)S(1)} %collective-permute-done.3.rest_1_, f32[8,544,128]{2,1,0:T(8,128)S(1)} %field.4.rest_2_), custom_call_target="tpu_custom_call", output_to_operand_aliasing={{}: (3, {})} | custom-call | flops 3221225472 | bytes 6291456 | tf_op jit(solution)/shard_map/field/pallas_call | solution.py:221
  41.2 4.6 %field_and_gram.1 = (bf16[8,544,256]{2,1,0:T(8,128)(2,1)S(1)}, f32[128,128]{1,0:T(8,128)S(1)}) custom-call(s32[1]{0:T(128)} %bitcast.band_hbm.band_ref, bf16[1408,128]{1,0:T(8,128)(2,1)S(1)} %collective-permute-done.rest_0_, bf16[1408,128]{1,0:T(8,128)(2,1)S(1)} %collective-permute-done.1.rest_1_, f32[8,544,128]{2,1,0:T(8,128)S(1)} %field.5.rest_2_), custom_call_target="tpu_custom_call" | custom-call | flops 3221225472 | bytes 6291456 | tf_op jit(solution)/shard_map/field_and_gram/pallas_call | solution.py:221
  46.0 1.2 %collective-permute-done.7 = f32[128,128]{0,1:T(8,128)S(1)} collective-permute-done((f32[128,128]{0,1:T(8,128)S(1)}, f32[128,128]{0,1:T(8,128)S(1)}, u32[]{:S(2)}, u32[]{:S(2)}) %collective-permute-start.7) | collective-permute-done | bytes 65568 | tf_op jit(solution)/shard_map/ppermute | solution.py:21
  47.2 2.5 %collective-permute-start.10 = (f32[128,128]{0,1:T(8,128)S(1)}, f32[128,128]{0,1:T(8,128)S(1)}, u32[]{:S(2)}, u32[]{:S(2)}) collective-permute-start(f32[128,128]{0,1:T(8,128)S(1)} %add.29), channel_id=1, source_target_pairs={{0,24},{8,16},{16,8},{24,0},{1,25},{9,17},{17,9},{25,1},{2,26},{10... | collective-permute-start | bytes 196616 | tf_op jit(solution)/shard_map/ppermute | solution.py:21
  50.8 2.1 %collective-permute-done.10 = f32[128,128]{0,1:T(8,128)S(1)} collective-permute-done((f32[128,128]{0,1:T(8,128)S(1)}, f32[128,128]{0,1:T(8,128)S(1)}, u32[]{:S(2)}, u32[]{:S(2)}) %collective-permute-start.10) | collective-permute-done | bytes 65568 | tf_op jit(solution)/shard_map/ppermute | solution.py:21
  52.8 1.2 %collective-permute-done.8 = f32[128,128]{0,1:T(8,128)S(1)} collective-permute-done((f32[128,128]{0,1:T(8,128)S(1)}, f32[128,128]{0,1:T(8,128)S(1)}, u32[]{:S(2)}, u32[]{:S(2)}) %collective-permute-start.8) | collective-permute-done | bytes 65568 | tf_op jit(solution)/shard_map/ppermute | solution.py:21
  54.5 3.6 %collective-permute-start.11 = (f32[128,128]{0,1:T(8,128)S(1)}, f32[128,128]{0,1:T(8,128)S(1)}, u32[]{:S(2)}, u32[]{:S(2)}) collective-permute-start(f32[128,128]{0,1:T(8,128)S(1)} %add_add_fusion), channel_id=1, source_target_pairs={{0,2},{1,3},{2,0},{3,1},{4,6},{5,7},{6,4},{7,5},{8,10},{9,11},{10,... | collective-permute-start | bytes 196616 | tf_op jit(solution)/shard_map/ppermute | solution.py:21
  58.2 2.2 %collective-permute-done.11 = f32[128,128]{0,1:T(8,128)S(1)} collective-permute-done((f32[128,128]{0,1:T(8,128)S(1)}, f32[128,128]{0,1:T(8,128)S(1)}, u32[]{:S(2)}, u32[]{:S(2)}) %collective-permute-start.11) | collective-permute-done | bytes 65568 | tf_op jit(solution)/shard_map/ppermute | solution.py:21
  60.4 3.1 %collective-permute-start.12 = (f32[128,128]{0,1:T(8,128)S(1)}, f32[128,128]{0,1:T(8,128)S(1)}, u32[]{:S(2)}, u32[]{:S(2)}) collective-permute-start(f32[128,128]{0,1:T(8,128)S(1)} %add.33), channel_id=1, source_target_pairs={{0,4},{1,5},{2,6},{3,7},{4,0},{5,1},{6,2},{7,3},{8,12},{9,13},{10,... | collective-permute-start | bytes 196616 | tf_op jit(solution)/shard_map/ppermute | solution.py:21
  63.5 2.2 %collective-permute-done.12 = f32[128,128]{0,1:T(8,128)S(1)} collective-permute-done((f32[128,128]{0,1:T(8,128)S(1)}, f32[128,128]{0,1:T(8,128)S(1)}, u32[]{:S(2)}, u32[]{:S(2)}) %collective-permute-start.12) | collective-permute-done | bytes 65568 | tf_op jit(solution)/shard_map/ppermute | solution.py:21
  65.9 11.7 %cholesky.14 = f32[128,128]{1,0:T(8,128)S(1)} custom-call(f32[128,128]{1,0:T(8,128)S(1)} %fusion.2), custom_call_target="Cholesky" | custom-call | tf_op jit(solution)/shard_map/jit(cholesky)/cholesky | solution.py:293
  77.6 0.6 compare_reduce_fusion
  78.3 0.7 fusion
  79.0 9.8 %custom-call.6 = f32[1,128,128]{1,2,0:T(8,128)S(1)} custom-call(f32[1,128,128]{2,1,0:T(8,128)S(1)} %fusion), custom_call_target="InvertDiagBlocksLowerTriangular" | custom-call | tf_op jit(solution)/shard_map/triangular_solve | solution.py:295
  89.0 2.1 %basis.1 = f32[4320,128]{1,0:T(8,128)} custom-call(f32[128,128]{1,0:T(8,128)S(1)} %convolution_multiply_fusion.weight_ref, bf16[8,544,256]{2,1,0:T(8,128)(2,1)S(1)} %get-tuple-element.16.split_ref), custom_call_target="tpu_custom_call" | custom-call | tf_op jit(solution)/shard_map/basis/pallas_call | solution.py:248
  (23 shorter events, 2.2 us)
Async XLA Ops:
  3.1 18.7 %collective-permute-start.4 = (bf16[1408,128]{1,0:T(8,128)(2,1)}, bf16[1408,128]{1,0:T(8,128)(2,1)S(1)}, u32[]{:S(2)}, u32[]{:S(2)}) collective-permute-start(bf16[1408,128]{1,0:T(8,128)(2,1)} %get-tuple-element.13), channel_id=1, source_target_pairs={{0,2},{1,3},{2,0},{3,1},{4,6},{5,7},{6,4},{7,5},{8,10},{9,11},{10,... | collective-permute-start | bytes 1081352 | tf_op jit(solution)/shard_map/ppermute | solution.py:21
  6.2 27.9 %collective-permute-start.2 = (bf16[1408,128]{1,0:T(8,128)(2,1)}, bf16[1408,128]{1,0:T(8,128)(2,1)S(1)}, u32[]{:S(2)}, u32[]{:S(2)}) collective-permute-start(bf16[1408,128]{1,0:T(8,128)(2,1)} %get-tuple-element.12), channel_id=1, source_target_pairs={{0,4},{1,5},{2,6},{3,7},{4,0},{5,1},{6,2},{7,3},{8,12},{9,13},{10,... | collective-permute-start | bytes 1081352 | tf_op jit(solution)/shard_map/ppermute | solution.py:21
  8.8 25.3 %collective-permute-start.6 = (bf16[1408,128]{1,0:T(8,128)(2,1)}, bf16[1408,128]{1,0:T(8,128)(2,1)S(1)}, u32[]{:S(2)}, u32[]{:S(2)}) collective-permute-start(bf16[1408,128]{1,0:T(8,128)(2,1)} %get-tuple-element.14.rest_0_), channel_id=1, source_target_pairs={{0,1},{1,0},{2,3},{3,2},{4,5},{5,4},{6,7},{7,6},{8,9},{9,8},{10,11... | collective-permute-start | bytes 1081352 | tf_op jit(solution)/shard_map/ppermute | solution.py:21
  8.8 28.2 %collective-permute-start = (bf16[1408,128]{1,0:T(8,128)(2,1)}, bf16[1408,128]{1,0:T(8,128)(2,1)S(1)}, u32[]{:S(2)}, u32[]{:S(2)}) collective-permute-start(bf16[1408,128]{1,0:T(8,128)(2,1)} %get-tuple-element.11), channel_id=1, source_target_pairs={{0,6},{1,7},{2,4},{3,5},{4,2},{5,3},{6,0},{7,1},{8,14},{9,15},{10,... | collective-permute-start | bytes 1081352 | tf_op jit(solution)/shard_map/ppermute | solution.py:21
  21.8 15.8 %collective-permute-start.5 = (bf16[1408,128]{1,0:T(8,128)(2,1)S(1)}, bf16[1408,128]{1,0:T(8,128)(2,1)S(1)}, u32[]{:S(2)}, u32[]{:S(2)}) collective-permute-start(bf16[1408,128]{1,0:T(8,128)(2,1)S(1)} %collective-permute-done.4.rest_0_), channel_id=1, source_target_pairs={{0,1},{1,0},{2,3},{3,2},{4,5},{5,4},{6,7},{7,6},{8,9},{9,8},{10,11... | collective-permute-start | bytes 1081352 | tf_op jit(solution)/shard_map/ppermute | solution.py:21
  34.1 5.2 %collective-permute-start.3 = (bf16[1408,128]{1,0:T(8,128)(2,1)S(1)}, bf16[1408,128]{1,0:T(8,128)(2,1)S(1)}, u32[]{:S(2)}, u32[]{:S(2)}) collective-permute-start(bf16[1408,128]{1,0:T(8,128)(2,1)S(1)} %collective-permute-done.2.rest_0_), channel_id=1, source_target_pairs={{0,1},{1,0},{2,3},{3,2},{4,5},{5,4},{6,7},{7,6},{8,9},{9,8},{10,11... | collective-permute-start | bytes 1081352 | tf_op jit(solution)/shard_map/ppermute | solution.py:21
  34.1 1.0 %copy-start = (bf16[1408,128]{1,0:T(8,128)(2,1)S(1)}, bf16[1408,128]{1,0:T(8,128)(2,1)}, u32[]{:S(2)}) copy-start(bf16[1408,128]{1,0:T(8,128)(2,1)} %get-tuple-element.14.rest_0_) | copy-start | bytes 1081348
  37.0 4.2 %collective-permute-start.1 = (bf16[1408,128]{1,0:T(8,128)(2,1)S(1)}, bf16[1408,128]{1,0:T(8,128)(2,1)S(1)}, u32[]{:S(2)}, u32[]{:S(2)}) collective-permute-start(bf16[1408,128]{1,0:T(8,128)(2,1)S(1)} %collective-permute-done.rest_0_), channel_id=1, source_target_pairs={{0,1},{1,0},{2,3},{3,2},{4,5},{5,4},{6,7},{7,6},{8,9},{9,8},{10,11... | collective-permute-start | bytes 1081352 | tf_op jit(solution)/shard_map/ppermute | solution.py:21
  45.9 1.3 %collective-permute-start.7 = (f32[128,128]{0,1:T(8,128)S(1)}, f32[128,128]{0,1:T(8,128)S(1)}, u32[]{:S(2)}, u32[]{:S(2)}) collective-permute-start(f32[128,128]{0,1:T(8,128)S(1)} %copy.8), channel_id=1, source_target_pairs={{0,1},{1,0},{2,3},{3,2},{4,5},{5,4},{6,7},{7,6},{8,9},{9,8},{10,11... | collective-permute-start | bytes 196616 | tf_op jit(solution)/shard_map/ppermute | solution.py:21
  47.2 5.6 %collective-permute-start.10 = (f32[128,128]{0,1:T(8,128)S(1)}, f32[128,128]{0,1:T(8,128)S(1)}, u32[]{:S(2)}, u32[]{:S(2)}) collective-permute-start(f32[128,128]{0,1:T(8,128)S(1)} %add.29), channel_id=1, source_target_pairs={{0,24},{8,16},{16,8},{24,0},{1,25},{9,17},{17,9},{25,1},{2,26},{10... | collective-permute-start | bytes 196616 | tf_op jit(solution)/shard_map/ppermute | solution.py:21
  49.7 4.3 %collective-permute-start.8 = (f32[128,128]{0,1:T(8,128)S(1)}, f32[128,128]{0,1:T(8,128)S(1)}, u32[]{:S(2)}, u32[]{:S(2)}) collective-permute-start(f32[128,128]{0,1:T(8,128)S(1)} %add.29), channel_id=1, source_target_pairs={{0,8},{8,0},{16,24},{24,16},{1,9},{9,1},{17,25},{25,17},{2,10},{10... | collective-permute-start | bytes 196616 | tf_op jit(solution)/shard_map/ppermute | solution.py:21
  50.3 4.3 %collective-permute-start.9 = (f32[128,128]{0,1:T(8,128)S(1)}, f32[128,128]{0,1:T(8,128)S(1)}, u32[]{:S(2)}, u32[]{:S(2)}) collective-permute-start(f32[128,128]{0,1:T(8,128)S(1)} %add.29), channel_id=1, source_target_pairs={{0,16},{8,24},{16,0},{24,8},{1,17},{9,25},{17,1},{25,9},{2,18},{10... | collective-permute-start | bytes 196616 | tf_op jit(solution)/shard_map/ppermute | solution.py:21
  54.5 5.9 %collective-permute-start.11 = (f32[128,128]{0,1:T(8,128)S(1)}, f32[128,128]{0,1:T(8,128)S(1)}, u32[]{:S(2)}, u32[]{:S(2)}) collective-permute-start(f32[128,128]{0,1:T(8,128)S(1)} %add_add_fusion), channel_id=1, source_target_pairs={{0,2},{1,3},{2,0},{3,1},{4,6},{5,7},{6,4},{7,5},{8,10},{9,11},{10,... | collective-permute-start | bytes 196616 | tf_op jit(solution)/shard_map/ppermute | solution.py:21
  60.4 5.4 %collective-permute-start.12 = (f32[128,128]{0,1:T(8,128)S(1)}, f32[128,128]{0,1:T(8,128)S(1)}, u32[]{:S(2)}, u32[]{:S(2)}) collective-permute-start(f32[128,128]{0,1:T(8,128)S(1)} %add.33), channel_id=1, source_target_pairs={{0,4},{1,5},{2,6},{3,7},{4,0},{5,1},{6,2},{7,3},{8,12},{9,13},{10,... | collective-permute-start | bytes 196616 | tf_op jit(solution)/shard_map/ppermute | solution.py:21

commit v3 on v2

--- a/solution.py
+++ b/solution.py
@@ -10,6 +10,7 @@
 LANES = 128
 TILE = 16
 BLOCK = 144
+PANEL = 16
 
 
 def up(value, step):
@@ -41,11 +42,20 @@
         self.right = up(max(max(self.chip_starts) + self.window - length, TILE), TILE)
         self.tap_rows = -(-taps // LANES)
         self.extra = up(slots * self.tap_rows + 1, TILE)
-        self.message = self.window + self.extra
+        self.whole = self.window + self.extra
+        self.near = self.sub + self.extra
+        self.sends = [(0, False)] + [(m, True) for m in (2, 3)][: band_size - 2]
+        self.sends += [(m, False) for m in range(4, band_size, 2)]
+
+    def size(self, near):
+        return self.sub if near else self.window
+
+    def shapes(self):
+        return [jax.ShapeDtypeStruct((self.size(near) + self.extra, LANES), jnp.bfloat16) for _, near in self.sends]
 
 
 def pack_kernel(plan, band_hbm, station_hbm, count_hbm, taps_hbm, probes_hbm, *rest):
-    peers = plan.band // 2
+    peers = len(plan.sends)
     messages = rest[:peers]
     band_ref, station_ref, count_ref, taps_ref, held, rows_f32, rows_bf, in_sems, out_sems = rest[peers:]
     length, left, right = plan.length, plan.left, plan.right
@@ -82,19 +92,22 @@
         copy.wait()
     band = band_ref[0]
     stores = []
-    for peer in range(peers):
-        chip = (band ^ (2 * peer)) // 2
-        start = pl.multiple_of((chip * (2 * plan.segment) + left - plan.half) // TILE * TILE, TILE)
+    for peer, (mask, near) in enumerate(plan.sends):
+        other = band ^ mask
+        if not near:
+            other = other // 2 * 2
+        start = pl.multiple_of((other * plan.segment + left - plan.half) // TILE * TILE, TILE)
+        size = plan.size(near)
         stores.append(
             pltpu.make_async_copy(
-                held.at[pl.ds(start, plan.window)],
-                messages[peer].at[pl.ds(0, plan.window)],
+                held.at[pl.ds(start, size)],
+                messages[peer].at[pl.ds(0, size)],
                 out_sems.at[2 * peer],
             )
         )
         stores.append(
             pltpu.make_async_copy(
-                rows_bf, messages[peer].at[pl.ds(plan.window, plan.extra)], out_sems.at[2 * peer + 1]
+                rows_bf, messages[peer].at[pl.ds(size, plan.extra)], out_sems.at[2 * peer + 1]
             )
         )
     for copy in stores:
@@ -104,11 +117,11 @@
 
 
 def pack(plan, band, probes, taps, station, count):
-    peers = plan.band // 2
+    peers = len(plan.sends)
     hbm = pl.BlockSpec(memory_space=pltpu.HBM)
     return pl.pallas_call(
         functools.partial(pack_kernel, plan),
-        out_shape=[jax.ShapeDtypeStruct((plan.message, LANES), jnp.bfloat16)] * peers,
+        out_shape=plan.shapes(),
         in_specs=[hbm] * 5,
         out_specs=[pl.BlockSpec(memory_space=pl.ANY)] * peers,
         scratch_shapes=[
@@ -132,7 +145,9 @@
     offset, shift = place
     lanes = up(plan.depth, LANES)
     for source, message in enumerate(messages):
-        rows = message[pl.ds(plan.window, plan.extra), :].astype(jnp.float32)
+        near = message.shape[0] == plan.near
+        source = source % 2
+        rows = message[pl.ds(plan.size(near), plan.extra), :].astype(jnp.float32)
         names = rows[plan.slots * plan.tap_rows : plan.slots * plan.tap_rows + 1, :]
         for slot in range(plan.slots):
             pieces = [
@@ -146,7 +161,7 @@
             table[source, pl.ds(slot * BLOCK, BLOCK), :] = rolled[:, : plan.depth].astype(jnp.bfloat16)
         right = jnp.concatenate(
             [
-                message[pl.ds(pl.multiple_of(offset + start, TILE), plan.depth), :]
+                message[pl.ds(start if near else pl.multiple_of(offset + start, TILE), plan.depth), :]
                 for start in plan.block_starts
             ],
             axis=1,
@@ -165,8 +180,8 @@
                 done = start + BLOCK
 
 
-def split_and_gram(plan, field, split_ref, gram_ref):
-    gram_ref[...] = jnp.zeros_like(gram_ref)
+def split_and_gram(plan, field, split_ref, gram_ref, total):
+    total[...] = jnp.zeros_like(total)
     inside = lax.broadcasted_iota(jnp.int32, (plan.rows, LANES), 0) < plan.segment
 
     @pl.loop(0, plan.band)
@@ -176,15 +191,12 @@
         low = (values - high.astype(jnp.float32)).astype(jnp.bfloat16)
         both = jnp.concatenate([high, low], axis=1)
         split_ref[station] = both
-        square = lax.dot_general(
+        total[...] += lax.dot_general(
             both, both, (((0,), (0,)), ((), ())), preferred_element_type=jnp.float32
         )
-        gram_ref[...] += (
-            square[:LANES, :LANES]
-            + square[:LANES, LANES:]
-            + square[LANES:, :LANES]
-            + square[LANES:, LANES:]
-        )
+
+    rows = total[pl.ds(0, LANES), :] + total[pl.ds(LANES, LANES), :]
+    gram_ref[...] = folded(rows[:, :LANES] + rows[:, LANES:])
 
 
 def field_kernel(plan, first, last, count, band_ref, *rest):
@@ -196,9 +208,9 @@
     aligned = base // TILE * TILE
     place = (aligned - chip // TILE * TILE, base - aligned)
     if last:
-        split_ref, gram_ref, table = rest
+        split_ref, gram_ref, table, total = rest
         add_products(plan, place, messages, field, table)
-        split_and_gram(plan, field, split_ref, gram_ref)
+        split_and_gram(plan, field, split_ref, gram_ref, total)
     else:
         out_ref, table = rest
         if first:
@@ -213,7 +225,7 @@
     if last:
         out_shape = [
             jax.ShapeDtypeStruct((plan.band, plan.rows, 2 * LANES), jnp.bfloat16),
-            jax.ShapeDtypeStruct((LANES, LANES), jnp.float32),
+            jax.ShapeDtypeStruct((LANES * 3 // 4, LANES), jnp.float32),
         ]
     else:
         out_shape = field_shape
@@ -224,35 +236,112 @@
         in_specs=[pl.BlockSpec(memory_space=pltpu.SMEM)] + [vmem] * (len(operands) - 1),
         out_specs=[vmem] * 2 if last else vmem,
         input_output_aliases={} if first or last else {len(operands) - 1: 0},
-        scratch_shapes=[pltpu.VMEM((count, plan.slots * BLOCK, plan.depth), jnp.bfloat16)],
+        scratch_shapes=[pltpu.VMEM((min(count, 2), plan.slots * BLOCK, plan.depth), jnp.bfloat16)]
+        + ([pltpu.VMEM((2 * LANES, 2 * LANES), jnp.float32)] if last else []),
         compiler_params=pltpu.CompilerParams(vmem_limit_bytes=24 << 20),
-        cost_estimate=pl.CostEstimate(flops=3 << 30, bytes_accessed=6 << 20, transcendentals=0),
+        cost_estimate=pl.CostEstimate(flops=1 << 20, bytes_accessed=1 << 16, transcendentals=0),
         name="field_and_gram" if last else "field",
     )(*operands)
 
 
-def basis_kernel(plan, weight_ref, split_ref, out_ref):
-    weight = weight_ref[...]
+def three_parts(value):
+    first = value.astype(jnp.bfloat16)
+    value = value - first.astype(jnp.float32)
+    second = value.astype(jnp.bfloat16)
+    return first, second, (value - second.astype(jnp.float32)).astype(jnp.bfloat16)
+
+
+def invert_factor(gram, left, right):
+    size = gram.shape[0]
+    row = lax.broadcasted_iota(jnp.int32, (size, size), 0)
+    col = lax.broadcasted_iota(jnp.int32, (size, size), 1)
+    left[...] = gram
+    right[...] = (row == col).astype(jnp.float32)
+    sub = lax.broadcasted_iota(jnp.int32, (8, size), 0)
+    for base in range(0, size, PANEL):
+        x, y = left[pl.ds(base, PANEL), :], right[pl.ds(base, PANEL), :]
+        square = {}
+        for i in range(PANEL):
+            for k in range(i, PANEL):
+                square[i, k] = jnp.broadcast_to(x[i : i + 1, base + k : base + k + 1], (8, size))
+        xs = [jnp.broadcast_to(x[i : i + 1, :], (8, size)) for i in range(PANEL)]
+        ys = [jnp.broadcast_to(y[i : i + 1, :], (8, size)) for i in range(PANEL)]
+        for i in range(PANEL):
+            scale = lax.rsqrt(square[i, i])
+            scaled = {k: square[i, k] * scale for k in range(i + 1, PANEL)}
+            xs[i], ys[i] = xs[i] * scale, ys[i] * scale
+            for k in range(i + 1, PANEL):
+                for m in range(k, PANEL):
+                    square[k, m] = square[k, m] - scaled[k] * scaled[m]
+                xs[k] = xs[k] - scaled[k] * xs[i]
+                ys[k] = ys[k] - scaled[k] * ys[i]
+        upper, lower = [], []
+        for tile in range(0, PANEL, 8):
+            u, v = xs[tile], ys[tile]
+            for i in range(1, 8):
+                u = jnp.where(sub == i, xs[tile + i], u)
+                v = jnp.where(sub == i, ys[tile + i], v)
+            upper.append(u)
+            lower.append(v)
+        u, v = jnp.concatenate(upper, axis=0), jnp.concatenate(lower, axis=0)
+        right[pl.ds(base, PANEL), :] = v
+        rest = size - base - PANEL
+        if rest:
+            a, b, c = three_parts(jnp.concatenate([u, v], axis=1))
+            one = jnp.concatenate([part[:, :size] for part in (a, a, b, a, b, c)], axis=0)
+            two = jnp.concatenate([a, b, a, c, b, a], axis=0)
+            update = lax.dot_general(
+                one, two, (((0,), (0,)), ((), ())), preferred_element_type=jnp.float32
+            )[base + PANEL :]
+            left[pl.ds(base + PANEL, rest), :] -= update[:, :size]
+            right[pl.ds(base + PANEL, rest), :] -= update[:, size:]
+
+
+def folded(gram):
+    half = LANES // 2
+    corner = pltpu.roll(gram[half:, :], half, 1)
+    first = lax.broadcasted_iota(jnp.int32, (half // 2, LANES), 1) < half
+    joined = jnp.where(first, corner[: half // 2], gram[half + half // 2 :, :])
+    return jnp.concatenate([gram[:half], joined], axis=0)
+
+
+def unfolded(packed):
+    half = LANES // 2
+    joined = packed[half:]
+    return jnp.concatenate([packed[:half], pltpu.roll(joined, half, 1), joined], axis=0)
+
+
+def basis_kernel(plan, scale, addends, *rest):
+    packed = rest[0][...]
+    for other in rest[1:addends]:
+        packed = packed + other[...]
+    split_ref, out_ref, left, right = rest[addends:]
+    invert_factor(unfolded(packed), left, right)
+    weight = right[...] * scale
     high = weight.astype(jnp.bfloat16)
     low = (weight - high.astype(jnp.float32)).astype(jnp.bfloat16)
-    both = jnp.concatenate([high, low], axis=1)
-    right = jnp.concatenate([both, both], axis=0)
+    turned = jnp.concatenate(
+        [jnp.concatenate([high, high], axis=1), jnp.concatenate([low, low], axis=1)], axis=0
+    )
     for station in range(plan.band):
-        product = jnp.dot(split_ref[station], right, preferred_element_type=jnp.float32)
+        product = lax.dot_general(
+            split_ref[station], turned, (((1,), (1,)), ((), ())), preferred_element_type=jnp.float32
+        )
         total = product[:, :LANES] + product[:, LANES:]
         out_ref[pl.ds(station, plan.segment, stride=plan.band), :] = total[: plan.segment]
 
 
-def make_basis(plan, weight, split):
+def make_basis(plan, scale, grams, split):
     vmem = pl.BlockSpec(memory_space=pltpu.VMEM)
     rows = pl.pallas_call(
-        functools.partial(basis_kernel, plan),
+        functools.partial(basis_kernel, plan, scale, len(grams)),
         out_shape=jax.ShapeDtypeStruct((plan.segment * plan.band, LANES), jnp.float32),
-        in_specs=[vmem, vmem],
+        in_specs=[vmem] * (len(grams) + 1),
         out_specs=vmem,
+        scratch_shapes=[pltpu.VMEM((LANES, LANES), jnp.float32)] * 2,
         compiler_params=pltpu.CompilerParams(vmem_limit_bytes=24 << 20),
-        name="basis",
-    )(weight, split)
+        name="factor_and_basis",
+    )(*grams, split)
     return rows.reshape(plan.segment, plan.band, LANES).transpose(1, 0, 2)
 
 
@@ -271,6 +360,10 @@
     return value
 
 
+def both_cores(values):
+    return values + [swapped(value, "band", 1) for value in values]
+
+
 def local(probes, kernel, pair_station, pair_count):
     length, probe_count = probes.shape[2:]
     slots, taps = kernel.shape[1], kernel.shape[3]
@@ -280,22 +373,23 @@
     messages = pack(
         plan, band, probes.reshape(length, probe_count), kernel.reshape(slots, taps), pair_station, pair_count
     )
-    peers = band_size // 2
-    arrived = [messages[0]] + [swapped(messages[k], "band", 2 * k) for k in range(1, peers)]
-    field = None
-    for k, value in enumerate(arrived):
-        field = add_rows(plan, band, [value, swapped(value, "band", 1)], field, k == peers - 1)
+    arrived = [
+        value if mask == 0 else swapped(value, "band", mask)
+        for value, (mask, near) in zip(messages, plan.sends)
+    ]
+    near = sum(near for _, near in plan.sends)
+    field = add_rows(plan, band, both_cores(arrived[:1]), None, False)
+    field = add_rows(plan, band, arrived[1 : 1 + near], field, False)
+    rest, field = lax.optimization_barrier((arrived[1 + near :], field))
+    field = add_rows(plan, band, both_cores(rest), field, True)
     split, gram = field
     band_bits, grp_bits = (list(range(n.bit_length() - 1)) for n in (band_size, grp_size))
     gram = sum_over(gram, "band", band_bits[:1])
     gram = sum_over(gram, "grp", grp_bits)
-    gram = sum_over(gram, "band", band_bits[1:])
-    factor_low = jnp.linalg.cholesky(gram)
-    identity = jnp.eye(probe_count, dtype=jnp.float32)
-    inverse = lax.linalg.triangular_solve(factor_low, identity, left_side=True, lower=True)
-    total_cells = grp_size * band_size * length
-    weight = inverse.T * jnp.sqrt(jnp.float32(total_cells))
-    return make_basis(plan, weight, split)
+    gram = sum_over(gram, "band", band_bits[1:-1])
+    grams = [gram, swapped(gram, "band", 1 << band_bits[-1])]
+    scale = float(grp_size * band_size * length) ** 0.5
+    return make_basis(plan, scale, grams, split)
 
 
 def solution(mesh):

time: 91.3 us -> 72.8 us (0.80)
  other arithmetic: 22.9 us -> 0.03 us
  Pallas kernels: 14.6 us -> 19.3 us
  starting transfers between devices: 16.6 us -> 19.9 us
  waiting for transfers between devices: 34.8 us -> 31.6 us
    another operation x5 -> x0, other arithmetic: 22.9 us -> none  [the longest x3 12.4 us: local(): factor_low = jnp.linalg.cholesky(gram)]
    pallas_call x2, Pallas kernels: 4.6 us -> 9.52 us  [the longest x1 7 us: make_basis(): pl.pallas_call(functools.partial(basis_kernel, plan, scale, len(grams)),...]
    ppermute x13, starting transfers between devices: 16.6 us -> 19.9 us  [swapped(): return lax.ppermute(value, axis, pairs)]
    ppermute x13, waiting for transfers between devices: 34.8 us -> 31.6 us  [swapped(): return lax.ppermute(value, axis, pairs)]
    pallas_call x4 -> x3, Pallas kernels: 10 us -> 9.82 us  [add_rows(): pl.pallas_call(functools.partial(field_kernel, plan, first, last, count),...]
  transfers between devices with their start and end apart: 13 -> 13, of which waited for: 8 -> 10; matrix products, arithmetic and copies ran while one was open for 0% -> 0% of each run, Pallas kernels for 6% -> 5%
where the time goes in v3:
time: 72.8 us; the launch traced here: 72.6 us
  waiting for transfers between devices  31.6 us (43%)
  starting transfers between devices  19.9 us (27%)
  Pallas kernels  19.3 us (27%)
  local copies, waits for them, and re-layouts  0.98 us (1%)
    ppermute x13, waiting for transfers between devices, swapped(): return lax.ppermute(value, axis, pairs)  31.6 us
    ppermute x13, starting transfers between devices, swapped(): return lax.ppermute(value, axis, pairs)  19.9 us
    pallas_call x3, Pallas kernels, add_rows(): pl.pallas_call(functools.partial(field_kernel, plan, first, last, count),...  9.82 us
    pallas_call x1, Pallas kernels, make_basis(): pl.pallas_call(functools.partial(basis_kernel, plan, scale, len(grams)),...  7 us
    pallas_call x1, Pallas kernels, pack(): pl.pallas_call(functools.partial(pack_kernel, plan), out_shape=plan.shape...  2.52 us
  transfers between devices with their start and end apart: 13, of which 10 were waited for; matrix products, arithmetic and copies ran while one was open for 0% of the time, Pallas kernels for 5%

profile of v3, /device:TPU:0, one launch (start us, length us, event | category | flops | bytes accessed | tf_op | source)
XLA Modules:
  0.0 72.6 jit_solution(12702885875927327603)
XLA Ops:
  0.7 2.5 %pack_windows.1 = (bf16[1408,128]{1,0:T(8,128)(2,1)}, bf16[864,128]{1,0:T(8,128)(2,1)}, bf16[864,128]{1,0:T(8,128)(2,1)}, bf16[1408,128]{1,0:T(8,128)(2,1)}, bf16[1408,128]{1,0:T(8,128)(2,1)}) custom-call(s32[1]{0:T(128)} %bitcast.band_hbm.band_ref, s32[1,5]{1,0:T(1,128)} %station_hbm.1, s32[1]{0:T(128)S(6)} %copy.7.count_hbm, bf16[5,289]{1,0:T(8,128)(2,1)} %bitcast.7, ...), custom_call_target="tpu_custom_call" | custom-call | bytes 4194304 | tf_op jit(solution)/shard_map/pack_windows/pallas_call | solution.py:122
  3.2 0.5 collective-permute-start.4
  3.7 3.7 %collective-permute-start = (bf16[1408,128]{1,0:T(8,128)(2,1)}, bf16[1408,128]{1,0:T(8,128)(2,1)S(1)}, u32[]{:S(2)}, u32[]{:S(2)}) collective-permute-start(bf16[1408,128]{1,0:T(8,128)(2,1)} %get-tuple-element.15), channel_id=1, source_target_pairs={{0,4},{1,5},{2,6},{3,7},{4,0},{5,1},{6,2},{7,3},{8,12},{9,13},{10,... | collective-permute-start | bytes 1081352 | tf_op jit(solution)/shard_map/ppermute | solution.py:22
  7.4 1.3 %collective-permute-start.1 = (bf16[1408,128]{1,0:T(8,128)(2,1)}, bf16[1408,128]{1,0:T(8,128)(2,1)S(1)}, u32[]{:S(2)}, u32[]{:S(2)}) collective-permute-start(bf16[1408,128]{1,0:T(8,128)(2,1)} %get-tuple-element.16), channel_id=1, source_target_pairs={{0,6},{1,7},{2,4},{3,5},{4,2},{5,3},{6,0},{7,1},{8,14},{9,15},{10,... | collective-permute-start | bytes 1081352 | tf_op jit(solution)/shard_map/ppermute | solution.py:22
  8.9 1.0 %collective-permute-start.3 = (bf16[864,128]{1,0:T(8,128)(2,1)}, bf16[864,128]{1,0:T(8,128)(2,1)S(1)}, u32[]{:S(2)}, u32[]{:S(2)}) collective-permute-start(bf16[864,128]{1,0:T(8,128)(2,1)} %get-tuple-element.18), channel_id=1, source_target_pairs={{0,3},{1,2},{2,1},{3,0},{4,7},{5,6},{6,5},{7,4},{8,11},{9,10},{10,... | collective-permute-start | bytes 663560 | tf_op jit(solution)/shard_map/ppermute | solution.py:22
  10.0 1.0 %copy-done = bf16[1408,128]{1,0:T(8,128)(2,1)S(1)} copy-done((bf16[1408,128]{1,0:T(8,128)(2,1)S(1)}, bf16[1408,128]{1,0:T(8,128)(2,1)}, u32[]{:S(2)}) %copy-start) | copy-done | bytes 360472
  10.9 1.9 %field.2.rest_2_ = f32[8,544,128]{2,1,0:T(8,128)S(1)} custom-call(s32[1]{0:T(128)} %bitcast.band_hbm.band_ref, bf16[1408,128]{1,0:T(8,128)(2,1)S(1)} %copy-done, bf16[1408,128]{1,0:T(8,128)(2,1)S(1)} %collective-permute-done.4.rest_1_), custom_call_target="tpu_custom_call" | custom-call | flops 1048576 | bytes 65536 | tf_op jit(solution)/shard_map/field/pallas_call | solution.py:233
  12.8 16.2 %collective-permute-done.2.rest_0_ = bf16[864,128]{1,0:T(8,128)(2,1)S(1)} collective-permute-done((bf16[864,128]{1,0:T(8,128)(2,1)}, bf16[864,128]{1,0:T(8,128)(2,1)S(1)}, u32[]{:S(2)}, u32[]{:S(2)}) %collective-permute-start.2) | collective-permute-done | bytes 221216 | tf_op jit(solution)/shard_map/ppermute | solution.py:22
  29.0 5.1 %collective-permute-done.3.rest_1_ = bf16[864,128]{1,0:T(8,128)(2,1)S(1)} collective-permute-done((bf16[864,128]{1,0:T(8,128)(2,1)}, bf16[864,128]{1,0:T(8,128)(2,1)S(1)}, u32[]{:S(2)}, u32[]{:S(2)}) %collective-permute-start.3) | collective-permute-done | bytes 221216 | tf_op jit(solution)/shard_map/ppermute | solution.py:22
  34.1 1.8 %field.3.rest_4_ = f32[8,544,128]{2,1,0:T(8,128)S(1)} custom-call(s32[1]{0:T(128)} %bitcast.band_hbm.band_ref, bf16[864,128]{1,0:T(8,128)(2,1)S(1)} %collective-permute-done.2.rest_0_, bf16[864,128]{1,0:T(8,128)(2,1)S(1)} %collective-permute-done.3.rest_1_, f32[8,544,128]{2,1,0:T(8,128)S(1)} %field.2.rest_2_), custom_call_target="tpu_custom_call", output_to_operand_aliasing={{}: (3, {})} | custom-call | flops 1048576 | bytes 65536 | tf_op jit(solution)/shard_map/field/pallas_call | solution.py:233
  35.9 1.0 %collective-permute-start.5 = (bf16[1408,128]{1,0:T(8,128)(2,1)S(1)}, bf16[1408,128]{1,0:T(8,128)(2,1)S(1)}, u32[]{:S(2)}, u32[]{:S(2)}) collective-permute-start(bf16[1408,128]{1,0:T(8,128)(2,1)S(1)} %collective-permute-done.rest_0_), channel_id=1, source_target_pairs={{0,1},{1,0},{2,3},{3,2},{4,5},{5,4},{6,7},{7,6},{8,9},{9,8},{10,11... | collective-permute-start | bytes 1081352 | tf_op jit(solution)/shard_map/ppermute | solution.py:22
  36.9 1.2 %collective-permute-done.5.rest_2_ = bf16[1408,128]{1,0:T(8,128)(2,1)S(1)} collective-permute-done((bf16[1408,128]{1,0:T(8,128)(2,1)S(1)}, bf16[1408,128]{1,0:T(8,128)(2,1)S(1)}, u32[]{:S(2)}, u32[]{:S(2)}) %collective-permute-start.5) | collective-permute-done | bytes 360480 | tf_op jit(solution)/shard_map/ppermute | solution.py:22
  38.1 0.5 collective-permute-done.6.rest_3_
  38.7 6.2 %field_and_gram.1 = (bf16[8,544,256]{2,1,0:T(8,128)(2,1)S(1)}, f32[96,128]{1,0:T(8,128)S(1)}) custom-call(s32[1]{0:T(128)} %bitcast.band_hbm.band_ref, bf16[1408,128]{1,0:T(8,128)(2,1)S(1)} %collective-permute-done.rest_0_, bf16[1408,128]{1,0:T(8,128)(2,1)S(1)} %collective-permute-done.1.rest_1_, bf16[1408,128]{1,0:T(8,128)(2,1)S(1)} %collective-permute-done.5.rest_2_, ...), custom_call_target="tpu_custom_call" | custom-call | flops 1048576 | bytes 65536 | tf_op jit(solution)/shard_map/field_and_gram/pallas_call | solution.py:233
  45.2 0.9 %collective-permute-done.7 = f32[96,128]{1,0:T(8,128)S(1)} collective-permute-done((f32[96,128]{1,0:T(8,128)S(1)}, f32[96,128]{1,0:T(8,128)S(1)}, u32[]{:S(2)}, u32[]{:S(2)}) %collective-permute-start.7) | collective-permute-done | bytes 49184 | tf_op jit(solution)/shard_map/ppermute | solution.py:22
  46.1 2.6 %collective-permute-start.10 = (f32[96,128]{1,0:T(8,128)S(1)}, f32[96,128]{1,0:T(8,128)S(1)}, u32[]{:S(2)}, u32[]{:S(2)}) collective-permute-start(f32[96,128]{1,0:T(8,128)S(1)} %add.15), channel_id=1, source_target_pairs={{0,24},{8,16},{16,8},{24,0},{1,25},{9,17},{17,9},{25,1},{2,26},{10... | collective-permute-start | bytes 147464 | tf_op jit(solution)/shard_map/ppermute | solution.py:22
  48.7 0.5 collective-permute-start.9
  49.7 1.5 %collective-permute-done.10 = f32[96,128]{1,0:T(8,128)S(1)} collective-permute-done((f32[96,128]{1,0:T(8,128)S(1)}, f32[96,128]{1,0:T(8,128)S(1)}, u32[]{:S(2)}, u32[]{:S(2)}) %collective-permute-start.10) | collective-permute-done | bytes 49184 | tf_op jit(solution)/shard_map/ppermute | solution.py:22
  51.2 1.6 %collective-permute-done.9 = f32[96,128]{1,0:T(8,128)S(1)} collective-permute-done((f32[96,128]{1,0:T(8,128)S(1)}, f32[96,128]{1,0:T(8,128)S(1)}, u32[]{:S(2)}, u32[]{:S(2)}) %collective-permute-start.9) | collective-permute-done | bytes 49184 | tf_op jit(solution)/shard_map/ppermute | solution.py:22
  53.3 4.2 %collective-permute-start.11 = (f32[96,128]{1,0:T(8,128)S(1)}, f32[96,128]{1,0:T(8,128)S(1)}, u32[]{:S(2)}, u32[]{:S(2)}) collective-permute-start(f32[96,128]{1,0:T(8,128)S(1)} %add_add_fusion), channel_id=1, source_target_pairs={{0,2},{1,3},{2,0},{3,1},{4,6},{5,7},{6,4},{7,5},{8,10},{9,11},{10,... | collective-permute-start | bytes 147464 | tf_op jit(solution)/shard_map/ppermute | solution.py:22
  57.5 2.1 %collective-permute-done.11 = f32[96,128]{1,0:T(8,128)S(1)} collective-permute-done((f32[96,128]{1,0:T(8,128)S(1)}, f32[96,128]{1,0:T(8,128)S(1)}, u32[]{:S(2)}, u32[]{:S(2)}) %collective-permute-start.11) | collective-permute-done | bytes 49184 | tf_op jit(solution)/shard_map/ppermute | solution.py:22
  59.5 4.0 %collective-permute-start.12 = (f32[96,128]{1,0:T(8,128)S(1)}, f32[96,128]{1,0:T(8,128)S(1)}, u32[]{:S(2)}, u32[]{:S(2)}) collective-permute-start(f32[96,128]{1,0:T(8,128)S(1)} %add.19.rest_0_), channel_id=1, source_target_pairs={{0,4},{1,5},{2,6},{3,7},{4,0},{5,1},{6,2},{7,3},{8,12},{9,13},{10,... | collective-permute-start | bytes 147464 | tf_op jit(solution)/shard_map/ppermute | solution.py:22
  63.5 2.1 %collective-permute-done.12.rest_1_ = f32[96,128]{1,0:T(8,128)S(1)} collective-permute-done((f32[96,128]{1,0:T(8,128)S(1)}, f32[96,128]{1,0:T(8,128)S(1)}, u32[]{:S(2)}, u32[]{:S(2)}) %collective-permute-start.12) | collective-permute-done | bytes 49184 | tf_op jit(solution)/shard_map/ppermute | solution.py:22
  65.6 7.0 %factor_and_basis.1 = f32[4320,128]{1,0:T(8,128)} custom-call(f32[96,128]{1,0:T(8,128)S(1)} %add.19.rest_0_, f32[96,128]{1,0:T(8,128)S(1)} %collective-permute-done.12.rest_1_, bf16[8,544,256]{2,1,0:T(8,128)(2,1)S(1)} %get-tuple-element.24.rest_2_), custom_call_target="tpu_custom_call" | custom-call | tf_op jit(solution)/shard_map/factor_and_basis/pallas_call | solution.py:336
  (12 shorter events, 1.7 us)
Async XLA Ops:
  3.2 6.8 %collective-permute-start.4 = (bf16[1408,128]{1,0:T(8,128)(2,1)}, bf16[1408,128]{1,0:T(8,128)(2,1)S(1)}, u32[]{:S(2)}, u32[]{:S(2)}) collective-permute-start(bf16[1408,128]{1,0:T(8,128)(2,1)} %get-tuple-element.19.rest_0_), channel_id=1, source_target_pairs={{0,1},{1,0},{2,3},{3,2},{4,5},{5,4},{6,7},{7,6},{8,9},{9,8},{10,11... | collective-permute-start | bytes 1081352 | tf_op jit(solution)/shard_map/ppermute | solution.py:22
  3.7 32.1 %collective-permute-start = (bf16[1408,128]{1,0:T(8,128)(2,1)}, bf16[1408,128]{1,0:T(8,128)(2,1)S(1)}, u32[]{:S(2)}, u32[]{:S(2)}) collective-permute-start(bf16[1408,128]{1,0:T(8,128)(2,1)} %get-tuple-element.15), channel_id=1, source_target_pairs={{0,4},{1,5},{2,6},{3,7},{4,0},{5,1},{6,2},{7,3},{8,12},{9,13},{10,... | collective-permute-start | bytes 1081352 | tf_op jit(solution)/shard_map/ppermute | solution.py:22
  7.4 28.5 %collective-permute-start.1 = (bf16[1408,128]{1,0:T(8,128)(2,1)}, bf16[1408,128]{1,0:T(8,128)(2,1)S(1)}, u32[]{:S(2)}, u32[]{:S(2)}) collective-permute-start(bf16[1408,128]{1,0:T(8,128)(2,1)} %get-tuple-element.16), channel_id=1, source_target_pairs={{0,6},{1,7},{2,4},{3,5},{4,2},{5,3},{6,0},{7,1},{8,14},{9,15},{10,... | collective-permute-start | bytes 1081352 | tf_op jit(solution)/shard_map/ppermute | solution.py:22
  8.7 20.3 %collective-permute-start.2 = (bf16[864,128]{1,0:T(8,128)(2,1)}, bf16[864,128]{1,0:T(8,128)(2,1)S(1)}, u32[]{:S(2)}, u32[]{:S(2)}) collective-permute-start(bf16[864,128]{1,0:T(8,128)(2,1)} %get-tuple-element.17), channel_id=1, source_target_pairs={{0,2},{1,3},{2,0},{3,1},{4,6},{5,7},{6,4},{7,5},{8,10},{9,11},{10,... | collective-permute-start | bytes 663560 | tf_op jit(solution)/shard_map/ppermute | solution.py:22
  8.9 25.1 %collective-permute-start.3 = (bf16[864,128]{1,0:T(8,128)(2,1)}, bf16[864,128]{1,0:T(8,128)(2,1)S(1)}, u32[]{:S(2)}, u32[]{:S(2)}) collective-permute-start(bf16[864,128]{1,0:T(8,128)(2,1)} %get-tuple-element.18), channel_id=1, source_target_pairs={{0,3},{1,2},{2,1},{3,0},{4,7},{5,6},{6,5},{7,4},{8,11},{9,10},{10,... | collective-permute-start | bytes 663560 | tf_op jit(solution)/shard_map/ppermute | solution.py:22
  10.0 1.0 %copy-start = (bf16[1408,128]{1,0:T(8,128)(2,1)S(1)}, bf16[1408,128]{1,0:T(8,128)(2,1)}, u32[]{:S(2)}) copy-start(bf16[1408,128]{1,0:T(8,128)(2,1)} %get-tuple-element.19.rest_0_) | copy-start | bytes 1081348
  35.9 2.3 %collective-permute-start.5 = (bf16[1408,128]{1,0:T(8,128)(2,1)S(1)}, bf16[1408,128]{1,0:T(8,128)(2,1)S(1)}, u32[]{:S(2)}, u32[]{:S(2)}) collective-permute-start(bf16[1408,128]{1,0:T(8,128)(2,1)S(1)} %collective-permute-done.rest_0_), channel_id=1, source_target_pairs={{0,1},{1,0},{2,3},{3,2},{4,5},{5,4},{6,7},{7,6},{8,9},{9,8},{10,11... | collective-permute-start | bytes 1081352 | tf_op jit(solution)/shard_map/ppermute | solution.py:22
  36.8 1.8 %collective-permute-start.6 = (bf16[1408,128]{1,0:T(8,128)(2,1)S(1)}, bf16[1408,128]{1,0:T(8,128)(2,1)S(1)}, u32[]{:S(2)}, u32[]{:S(2)}) collective-permute-start(bf16[1408,128]{1,0:T(8,128)(2,1)S(1)} %collective-permute-done.1.rest_1_), channel_id=1, source_target_pairs={{0,1},{1,0},{2,3},{3,2},{4,5},{5,4},{6,7},{7,6},{8,9},{9,8},{10,11... | collective-permute-start | bytes 1081352 | tf_op jit(solution)/shard_map/ppermute | solution.py:22
  44.8 1.3 %collective-permute-start.7 = (f32[96,128]{1,0:T(8,128)S(1)}, f32[96,128]{1,0:T(8,128)S(1)}, u32[]{:S(2)}, u32[]{:S(2)}) collective-permute-start(f32[96,128]{1,0:T(8,128)S(1)} %get-tuple-element.23), channel_id=1, source_target_pairs={{0,1},{1,0},{2,3},{3,2},{4,5},{5,4},{6,7},{7,6},{8,9},{9,8},{10,11... | collective-permute-start | bytes 147464 | tf_op jit(solution)/shard_map/ppermute | solution.py:22
  46.1 5.1 %collective-permute-start.10 = (f32[96,128]{1,0:T(8,128)S(1)}, f32[96,128]{1,0:T(8,128)S(1)}, u32[]{:S(2)}, u32[]{:S(2)}) collective-permute-start(f32[96,128]{1,0:T(8,128)S(1)} %add.15), channel_id=1, source_target_pairs={{0,24},{8,16},{16,8},{24,0},{1,25},{9,17},{17,9},{25,1},{2,26},{10... | collective-permute-start | bytes 147464 | tf_op jit(solution)/shard_map/ppermute | solution.py:22
  48.7 4.1 %collective-permute-start.9 = (f32[96,128]{1,0:T(8,128)S(1)}, f32[96,128]{1,0:T(8,128)S(1)}, u32[]{:S(2)}, u32[]{:S(2)}) collective-permute-start(f32[96,128]{1,0:T(8,128)S(1)} %add.15), channel_id=1, source_target_pairs={{0,16},{8,24},{16,0},{24,8},{1,17},{9,25},{17,1},{25,9},{2,18},{10... | collective-permute-start | bytes 147464 | tf_op jit(solution)/shard_map/ppermute | solution.py:22
  49.2 4.1 %collective-permute-start.8 = (f32[96,128]{1,0:T(8,128)S(1)}, f32[96,128]{1,0:T(8,128)S(1)}, u32[]{:S(2)}, u32[]{:S(2)}) collective-permute-start(f32[96,128]{1,0:T(8,128)S(1)} %add.15), channel_id=1, source_target_pairs={{0,8},{8,0},{16,24},{24,16},{1,9},{9,1},{17,25},{25,17},{2,10},{10... | collective-permute-start | bytes 147464 | tf_op jit(solution)/shard_map/ppermute | solution.py:22
  53.3 6.2 %collective-permute-start.11 = (f32[96,128]{1,0:T(8,128)S(1)}, f32[96,128]{1,0:T(8,128)S(1)}, u32[]{:S(2)}, u32[]{:S(2)}) collective-permute-start(f32[96,128]{1,0:T(8,128)S(1)} %add_add_fusion), channel_id=1, source_target_pairs={{0,2},{1,3},{2,0},{3,1},{4,6},{5,7},{6,4},{7,5},{8,10},{9,11},{10,... | collective-permute-start | bytes 147464 | tf_op jit(solution)/shard_map/ppermute | solution.py:22
  59.5 6.1 %collective-permute-start.12 = (f32[96,128]{1,0:T(8,128)S(1)}, f32[96,128]{1,0:T(8,128)S(1)}, u32[]{:S(2)}, u32[]{:S(2)}) collective-permute-start(f32[96,128]{1,0:T(8,128)S(1)} %add.19.rest_0_), channel_id=1, source_target_pairs={{0,4},{1,5},{2,6},{3,7},{4,0},{5,1},{6,2},{7,3},{8,12},{9,13},{10,... | collective-permute-start | bytes 147464 | tf_op jit(solution)/shard_map/ppermute | solution.py:22

commit v4 on v3

--- a/solution.py
+++ b/solution.py
@@ -9,8 +9,9 @@
 
 LANES = 128
 TILE = 16
-BLOCK = 144
+BLOCK = 32
 PANEL = 16
+CHUNK = 192
 
 
 def up(value, step):
@@ -37,12 +38,13 @@
         self.sub = self.block_starts[-1] + self.depth
         self.chip_starts = [self.aligned[b // 2 * 2] for b in range(band_size)]
         self.offsets = [a - c for a, c in zip(self.aligned, self.chip_starts)]
-        self.window = up(max(o + self.sub for o in self.offsets), TILE)
+        reach = self.segment + taps - 1
+        self.window = up(max(o + s + reach for o, s in zip(self.offsets, self.shifts)), TILE)
         self.left = -min(self.chip_starts)
-        self.right = up(max(max(self.chip_starts) + self.window - length, TILE), TILE)
         self.tap_rows = -(-taps // LANES)
         self.extra = up(slots * self.tap_rows + 1, TILE)
         self.whole = self.window + self.extra
+        assert max(self.offsets) + self.sub <= self.whole
         self.near = self.sub + self.extra
         self.sends = [(0, False)] + [(m, True) for m in (2, 3)][: band_size - 2]
         self.sends += [(m, False) for m in range(4, band_size, 2)]
@@ -54,25 +56,59 @@
         return [jax.ShapeDtypeStruct((self.size(near) + self.extra, LANES), jnp.bfloat16) for _, near in self.sends]
 
 
-def pack_kernel(plan, band_hbm, station_hbm, count_hbm, taps_hbm, probes_hbm, *rest):
+def pack_kernel(plan, band_ref, count_ref, station_hbm, taps_hbm, probes_hbm, *rest):
     peers = len(plan.sends)
     messages = rest[:peers]
-    band_ref, station_ref, count_ref, taps_ref, held, rows_f32, rows_bf, in_sems, out_sems = rest[peers:]
-    length, left, right = plan.length, plan.left, plan.right
-    loads = [
-        (probes_hbm.at[pl.ds(0, length)], held.at[pl.ds(left, length)]),
-        (probes_hbm.at[pl.ds(length - left, left)], held.at[pl.ds(0, left)]),
-        (probes_hbm.at[pl.ds(0, right)], held.at[pl.ds(left + length, right)]),
-        (band_hbm, band_ref),
-        (station_hbm, station_ref),
-        (count_hbm, count_ref),
-        (taps_hbm, taps_ref),
-    ]
+    station_ref, taps_ref, rows_f32, in_sems, out_sems = rest[peers:]
+    loads = [(station_hbm, station_ref), (taps_hbm, taps_ref)]
     loads = [pltpu.make_async_copy(a, b, in_sems.at[i]) for i, (a, b) in enumerate(loads)]
     for copy in loads:
         copy.start()
+
+    def windows(peer, act):
+        mask, near = plan.sends[peer]
+        size = plan.size(near)
+        other = band_ref[0] ^ mask
+        if not near:
+            other = other // 2 * 2
+        plain = other >= 0
+        for index in range(0, plan.band, 1 if near else 2):
+            start = plan.aligned[index]
+            if start < 0:
+                first, cut = plan.length + start, -start
+            elif start + size > plan.length:
+                first, cut = start, plan.length - start
+            else:
+                continue
+            plain = jnp.logical_and(plain, other != index)
+
+            @pl.when(other == index)
+            def _():
+                for piece, (low, to, count) in enumerate([(first, 0, cut), (0, cut, size - cut)]):
+                    act(
+                        pltpu.make_async_copy(
+                            probes_hbm.at[pl.ds(low, count)],
+                            messages[peer].at[pl.ds(to, count)],
+                            out_sems.at[2 * peer + piece],
+                        )
+                    )
+
+        @pl.when(plain)
+        def _():
+            low = (other * plan.segment + plan.left - plan.half) // TILE * TILE - plan.left
+            act(
+                pltpu.make_async_copy(
+                    probes_hbm.at[pl.ds(pl.multiple_of(low, TILE), size)],
+                    messages[peer].at[pl.ds(0, size)],
+                    out_sems.at[2 * peer],
+                )
+            )
+
+    order = list(range(peers))[::-1]
+    for peer in order:
+        windows(peer, lambda copy: copy.start())
     rows_f32[...] = jnp.zeros_like(rows_f32)
-    for copy in loads[3:]:
+    for copy in loads:
         copy.wait()
     live = count_ref[0]
     for slot in range(plan.slots):
@@ -87,58 +123,37 @@
     for slot in range(plan.slots):
         names = jnp.where(lane == slot, station_ref[0, slot].astype(jnp.float32), names)
     rows_f32[pl.ds(plan.slots * plan.tap_rows, 1), :] = names
-    rows_bf[...] = rows_f32[...].astype(jnp.bfloat16)
-    for copy in loads[:3]:
-        copy.wait()
-    band = band_ref[0]
-    stores = []
-    for peer, (mask, near) in enumerate(plan.sends):
-        other = band ^ mask
-        if not near:
-            other = other // 2 * 2
-        start = pl.multiple_of((other * plan.segment + left - plan.half) // TILE * TILE, TILE)
-        size = plan.size(near)
-        stores.append(
-            pltpu.make_async_copy(
-                held.at[pl.ds(start, size)],
-                messages[peer].at[pl.ds(0, size)],
-                out_sems.at[2 * peer],
-            )
-        )
-        stores.append(
-            pltpu.make_async_copy(
-                rows_bf, messages[peer].at[pl.ds(size, plan.extra)], out_sems.at[2 * peer + 1]
-            )
-        )
-    for copy in stores:
-        copy.start()
-    for copy in stores:
-        copy.wait()
+    rows_bf = rows_f32[...].astype(jnp.bfloat16)
+    for peer in order:
+        messages[peer][pl.ds(plan.size(plan.sends[peer][1]), plan.extra), :] = rows_bf
+    for peer in order:
+        windows(peer, lambda copy: copy.wait())
+
+
+def stay(value):
+    return pltpu.with_memory_space_constraint(value, pltpu.HBM)
 
 
 def pack(plan, band, probes, taps, station, count):
     peers = len(plan.sends)
     hbm = pl.BlockSpec(memory_space=pltpu.HBM)
+    smem = pl.BlockSpec(memory_space=pltpu.SMEM)
     return pl.pallas_call(
         functools.partial(pack_kernel, plan),
         out_shape=plan.shapes(),
-        in_specs=[hbm] * 5,
-        out_specs=[pl.BlockSpec(memory_space=pl.ANY)] * peers,
+        in_specs=[smem] * 2 + [hbm] * 3,
+        out_specs=[pl.BlockSpec(memory_space=pltpu.VMEM)] * peers,
         scratch_shapes=[
-            pltpu.SMEM((1,), jnp.int32),
             pltpu.SMEM(station.shape, jnp.int32),
-            pltpu.SMEM((1,), jnp.int32),
             pltpu.VMEM(taps.shape, jnp.bfloat16),
-            pltpu.VMEM((plan.left + plan.length + plan.right, LANES), jnp.bfloat16),
             pltpu.VMEM((plan.extra, LANES), jnp.float32),
-            pltpu.VMEM((plan.extra, LANES), jnp.bfloat16),
-            pltpu.SemaphoreType.DMA((7,)),
+            pltpu.SemaphoreType.DMA((2,)),
             pltpu.SemaphoreType.DMA((2 * peers,)),
         ],
-        compiler_params=pltpu.CompilerParams(vmem_limit_bytes=60 << 20),
+        compiler_params=pltpu.CompilerParams(vmem_limit_bytes=8 << 20),
         cost_estimate=pl.CostEstimate(flops=0, bytes_accessed=4 << 20, transcendentals=0),
         name="pack_windows",
-    )(band, station, count, taps, probes)
+    )(band, count, stay(station), stay(taps), stay(probes))
 
 
 def add_products(plan, place, messages, field, table):
@@ -166,10 +181,9 @@
             ],
             axis=1,
         )
+        products = jnp.dot(table[source], right, preferred_element_type=jnp.float32)
         for slot in range(plan.slots):
-            product = jnp.dot(
-                table[source, pl.ds(slot * BLOCK, BLOCK), :], right, preferred_element_type=jnp.float32
-            )
+            product = products[slot * BLOCK : (slot + 1) * BLOCK]
             station = names[0, slot].astype(jnp.int32)
             done = 0
             for i, start in enumerate(plan.block_starts):
@@ -184,8 +198,7 @@
     total[...] = jnp.zeros_like(total)
     inside = lax.broadcasted_iota(jnp.int32, (plan.rows, LANES), 0) < plan.segment
 
-    @pl.loop(0, plan.band)
-    def _(station):
+    for station in range(plan.band):
         values = jnp.where(inside, field[station], 0.0)
         high = values.astype(jnp.bfloat16)
         low = (values - high.astype(jnp.float32)).astype(jnp.bfloat16)
@@ -225,7 +238,7 @@
     if last:
         out_shape = [
             jax.ShapeDtypeStruct((plan.band, plan.rows, 2 * LANES), jnp.bfloat16),
-            jax.ShapeDtypeStruct((LANES * 3 // 4, LANES), jnp.float32),
+            jax.ShapeDtypeStruct((LANES * 5 // 8, LANES), jnp.float32),
         ]
     else:
         out_shape = field_shape
@@ -298,24 +311,23 @@
 
 
 def folded(gram):
-    half = LANES // 2
-    corner = pltpu.roll(gram[half:, :], half, 1)
-    first = lax.broadcasted_iota(jnp.int32, (half // 2, LANES), 1) < half
-    joined = jnp.where(first, corner[: half // 2], gram[half + half // 2 :, :])
-    return jnp.concatenate([gram[:half], joined], axis=0)
+    lane = lax.broadcasted_iota(jnp.int32, (32, LANES), 1)
+    second = jnp.where(lane < 32, pltpu.roll(gram[96:], 32, 1), gram[32:64])
+    third = jnp.where(lane[:16] < 64, pltpu.roll(gram[64:80], 64, 1), gram[80:96])
+    return jnp.concatenate([gram[:32], second, third], axis=0)
 
 
 def unfolded(packed):
-    half = LANES // 2
-    joined = packed[half:]
-    return jnp.concatenate([packed[:half], pltpu.roll(joined, half, 1), joined], axis=0)
+    third = packed[64:]
+    corner = pltpu.roll(packed[32:64], 96, 1)
+    return jnp.concatenate([packed[:64], pltpu.roll(third, 64, 1), third, corner], axis=0)
 
 
 def basis_kernel(plan, scale, addends, *rest):
     packed = rest[0][...]
     for other in rest[1:addends]:
         packed = packed + other[...]
-    split_ref, out_ref, left, right = rest[addends:]
+    split_ref, out_hbm, left, right, held, sems = rest[addends:]
     invert_factor(unfolded(packed), left, right)
     weight = right[...] * scale
     high = weight.astype(jnp.bfloat16)
@@ -323,22 +335,36 @@
     turned = jnp.concatenate(
         [jnp.concatenate([high, high], axis=1), jnp.concatenate([low, low], axis=1)], axis=0
     )
-    for station in range(plan.band):
-        product = lax.dot_general(
-            split_ref[station], turned, (((1,), (1,)), ((), ())), preferred_element_type=jnp.float32
-        )
-        total = product[:, :LANES] + product[:, LANES:]
-        out_ref[pl.ds(station, plan.segment, stride=plan.band), :] = total[: plan.segment]
+    copies = []
+    for start in range(0, plan.rows, CHUNK):
+        size = min(CHUNK, plan.rows - start)
+        kept = min(size, plan.segment - start)
+        for station in range(plan.band):
+            product = lax.dot_general(
+                split_ref[station, pl.ds(start, size), :],
+                turned,
+                (((1,), (1,)), ((), ())),
+                preferred_element_type=jnp.float32,
+            )
+            total = product[:, :LANES] + product[:, LANES:]
+            held[pl.ds(start * plan.band + station, kept, stride=plan.band), :] = total[:kept]
+        rows = pl.ds(start * plan.band, kept * plan.band)
+        copies.append(pltpu.make_async_copy(held.at[rows], out_hbm.at[rows], sems.at[len(copies)]))
+        copies[-1].start()
+    for copy in copies:
+        copy.wait()
 
 
 def make_basis(plan, scale, grams, split):
     vmem = pl.BlockSpec(memory_space=pltpu.VMEM)
+    shape = (plan.segment * plan.band, LANES)
     rows = pl.pallas_call(
         functools.partial(basis_kernel, plan, scale, len(grams)),
-        out_shape=jax.ShapeDtypeStruct((plan.segment * plan.band, LANES), jnp.float32),
+        out_shape=jax.ShapeDtypeStruct(shape, jnp.float32),
         in_specs=[vmem] * (len(grams) + 1),
-        out_specs=vmem,
-        scratch_shapes=[pltpu.VMEM((LANES, LANES), jnp.float32)] * 2,
+        out_specs=pl.BlockSpec(memory_space=pl.ANY),
+        scratch_shapes=[pltpu.VMEM((LANES, LANES), jnp.float32)] * 2
+        + [pltpu.VMEM(shape, jnp.float32), pltpu.SemaphoreType.DMA((-(-plan.rows // CHUNK),))],
         compiler_params=pltpu.CompilerParams(vmem_limit_bytes=24 << 20),
         name="factor_and_basis",
     )(*grams, split)
@@ -381,7 +407,9 @@
     field = add_rows(plan, band, both_cores(arrived[:1]), None, False)
     field = add_rows(plan, band, arrived[1 : 1 + near], field, False)
     rest, field = lax.optimization_barrier((arrived[1 + near :], field))
-    field = add_rows(plan, band, both_cores(rest), field, True)
+    passed = [swapped(value, "band", 1) for value in rest]
+    field = add_rows(plan, band, rest, field, False)
+    field = add_rows(plan, band, passed, field, True)
     split, gram = field
     band_bits, grp_bits = (list(range(n.bit_length() - 1)) for n in (band_size, grp_size))
     gram = sum_over(gram, "band", band_bits[:1])

time: 72.8 us -> 67 us (0.920)
  Pallas kernels: 19.3 us -> 15 us
  local copies, waits for them, and re-layouts: 0.98 us -> 0 us
    pallas_call x3 -> x4, Pallas kernels: 9.82 us -> 6.59 us  [add_rows(): pl.pallas_call(functools.partial(field_kernel, plan, first, last, count),...]
    pallas_call x1, Pallas kernels: 2.52 us -> 1.47 us  [pack(): pl.pallas_call(functools.partial(pack_kernel, plan), out_shape=plan.shape...]
    unnamed x2 -> x0, local copies, waits for them, and re-layouts: 0.98 us -> none
  transfers between devices with their start and end apart: 13 -> 13, of which waited for: 10 -> 9; matrix products, arithmetic and copies ran while one was open for 0% -> 0% of each run, Pallas kernels for 5% -> 6%
where the time goes in v4:
time: 67 us; the launch traced here: 66.8 us
  waiting for transfers between devices  31.1 us (46%)
  starting transfers between devices  20.1 us (30%)
  Pallas kernels  15 us (22%)
  between operations  0.71 us (1%)
    ppermute x13, waiting for transfers between devices, swapped(): return lax.ppermute(value, axis, pairs)  31.1 us
    ppermute x13, starting transfers between devices, swapped(): return lax.ppermute(value, axis, pairs)  20.1 us
    pallas_call x1, Pallas kernels, make_basis(): pl.pallas_call(functools.partial(basis_kernel, plan, scale, len(grams)),...  6.91 us
    pallas_call x4, Pallas kernels, add_rows(): pl.pallas_call(functools.partial(field_kernel, plan, first, last, count),...  6.59 us
    pallas_call x1, Pallas kernels, pack(): pl.pallas_call(functools.partial(pack_kernel, plan), out_shape=plan.shape...  1.47 us
  transfers between devices with their start and end apart: 13, of which 9 were waited for; matrix products, arithmetic and copies ran while one was open for 0% of the time, Pallas kernels for 6%

profile of v4, /device:TPU:0, one launch (start us, length us, event | category | flops | bytes accessed | tf_op | source)
XLA Modules:
  0.0 66.8 jit_solution(1354510512013048385)
XLA Ops:
  0.7 1.5 %pack_windows.1 = (bf16[1392,128]{1,0:T(8,128)(2,1)S(1)}, bf16[864,128]{1,0:T(8,128)(2,1)S(1)}, bf16[864,128]{1,0:T(8,128)(2,1)S(1)}, bf16[1392,128]{1,0:T(8,128)(2,1)S(1)}, bf16[1392,128]{1,0:T(8,128)(2,1)S(1)}) custom-call(s32[1]{0:T(128)} %bitcast.band_ref, s32[1]{0:T(128)S(6)} %copy.9.count_ref, s32[1,5]{1,0:T(1,128)} %station_hbm.1, ...), custom_call_target="tpu_custom_call" | custom-call | bytes 4194304 | tf_op jit(solution)/shard_map/pack_windows/pallas_call | solution.py:141
  2.1 0.5 collective-permute-start.4
  2.6 3.7 %collective-permute-start = (bf16[1392,128]{1,0:T(8,128)(2,1)S(1)}, bf16[1392,128]{1,0:T(8,128)(2,1)S(1)}, u32[]{:S(2)}, u32[]{:S(2)}) collective-permute-start(bf16[1392,128]{1,0:T(8,128)(2,1)S(1)} %get-tuple-element.15), channel_id=1, source_target_pairs={{0,4},{1,5},{2,6},{3,7},{4,0},{5,1},{6,2},{7,3},{8,12},{9,13},{10,... | collective-permute-start | bytes 1069064 | tf_op jit(solution)/shard_map/ppermute | solution.py:23
  6.3 1.3 %collective-permute-start.1 = (bf16[1392,128]{1,0:T(8,128)(2,1)S(1)}, bf16[1392,128]{1,0:T(8,128)(2,1)S(1)}, u32[]{:S(2)}, u32[]{:S(2)}) collective-permute-start(bf16[1392,128]{1,0:T(8,128)(2,1)S(1)} %get-tuple-element.16), channel_id=1, source_target_pairs={{0,6},{1,7},{2,4},{3,5},{4,2},{5,3},{6,0},{7,1},{8,14},{9,15},{10,... | collective-permute-start | bytes 1069064 | tf_op jit(solution)/shard_map/ppermute | solution.py:23
  7.9 1.0 %collective-permute-start.3 = (bf16[864,128]{1,0:T(8,128)(2,1)S(1)}, bf16[864,128]{1,0:T(8,128)(2,1)S(1)}, u32[]{:S(2)}, u32[]{:S(2)}) collective-permute-start(bf16[864,128]{1,0:T(8,128)(2,1)S(1)} %get-tuple-element.18), channel_id=1, source_target_pairs={{0,3},{1,2},{2,1},{3,0},{4,7},{5,6},{6,5},{7,4},{8,11},{9,10},{10,... | collective-permute-start | bytes 663560 | tf_op jit(solution)/shard_map/ppermute | solution.py:23
  8.9 1.4 %field.3.rest_2_ = f32[8,544,128]{2,1,0:T(8,128)S(1)} custom-call(s32[1]{0:T(128)} %bitcast.band_ref, bf16[1392,128]{1,0:T(8,128)(2,1)S(1)} %get-tuple-element.19.rest_0_, bf16[1392,128]{1,0:T(8,128)(2,1)S(1)} %collective-permute-done.4.rest_1_), custom_call_target="tpu_custom_call" | custom-call | flops 1048576 | bytes 65536 | tf_op jit(solution)/shard_map/field/pallas_call | solution.py:246
  10.3 17.1 %collective-permute-done.2.rest_0_ = bf16[864,128]{1,0:T(8,128)(2,1)S(1)} collective-permute-done((bf16[864,128]{1,0:T(8,128)(2,1)S(1)}, bf16[864,128]{1,0:T(8,128)(2,1)S(1)}, u32[]{:S(2)}, u32[]{:S(2)}) %collective-permute-start.2) | collective-permute-done | bytes 221216 | tf_op jit(solution)/shard_map/ppermute | solution.py:23
  27.4 5.2 %collective-permute-done.3.rest_1_ = bf16[864,128]{1,0:T(8,128)(2,1)S(1)} collective-permute-done((bf16[864,128]{1,0:T(8,128)(2,1)S(1)}, bf16[864,128]{1,0:T(8,128)(2,1)S(1)}, u32[]{:S(2)}, u32[]{:S(2)}) %collective-permute-start.3) | collective-permute-done | bytes 221216 | tf_op jit(solution)/shard_map/ppermute | solution.py:23
  32.6 1.3 %field.4.rest_2_ = f32[8,544,128]{2,1,0:T(8,128)S(1)} custom-call(s32[1]{0:T(128)} %bitcast.band_ref, bf16[864,128]{1,0:T(8,128)(2,1)S(1)} %collective-permute-done.2.rest_0_, bf16[864,128]{1,0:T(8,128)(2,1)S(1)} %collective-permute-done.3.rest_1_, f32[8,544,128]{2,1,0:T(8,128)S(1)} %field.3.rest_2_), custom_call_target="tpu_custom_call", output_to_operand_aliasing={{}: (3, {})} | custom-call | flops 1048576 | bytes 65536 | tf_op jit(solution)/shard_map/field/pallas_call | solution.py:246
  34.0 1.0 %collective-permute-start.5 = (bf16[1392,128]{1,0:T(8,128)(2,1)S(1)}, bf16[1392,128]{1,0:T(8,128)(2,1)S(1)}, u32[]{:S(2)}, u32[]{:S(2)}) collective-permute-start(bf16[1392,128]{1,0:T(8,128)(2,1)S(1)} %collective-permute-done.rest_0_), channel_id=1, source_target_pairs={{0,1},{1,0},{2,3},{3,2},{4,5},{5,4},{6,7},{7,6},{8,9},{9,8},{10,11... | collective-permute-start | bytes 1069064 | tf_op jit(solution)/shard_map/ppermute | solution.py:23
  35.0 1.3 %field.5.rest_2_ = f32[8,544,128]{2,1,0:T(8,128)S(1)} custom-call(s32[1]{0:T(128)} %bitcast.band_ref, bf16[1392,128]{1,0:T(8,128)(2,1)S(1)} %collective-permute-done.rest_0_, bf16[1392,128]{1,0:T(8,128)(2,1)S(1)} %collective-permute-done.1.rest_1_, f32[8,544,128]{2,1,0:T(8,128)S(1)} %field.4.rest_2_), custom_call_target="tpu_custom_call", output_to_operand_aliasing={{}: (3, {})} | custom-call | flops 1048576 | bytes 65536 | tf_op jit(solution)/shard_map/field/pallas_call | solution.py:246
  36.7 2.6 %field_and_gram.1 = (bf16[8,544,256]{2,1,0:T(8,128)(2,1)S(1)}, f32[80,128]{1,0:T(8,128)S(1)}) custom-call(s32[1]{0:T(128)} %bitcast.band_ref, bf16[1392,128]{1,0:T(8,128)(2,1)S(1)} %collective-permute-done.5.rest_0_, bf16[1392,128]{1,0:T(8,128)(2,1)S(1)} %collective-permute-done.6.rest_1_, f32[8,544,128]{2,1,0:T(8,128)S(1)} %field.5.rest_2_), custom_call_target="tpu_custom_call" | custom-call | flops 1048576 | bytes 65536 | tf_op jit(solution)/shard_map/field_and_gram/pallas_call | solution.py:246
  39.7 0.9 %collective-permute-done.7 = f32[80,128]{1,0:T(8,128)S(1)} collective-permute-done((f32[80,128]{1,0:T(8,128)S(1)}, f32[80,128]{1,0:T(8,128)S(1)}, u32[]{:S(2)}, u32[]{:S(2)}) %collective-permute-start.7) | collective-permute-done | bytes 40992 | tf_op jit(solution)/shard_map/ppermute | solution.py:23
  40.6 2.5 %collective-permute-start.10 = (f32[80,128]{1,0:T(8,128)S(1)}, f32[80,128]{1,0:T(8,128)S(1)}, u32[]{:S(2)}, u32[]{:S(2)}) collective-permute-start(f32[80,128]{1,0:T(8,128)S(1)} %add.15), channel_id=1, source_target_pairs={{0,24},{8,16},{16,8},{24,0},{1,25},{9,17},{17,9},{25,1},{2,26},{10... | collective-permute-start | bytes 122888 | tf_op jit(solution)/shard_map/ppermute | solution.py:23
  43.1 0.5 collective-permute-start.9
  43.6 0.5 collective-permute-start.8
  44.1 1.4 %collective-permute-done.10 = f32[80,128]{1,0:T(8,128)S(1)} collective-permute-done((f32[80,128]{1,0:T(8,128)S(1)}, f32[80,128]{1,0:T(8,128)S(1)}, u32[]{:S(2)}, u32[]{:S(2)}) %collective-permute-start.10) | collective-permute-done | bytes 40992 | tf_op jit(solution)/shard_map/ppermute | solution.py:23
  45.5 1.6 %collective-permute-done.9 = f32[80,128]{1,0:T(8,128)S(1)} collective-permute-done((f32[80,128]{1,0:T(8,128)S(1)}, f32[80,128]{1,0:T(8,128)S(1)}, u32[]{:S(2)}, u32[]{:S(2)}) %collective-permute-start.9) | collective-permute-done | bytes 40992 | tf_op jit(solution)/shard_map/ppermute | solution.py:23
  47.1 0.5 collective-permute-done.8
  47.6 4.4 %collective-permute-start.11 = (f32[80,128]{1,0:T(8,128)S(1)}, f32[80,128]{1,0:T(8,128)S(1)}, u32[]{:S(2)}, u32[]{:S(2)}) collective-permute-start(f32[80,128]{1,0:T(8,128)S(1)} %add_add_fusion), channel_id=1, source_target_pairs={{0,2},{1,3},{2,0},{3,1},{4,6},{5,7},{6,4},{7,5},{8,10},{9,11},{10,... | collective-permute-start | bytes 122888 | tf_op jit(solution)/shard_map/ppermute | solution.py:23
  52.0 2.0 %collective-permute-done.11 = f32[80,128]{1,0:T(8,128)S(1)} collective-permute-done((f32[80,128]{1,0:T(8,128)S(1)}, f32[80,128]{1,0:T(8,128)S(1)}, u32[]{:S(2)}, u32[]{:S(2)}) %collective-permute-start.11) | collective-permute-done | bytes 40992 | tf_op jit(solution)/shard_map/ppermute | solution.py:23
  54.0 3.9 %collective-permute-start.12 = (f32[80,128]{1,0:T(8,128)S(1)}, f32[80,128]{1,0:T(8,128)S(1)}, u32[]{:S(2)}, u32[]{:S(2)}) collective-permute-start(f32[80,128]{1,0:T(8,128)S(1)} %add.19.rest_0_), channel_id=1, source_target_pairs={{0,4},{1,5},{2,6},{3,7},{4,0},{5,1},{6,2},{7,3},{8,12},{9,13},{10,... | collective-permute-start | bytes 122888 | tf_op jit(solution)/shard_map/ppermute | solution.py:23
  57.9 2.0 %collective-permute-done.12.rest_1_ = f32[80,128]{1,0:T(8,128)S(1)} collective-permute-done((f32[80,128]{1,0:T(8,128)S(1)}, f32[80,128]{1,0:T(8,128)S(1)}, u32[]{:S(2)}, u32[]{:S(2)}) %collective-permute-start.12) | collective-permute-done | bytes 40992 | tf_op jit(solution)/shard_map/ppermute | solution.py:23
  59.9 6.9 %factor_and_basis.1 = f32[4320,128]{1,0:T(8,128)} custom-call(f32[80,128]{1,0:T(8,128)S(1)} %add.19.rest_0_, f32[80,128]{1,0:T(8,128)S(1)} %collective-permute-done.12.rest_1_, bf16[8,544,256]{2,1,0:T(8,128)(2,1)S(1)} %get-tuple-element.24.rest_2_), custom_call_target="tpu_custom_call" | custom-call | tf_op jit(solution)/shard_map/factor_and_basis/pallas_call | solution.py:361
  (11 shorter events, 1.2 us)
Async XLA Ops:
  2.1 6.8 %collective-permute-start.4 = (bf16[1392,128]{1,0:T(8,128)(2,1)S(1)}, bf16[1392,128]{1,0:T(8,128)(2,1)S(1)}, u32[]{:S(2)}, u32[]{:S(2)}) collective-permute-start(bf16[1392,128]{1,0:T(8,128)(2,1)S(1)} %get-tuple-element.19.rest_0_), channel_id=1, source_target_pairs={{0,1},{1,0},{2,3},{3,2},{4,5},{5,4},{6,7},{7,6},{8,9},{9,8},{10,11... | collective-permute-start | bytes 1069064 | tf_op jit(solution)/shard_map/ppermute | solution.py:23
  2.6 31.3 %collective-permute-start = (bf16[1392,128]{1,0:T(8,128)(2,1)S(1)}, bf16[1392,128]{1,0:T(8,128)(2,1)S(1)}, u32[]{:S(2)}, u32[]{:S(2)}) collective-permute-start(bf16[1392,128]{1,0:T(8,128)(2,1)S(1)} %get-tuple-element.15), channel_id=1, source_target_pairs={{0,4},{1,5},{2,6},{3,7},{4,0},{5,1},{6,2},{7,3},{8,12},{9,13},{10,... | collective-permute-start | bytes 1069064 | tf_op jit(solution)/shard_map/ppermute | solution.py:23
  6.3 27.6 %collective-permute-start.1 = (bf16[1392,128]{1,0:T(8,128)(2,1)S(1)}, bf16[1392,128]{1,0:T(8,128)(2,1)S(1)}, u32[]{:S(2)}, u32[]{:S(2)}) collective-permute-start(bf16[1392,128]{1,0:T(8,128)(2,1)S(1)} %get-tuple-element.16), channel_id=1, source_target_pairs={{0,6},{1,7},{2,4},{3,5},{4,2},{5,3},{6,0},{7,1},{8,14},{9,15},{10,... | collective-permute-start | bytes 1069064 | tf_op jit(solution)/shard_map/ppermute | solution.py:23
  7.7 19.8 %collective-permute-start.2 = (bf16[864,128]{1,0:T(8,128)(2,1)S(1)}, bf16[864,128]{1,0:T(8,128)(2,1)S(1)}, u32[]{:S(2)}, u32[]{:S(2)}) collective-permute-start(bf16[864,128]{1,0:T(8,128)(2,1)S(1)} %get-tuple-element.17), channel_id=1, source_target_pairs={{0,2},{1,3},{2,0},{3,1},{4,6},{5,7},{6,4},{7,5},{8,10},{9,11},{10,... | collective-permute-start | bytes 663560 | tf_op jit(solution)/shard_map/ppermute | solution.py:23
  7.9 24.7 %collective-permute-start.3 = (bf16[864,128]{1,0:T(8,128)(2,1)S(1)}, bf16[864,128]{1,0:T(8,128)(2,1)S(1)}, u32[]{:S(2)}, u32[]{:S(2)}) collective-permute-start(bf16[864,128]{1,0:T(8,128)(2,1)S(1)} %get-tuple-element.18), channel_id=1, source_target_pairs={{0,3},{1,2},{2,1},{3,0},{4,7},{5,6},{6,5},{7,4},{8,11},{9,10},{10,... | collective-permute-start | bytes 663560 | tf_op jit(solution)/shard_map/ppermute | solution.py:23
  34.0 2.4 %collective-permute-start.5 = (bf16[1392,128]{1,0:T(8,128)(2,1)S(1)}, bf16[1392,128]{1,0:T(8,128)(2,1)S(1)}, u32[]{:S(2)}, u32[]{:S(2)}) collective-permute-start(bf16[1392,128]{1,0:T(8,128)(2,1)S(1)} %collective-permute-done.rest_0_), channel_id=1, source_target_pairs={{0,1},{1,0},{2,3},{3,2},{4,5},{5,4},{6,7},{7,6},{8,9},{9,8},{10,11... | collective-permute-start | bytes 1069064 | tf_op jit(solution)/shard_map/ppermute | solution.py:23
  34.9 1.8 %collective-permute-start.6 = (bf16[1392,128]{1,0:T(8,128)(2,1)S(1)}, bf16[1392,128]{1,0:T(8,128)(2,1)S(1)}, u32[]{:S(2)}, u32[]{:S(2)}) collective-permute-start(bf16[1392,128]{1,0:T(8,128)(2,1)S(1)} %collective-permute-done.1.rest_1_), channel_id=1, source_target_pairs={{0,1},{1,0},{2,3},{3,2},{4,5},{5,4},{6,7},{7,6},{8,9},{9,8},{10,11... | collective-permute-start | bytes 1069064 | tf_op jit(solution)/shard_map/ppermute | solution.py:23
  39.3 1.3 %collective-permute-start.7 = (f32[80,128]{1,0:T(8,128)S(1)}, f32[80,128]{1,0:T(8,128)S(1)}, u32[]{:S(2)}, u32[]{:S(2)}) collective-permute-start(f32[80,128]{1,0:T(8,128)S(1)} %get-tuple-element.23), channel_id=1, source_target_pairs={{0,1},{1,0},{2,3},{3,2},{4,5},{5,4},{6,7},{7,6},{8,9},{9,8},{10,11... | collective-permute-start | bytes 122888 | tf_op jit(solution)/shard_map/ppermute | solution.py:23
  40.6 4.9 %collective-permute-start.10 = (f32[80,128]{1,0:T(8,128)S(1)}, f32[80,128]{1,0:T(8,128)S(1)}, u32[]{:S(2)}, u32[]{:S(2)}) collective-permute-start(f32[80,128]{1,0:T(8,128)S(1)} %add.15), channel_id=1, source_target_pairs={{0,24},{8,16},{16,8},{24,0},{1,25},{9,17},{17,9},{25,1},{2,26},{10... | collective-permute-start | bytes 122888 | tf_op jit(solution)/shard_map/ppermute | solution.py:23
  43.1 4.0 %collective-permute-start.9 = (f32[80,128]{1,0:T(8,128)S(1)}, f32[80,128]{1,0:T(8,128)S(1)}, u32[]{:S(2)}, u32[]{:S(2)}) collective-permute-start(f32[80,128]{1,0:T(8,128)S(1)} %add.15), channel_id=1, source_target_pairs={{0,16},{8,24},{16,0},{24,8},{1,17},{9,25},{17,1},{25,9},{2,18},{10... | collective-permute-start | bytes 122888 | tf_op jit(solution)/shard_map/ppermute | solution.py:23
  43.6 4.0 %collective-permute-start.8 = (f32[80,128]{1,0:T(8,128)S(1)}, f32[80,128]{1,0:T(8,128)S(1)}, u32[]{:S(2)}, u32[]{:S(2)}) collective-permute-start(f32[80,128]{1,0:T(8,128)S(1)} %add.15), channel_id=1, source_target_pairs={{0,8},{8,0},{16,24},{24,16},{1,9},{9,1},{17,25},{25,17},{2,10},{10... | collective-permute-start | bytes 122888 | tf_op jit(solution)/shard_map/ppermute | solution.py:23
  47.6 6.4 %collective-permute-start.11 = (f32[80,128]{1,0:T(8,128)S(1)}, f32[80,128]{1,0:T(8,128)S(1)}, u32[]{:S(2)}, u32[]{:S(2)}) collective-permute-start(f32[80,128]{1,0:T(8,128)S(1)} %add_add_fusion), channel_id=1, source_target_pairs={{0,2},{1,3},{2,0},{3,1},{4,6},{5,7},{6,4},{7,5},{8,10},{9,11},{10,... | collective-permute-start | bytes 122888 | tf_op jit(solution)/shard_map/ppermute | solution.py:23
  54.0 5.9 %collective-permute-start.12 = (f32[80,128]{1,0:T(8,128)S(1)}, f32[80,128]{1,0:T(8,128)S(1)}, u32[]{:S(2)}, u32[]{:S(2)}) collective-permute-start(f32[80,128]{1,0:T(8,128)S(1)} %add.19.rest_0_), channel_id=1, source_target_pairs={{0,4},{1,5},{2,6},{3,7},{4,0},{5,1},{6,2},{7,3},{8,12},{9,13},{10,... | collective-permute-start | bytes 122888 | tf_op jit(solution)/shard_map/ppermute | solution.py:23

commit v5 on v4

--- a/solution.py
+++ b/solution.py
@@ -347,7 +347,7 @@
                 preferred_element_type=jnp.float32,
             )
             total = product[:, :LANES] + product[:, LANES:]
-            held[pl.ds(start * plan.band + station, kept, stride=plan.band), :] = total[:kept]
+            held[pl.ds(start * plan.band + station, size, stride=plan.band), :] = total
         rows = pl.ds(start * plan.band, kept * plan.band)
         copies.append(pltpu.make_async_copy(held.at[rows], out_hbm.at[rows], sems.at[len(copies)]))
         copies[-1].start()
@@ -364,7 +364,7 @@
         in_specs=[vmem] * (len(grams) + 1),
         out_specs=pl.BlockSpec(memory_space=pl.ANY),
         scratch_shapes=[pltpu.VMEM((LANES, LANES), jnp.float32)] * 2
-        + [pltpu.VMEM(shape, jnp.float32), pltpu.SemaphoreType.DMA((-(-plan.rows // CHUNK),))],
+        + [pltpu.VMEM((plan.rows * plan.band, LANES), jnp.float32), pltpu.SemaphoreType.DMA((-(-plan.rows // CHUNK),))],
         compiler_params=pltpu.CompilerParams(vmem_limit_bytes=24 << 20),
         name="factor_and_basis",
     )(*grams, split)
@@ -406,10 +406,13 @@
     near = sum(near for _, near in plan.sends)
     field = add_rows(plan, band, both_cores(arrived[:1]), None, False)
     field = add_rows(plan, band, arrived[1 : 1 + near], field, False)
-    rest, field = lax.optimization_barrier((arrived[1 + near :], field))
-    passed = [swapped(value, "band", 1) for value in rest]
-    field = add_rows(plan, band, rest, field, False)
-    field = add_rows(plan, band, passed, field, True)
+    *head, tail = arrived[1 + near :]
+    passed = [swapped(value, "band", 1) for value in head]
+    field = add_rows(plan, band, head, field, False)
+    tail, field = lax.optimization_barrier((tail, field))
+    tail_passed = swapped(tail, "band", 1)
+    field = add_rows(plan, band, [tail, *passed], field, False)
+    field = add_rows(plan, band, [tail_passed], field, True)
     split, gram = field
     band_bits, grp_bits = (list(range(n.bit_length() - 1)) for n in (band_size, grp_size))
     gram = sum_over(gram, "band", band_bits[:1])

time: 67 us -> 65.4 us (0.976)
  starting transfers between devices: 20.1 us -> 18 us
    ppermute x13, starting transfers between devices: 20.1 us -> 18 us  [swapped(): return lax.ppermute(value, axis, pairs)]
    pallas_call x4 -> x5, Pallas kernels: 6.59 us -> 6.98 us  [add_rows(): pl.pallas_call(functools.partial(field_kernel, plan, first, last, count),...]
  transfers between devices with their start and end apart: 13 -> 13, of which waited for: 9 -> 8; matrix products, arithmetic and copies ran while one was open for 0% -> 0% of each run, Pallas kernels for 6% -> 7%
where the time goes in v5:
time: 65.4 us; the launch traced here: 65.2 us
  waiting for transfers between devices  31.1 us (48%)
  starting transfers between devices  18 us (28%)
  Pallas kernels  15.4 us (24%)
  between operations  0.7 us (1%)
    ppermute x13, waiting for transfers between devices, swapped(): return lax.ppermute(value, axis, pairs)  31.1 us
    ppermute x13, starting transfers between devices, swapped(): return lax.ppermute(value, axis, pairs)  18 us
    pallas_call x5, Pallas kernels, add_rows(): pl.pallas_call(functools.partial(field_kernel, plan, first, last, count),...  6.98 us
    pallas_call x1, Pallas kernels, make_basis(): pl.pallas_call(functools.partial(basis_kernel, plan, scale, len(grams)),...  6.91 us
    pallas_call x1, Pallas kernels, pack(): pl.pallas_call(functools.partial(pack_kernel, plan), out_shape=plan.shape...  1.47 us
  transfers between devices with their start and end apart: 13, of which 8 were waited for; matrix products, arithmetic and copies ran while one was open for 0% of the time, Pallas kernels for 7%

profile of v5, /device:TPU:0, one launch (start us, length us, event | category | flops | bytes accessed | tf_op | source)
XLA Modules:
  0.0 65.2 jit_solution(12407960756563682523)
XLA Ops:
  0.7 1.5 %pack_windows.1 = (bf16[1392,128]{1,0:T(8,128)(2,1)S(1)}, bf16[864,128]{1,0:T(8,128)(2,1)S(1)}, bf16[864,128]{1,0:T(8,128)(2,1)S(1)}, bf16[1392,128]{1,0:T(8,128)(2,1)S(1)}, bf16[1392,128]{1,0:T(8,128)(2,1)S(1)}) custom-call(s32[1]{0:T(128)} %bitcast.band_ref, s32[1]{0:T(128)S(6)} %copy.11.count_ref, s32[1,5]{1,0:T(1,128)} %station_hbm.1, ...), custom_call_target="tpu_custom_call" | custom-call | bytes 4194304 | tf_op jit(solution)/shard_map/pack_windows/pallas_call | solution.py:141
  2.1 4.1 %collective-permute-start.1 = (bf16[1392,128]{1,0:T(8,128)(2,1)S(1)}, bf16[1392,128]{1,0:T(8,128)(2,1)S(1)}, u32[]{:S(2)}, u32[]{:S(2)}) collective-permute-start(bf16[1392,128]{1,0:T(8,128)(2,1)S(1)} %get-tuple-element.15), channel_id=1, source_target_pairs={{0,4},{1,5},{2,6},{3,7},{4,0},{5,1},{6,2},{7,3},{8,12},{9,13},{10,... | collective-permute-start | bytes 1069064 | tf_op jit(solution)/shard_map/ppermute | solution.py:23
  6.3 1.3 %collective-permute-start = (bf16[1392,128]{1,0:T(8,128)(2,1)S(1)}, bf16[1392,128]{1,0:T(8,128)(2,1)S(1)}, u32[]{:S(2)}, u32[]{:S(2)}) collective-permute-start(bf16[1392,128]{1,0:T(8,128)(2,1)S(1)} %get-tuple-element.14), channel_id=1, source_target_pairs={{0,6},{1,7},{2,4},{3,5},{4,2},{5,3},{6,0},{7,1},{8,14},{9,15},{10,... | collective-permute-start | bytes 1069064 | tf_op jit(solution)/shard_map/ppermute | solution.py:23
  7.8 1.3 %collective-permute-start.3 = (bf16[864,128]{1,0:T(8,128)(2,1)S(1)}, bf16[864,128]{1,0:T(8,128)(2,1)S(1)}, u32[]{:S(2)}, u32[]{:S(2)}) collective-permute-start(bf16[864,128]{1,0:T(8,128)(2,1)S(1)} %get-tuple-element.17), channel_id=1, source_target_pairs={{0,3},{1,2},{2,1},{3,0},{4,7},{5,6},{6,5},{7,4},{8,11},{9,10},{10,... | collective-permute-start | bytes 663560 | tf_op jit(solution)/shard_map/ppermute | solution.py:23
  9.2 21.5 %collective-permute-done.1.rest_0_ = bf16[1392,128]{1,0:T(8,128)(2,1)S(1)} collective-permute-done((bf16[1392,128]{1,0:T(8,128)(2,1)S(1)}, bf16[1392,128]{1,0:T(8,128)(2,1)S(1)}, u32[]{:S(2)}, u32[]{:S(2)}) %collective-permute-start.1) | collective-permute-done | bytes 356384 | tf_op jit(solution)/shard_map/ppermute | solution.py:23
  30.7 1.4 %field.4.rest_2_ = f32[8,544,128]{2,1,0:T(8,128)S(1)} custom-call(s32[1]{0:T(128)} %bitcast.band_ref, bf16[1392,128]{1,0:T(8,128)(2,1)S(1)} %get-tuple-element.18.rest_0_, bf16[1392,128]{1,0:T(8,128)(2,1)S(1)} %collective-permute-done.4.rest_1_), custom_call_target="tpu_custom_call" | custom-call | flops 1048576 | bytes 65536 | tf_op jit(solution)/shard_map/field/pallas_call | solution.py:246
  32.2 1.2 %collective-permute-done.3.rest_1_ = bf16[864,128]{1,0:T(8,128)(2,1)S(1)} collective-permute-done((bf16[864,128]{1,0:T(8,128)(2,1)S(1)}, bf16[864,128]{1,0:T(8,128)(2,1)S(1)}, u32[]{:S(2)}, u32[]{:S(2)}) %collective-permute-start.3) | collective-permute-done | bytes 221216 | tf_op jit(solution)/shard_map/ppermute | solution.py:23
  33.3 1.3 %field.5.rest_1_ = f32[8,544,128]{2,1,0:T(8,128)S(1)} custom-call(s32[1]{0:T(128)} %bitcast.band_ref, bf16[864,128]{1,0:T(8,128)(2,1)S(1)} %collective-permute-done.2.rest_0_, bf16[864,128]{1,0:T(8,128)(2,1)S(1)} %collective-permute-done.3.rest_1_, f32[8,544,128]{2,1,0:T(8,128)S(1)} %field.4.rest_2_), custom_call_target="tpu_custom_call", output_to_operand_aliasing={{}: (3, {})} | custom-call | flops 1048576 | bytes 65536 | tf_op jit(solution)/shard_map/field/pallas_call | solution.py:246
  34.6 0.9 %field.6.rest_2_ = f32[8,544,128]{2,1,0:T(8,128)S(1)} custom-call(s32[1]{0:T(128)} %bitcast.band_ref, bf16[1392,128]{1,0:T(8,128)(2,1)S(1)} %collective-permute-done.1.rest_0_, f32[8,544,128]{2,1,0:T(8,128)S(1)} %field.5.rest_1_), custom_call_target="tpu_custom_call", output_to_operand_aliasing={{}: (2, {})} | custom-call | flops 1048576 | bytes 65536 | tf_op jit(solution)/shard_map/field/pallas_call | solution.py:246
  35.5 0.6 collective-permute-start.5
  36.1 1.3 %field.7.rest_1_ = f32[8,544,128]{2,1,0:T(8,128)S(1)} custom-call(s32[1]{0:T(128)} %bitcast.band_ref, bf16[1392,128]{1,0:T(8,128)(2,1)S(1)} %collective-permute-done.rest_0_, bf16[1392,128]{1,0:T(8,128)(2,1)S(1)} %collective-permute-done.6.rest_1_, f32[8,544,128]{2,1,0:T(8,128)S(1)} %field.6.rest_2_), custom_call_target="tpu_custom_call", output_to_operand_aliasing={{}: (3, {})} | custom-call | flops 1048576 | bytes 65536 | tf_op jit(solution)/shard_map/field/pallas_call | solution.py:246
  37.4 2.1 %field_and_gram.1 = (bf16[8,544,256]{2,1,0:T(8,128)(2,1)S(1)}, f32[80,128]{1,0:T(8,128)S(1)}) custom-call(s32[1]{0:T(128)} %bitcast.band_ref, bf16[1392,128]{1,0:T(8,128)(2,1)S(1)} %collective-permute-done.5.rest_0_, f32[8,544,128]{2,1,0:T(8,128)S(1)} %field.7.rest_1_), custom_call_target="tpu_custom_call" | custom-call | flops 1048576 | bytes 65536 | tf_op jit(solution)/shard_map/field_and_gram/pallas_call | solution.py:246
  39.9 0.9 %collective-permute-done.7 = f32[80,128]{1,0:T(8,128)S(1)} collective-permute-done((f32[80,128]{1,0:T(8,128)S(1)}, f32[80,128]{1,0:T(8,128)S(1)}, u32[]{:S(2)}, u32[]{:S(2)}) %collective-permute-start.7) | collective-permute-done | bytes 40992 | tf_op jit(solution)/shard_map/ppermute | solution.py:23
  40.8 2.5 %collective-permute-start.10 = (f32[80,128]{1,0:T(8,128)S(1)}, f32[80,128]{1,0:T(8,128)S(1)}, u32[]{:S(2)}, u32[]{:S(2)}) collective-permute-start(f32[80,128]{1,0:T(8,128)S(1)} %add.15), channel_id=1, source_target_pairs={{0,24},{8,16},{16,8},{24,0},{1,25},{9,17},{17,9},{25,1},{2,26},{10... | collective-permute-start | bytes 122888 | tf_op jit(solution)/shard_map/ppermute | solution.py:23
  43.3 0.5 collective-permute-start.8
  43.8 0.5 collective-permute-start.9
  44.3 1.4 %collective-permute-done.10 = f32[80,128]{1,0:T(8,128)S(1)} collective-permute-done((f32[80,128]{1,0:T(8,128)S(1)}, f32[80,128]{1,0:T(8,128)S(1)}, u32[]{:S(2)}, u32[]{:S(2)}) %collective-permute-start.10) | collective-permute-done | bytes 40992 | tf_op jit(solution)/shard_map/ppermute | solution.py:23
  45.7 1.6 %collective-permute-done.8 = f32[80,128]{1,0:T(8,128)S(1)} collective-permute-done((f32[80,128]{1,0:T(8,128)S(1)}, f32[80,128]{1,0:T(8,128)S(1)}, u32[]{:S(2)}, u32[]{:S(2)}) %collective-permute-start.8) | collective-permute-done | bytes 40992 | tf_op jit(solution)/shard_map/ppermute | solution.py:23
  47.3 0.5 collective-permute-done.9
  47.8 2.6 %collective-permute-start.11 = (f32[80,128]{1,0:T(8,128)S(1)}, f32[80,128]{1,0:T(8,128)S(1)}, u32[]{:S(2)}, u32[]{:S(2)}) collective-permute-start(f32[80,128]{1,0:T(8,128)S(1)} %add_add_fusion), channel_id=1, source_target_pairs={{0,2},{1,3},{2,0},{3,1},{4,6},{5,7},{6,4},{7,5},{8,10},{9,11},{10,... | collective-permute-start | bytes 122888 | tf_op jit(solution)/shard_map/ppermute | solution.py:23
  50.4 2.0 %collective-permute-done.11 = f32[80,128]{1,0:T(8,128)S(1)} collective-permute-done((f32[80,128]{1,0:T(8,128)S(1)}, f32[80,128]{1,0:T(8,128)S(1)}, u32[]{:S(2)}, u32[]{:S(2)}) %collective-permute-start.11) | collective-permute-done | bytes 40992 | tf_op jit(solution)/shard_map/ppermute | solution.py:23
  52.4 3.9 %collective-permute-start.12 = (f32[80,128]{1,0:T(8,128)S(1)}, f32[80,128]{1,0:T(8,128)S(1)}, u32[]{:S(2)}, u32[]{:S(2)}) collective-permute-start(f32[80,128]{1,0:T(8,128)S(1)} %add.19.rest_0_), channel_id=1, source_target_pairs={{0,4},{1,5},{2,6},{3,7},{4,0},{5,1},{6,2},{7,3},{8,12},{9,13},{10,... | collective-permute-start | bytes 122888 | tf_op jit(solution)/shard_map/ppermute | solution.py:23
  56.3 2.0 %collective-permute-done.12.rest_1_ = f32[80,128]{1,0:T(8,128)S(1)} collective-permute-done((f32[80,128]{1,0:T(8,128)S(1)}, f32[80,128]{1,0:T(8,128)S(1)}, u32[]{:S(2)}, u32[]{:S(2)}) %collective-permute-start.12) | collective-permute-done | bytes 40992 | tf_op jit(solution)/shard_map/ppermute | solution.py:23
  58.3 6.9 %factor_and_basis.1 = f32[4320,128]{1,0:T(8,128)} custom-call(f32[80,128]{1,0:T(8,128)S(1)} %add.19.rest_0_, f32[80,128]{1,0:T(8,128)S(1)} %collective-permute-done.12.rest_1_, bf16[8,544,256]{2,1,0:T(8,128)(2,1)S(1)} %get-tuple-element.22.rest_2_), custom_call_target="tpu_custom_call" | custom-call | tf_op jit(solution)/shard_map/factor_and_basis/pallas_call | solution.py:361
  (12 shorter events, 0.7 us)
Async XLA Ops:
  2.1 28.6 %collective-permute-start.1 = (bf16[1392,128]{1,0:T(8,128)(2,1)S(1)}, bf16[1392,128]{1,0:T(8,128)(2,1)S(1)}, u32[]{:S(2)}, u32[]{:S(2)}) collective-permute-start(bf16[1392,128]{1,0:T(8,128)(2,1)S(1)} %get-tuple-element.15), channel_id=1, source_target_pairs={{0,4},{1,5},{2,6},{3,7},{4,0},{5,1},{6,2},{7,3},{8,12},{9,13},{10,... | collective-permute-start | bytes 1069064 | tf_op jit(solution)/shard_map/ppermute | solution.py:23
  6.3 24.5 %collective-permute-start.4 = (bf16[1392,128]{1,0:T(8,128)(2,1)S(1)}, bf16[1392,128]{1,0:T(8,128)(2,1)S(1)}, u32[]{:S(2)}, u32[]{:S(2)}) collective-permute-start(bf16[1392,128]{1,0:T(8,128)(2,1)S(1)} %get-tuple-element.18.rest_0_), channel_id=1, source_target_pairs={{0,1},{1,0},{2,3},{3,2},{4,5},{5,4},{6,7},{7,6},{8,9},{9,8},{10,11... | collective-permute-start | bytes 1069064 | tf_op jit(solution)/shard_map/ppermute | solution.py:23
  6.3 29.2 %collective-permute-start = (bf16[1392,128]{1,0:T(8,128)(2,1)S(1)}, bf16[1392,128]{1,0:T(8,128)(2,1)S(1)}, u32[]{:S(2)}, u32[]{:S(2)}) collective-permute-start(bf16[1392,128]{1,0:T(8,128)(2,1)S(1)} %get-tuple-element.14), channel_id=1, source_target_pairs={{0,6},{1,7},{2,4},{3,5},{4,2},{5,3},{6,0},{7,1},{8,14},{9,15},{10,... | collective-permute-start | bytes 1069064 | tf_op jit(solution)/shard_map/ppermute | solution.py:23
  7.6 24.5 %collective-permute-start.2 = (bf16[864,128]{1,0:T(8,128)(2,1)S(1)}, bf16[864,128]{1,0:T(8,128)(2,1)S(1)}, u32[]{:S(2)}, u32[]{:S(2)}) collective-permute-start(bf16[864,128]{1,0:T(8,128)(2,1)S(1)} %get-tuple-element.16), channel_id=1, source_target_pairs={{0,2},{1,3},{2,0},{3,1},{4,6},{5,7},{6,4},{7,5},{8,10},{9,11},{10,... | collective-permute-start | bytes 663560 | tf_op jit(solution)/shard_map/ppermute | solution.py:23
  7.8 25.5 %collective-permute-start.3 = (bf16[864,128]{1,0:T(8,128)(2,1)S(1)}, bf16[864,128]{1,0:T(8,128)(2,1)S(1)}, u32[]{:S(2)}, u32[]{:S(2)}) collective-permute-start(bf16[864,128]{1,0:T(8,128)(2,1)S(1)} %get-tuple-element.17), channel_id=1, source_target_pairs={{0,3},{1,2},{2,1},{3,0},{4,7},{5,6},{6,5},{7,4},{8,11},{9,10},{10,... | collective-permute-start | bytes 663560 | tf_op jit(solution)/shard_map/ppermute | solution.py:23
  30.7 5.3 %collective-permute-start.6 = (bf16[1392,128]{1,0:T(8,128)(2,1)S(1)}, bf16[1392,128]{1,0:T(8,128)(2,1)S(1)}, u32[]{:S(2)}, u32[]{:S(2)}) collective-permute-start(bf16[1392,128]{1,0:T(8,128)(2,1)S(1)} %collective-permute-done.1.rest_0_), channel_id=1, source_target_pairs={{0,1},{1,0},{2,3},{3,2},{4,5},{5,4},{6,7},{7,6},{8,9},{9,8},{10,11... | collective-permute-start | bytes 1069064 | tf_op jit(solution)/shard_map/ppermute | solution.py:23
  35.5 1.9 %collective-permute-start.5 = (bf16[1392,128]{1,0:T(8,128)(2,1)S(1)}, bf16[1392,128]{1,0:T(8,128)(2,1)S(1)}, u32[]{:S(2)}, u32[]{:S(2)}) collective-permute-start(bf16[1392,128]{1,0:T(8,128)(2,1)S(1)} %collective-permute-done.rest_0_), channel_id=1, source_target_pairs={{0,1},{1,0},{2,3},{3,2},{4,5},{5,4},{6,7},{7,6},{8,9},{9,8},{10,11... | collective-permute-start | bytes 1069064 | tf_op jit(solution)/shard_map/ppermute | solution.py:23
  39.5 1.3 %collective-permute-start.7 = (f32[80,128]{1,0:T(8,128)S(1)}, f32[80,128]{1,0:T(8,128)S(1)}, u32[]{:S(2)}, u32[]{:S(2)}) collective-permute-start(f32[80,128]{1,0:T(8,128)S(1)} %get-tuple-element.21), channel_id=1, source_target_pairs={{0,1},{1,0},{2,3},{3,2},{4,5},{5,4},{6,7},{7,6},{8,9},{9,8},{10,11... | collective-permute-start | bytes 122888 | tf_op jit(solution)/shard_map/ppermute | solution.py:23
  40.8 4.9 %collective-permute-start.10 = (f32[80,128]{1,0:T(8,128)S(1)}, f32[80,128]{1,0:T(8,128)S(1)}, u32[]{:S(2)}, u32[]{:S(2)}) collective-permute-start(f32[80,128]{1,0:T(8,128)S(1)} %add.15), channel_id=1, source_target_pairs={{0,24},{8,16},{16,8},{24,0},{1,25},{9,17},{17,9},{25,1},{2,26},{10... | collective-permute-start | bytes 122888 | tf_op jit(solution)/shard_map/ppermute | solution.py:23
  43.3 4.0 %collective-permute-start.8 = (f32[80,128]{1,0:T(8,128)S(1)}, f32[80,128]{1,0:T(8,128)S(1)}, u32[]{:S(2)}, u32[]{:S(2)}) collective-permute-start(f32[80,128]{1,0:T(8,128)S(1)} %add.15), channel_id=1, source_target_pairs={{0,8},{8,0},{16,24},{24,16},{1,9},{9,1},{17,25},{25,17},{2,10},{10... | collective-permute-start | bytes 122888 | tf_op jit(solution)/shard_map/ppermute | solution.py:23
  43.8 4.0 %collective-permute-start.9 = (f32[80,128]{1,0:T(8,128)S(1)}, f32[80,128]{1,0:T(8,128)S(1)}, u32[]{:S(2)}, u32[]{:S(2)}) collective-permute-start(f32[80,128]{1,0:T(8,128)S(1)} %add.15), channel_id=1, source_target_pairs={{0,16},{8,24},{16,0},{24,8},{1,17},{9,25},{17,1},{25,9},{2,18},{10... | collective-permute-start | bytes 122888 | tf_op jit(solution)/shard_map/ppermute | solution.py:23
  47.8 4.6 %collective-permute-start.11 = (f32[80,128]{1,0:T(8,128)S(1)}, f32[80,128]{1,0:T(8,128)S(1)}, u32[]{:S(2)}, u32[]{:S(2)}) collective-permute-start(f32[80,128]{1,0:T(8,128)S(1)} %add_add_fusion), channel_id=1, source_target_pairs={{0,2},{1,3},{2,0},{3,1},{4,6},{5,7},{6,4},{7,5},{8,10},{9,11},{10,... | collective-permute-start | bytes 122888 | tf_op jit(solution)/shard_map/ppermute | solution.py:23
  52.4 5.9 %collective-permute-start.12 = (f32[80,128]{1,0:T(8,128)S(1)}, f32[80,128]{1,0:T(8,128)S(1)}, u32[]{:S(2)}, u32[]{:S(2)}) collective-permute-start(f32[80,128]{1,0:T(8,128)S(1)} %add.19.rest_0_), channel_id=1, source_target_pairs={{0,4},{1,5},{2,6},{3,7},{4,0},{5,1},{6,2},{7,3},{8,12},{9,13},{10,... | collective-permute-start | bytes 122888 | tf_op jit(solution)/shard_map/ppermute | solution.py:23

commit v6 on v5

--- a/solution.py
+++ b/solution.py
@@ -11,7 +11,7 @@
 TILE = 16
 BLOCK = 32
 PANEL = 16
-CHUNK = 192
+CHUNK = 272
 
 
 def up(value, step):
@@ -377,7 +377,7 @@
 
 def sum_over(value, axis, bits):
     while bits:
-        if axis == "grp" and len(bits) > 1:
+        if len(bits) > 1:
             value = sum_four(value, axis, bits[0])
             bits = bits[2:]
         else:
@@ -417,8 +417,8 @@
     band_bits, grp_bits = (list(range(n.bit_length() - 1)) for n in (band_size, grp_size))
     gram = sum_over(gram, "band", band_bits[:1])
     gram = sum_over(gram, "grp", grp_bits)
-    gram = sum_over(gram, "band", band_bits[1:-1])
-    grams = [gram, swapped(gram, "band", 1 << band_bits[-1])]
+    gram = sum_over(gram, "band", band_bits[1:-2])
+    grams = [gram] + [swapped(gram, "band", k << band_bits[-2]) for k in (1, 2, 3)]
     scale = float(grp_size * band_size * length) ** 0.5
     return make_basis(plan, scale, grams, split)
 

time: 65.4 us -> 65.1 us (level)
    ppermute x13 -> x14, starting transfers between devices: 18 us -> 17.5 us  [swapped(): return lax.ppermute(value, axis, pairs)]
    ppermute x13 -> x14, waiting for transfers between devices: 31.1 us -> 31.6 us  [swapped(): return lax.ppermute(value, axis, pairs)]
  transfers between devices with their start and end apart: 13 -> 14, of which waited for: 8 -> 8; matrix products, arithmetic and copies ran while one was open for 0% -> 0% of each run, Pallas kernels for 7% -> 7%
where the time goes in v6:
time: 65.1 us; the launch traced here: 64.9 us
  waiting for transfers between devices  31.6 us (49%)
  starting transfers between devices  17.5 us (27%)
  Pallas kernels  15.2 us (23%)
  between operations  0.7 us (1%)
    ppermute x14, waiting for transfers between devices, swapped(): return lax.ppermute(value, axis, pairs)  31.6 us
    ppermute x14, starting transfers between devices, swapped(): return lax.ppermute(value, axis, pairs)  17.5 us
    pallas_call x5, Pallas kernels, add_rows(): pl.pallas_call(functools.partial(field_kernel, plan, first, last, count),...  6.98 us
    pallas_call x1, Pallas kernels, make_basis(): pl.pallas_call(functools.partial(basis_kernel, plan, scale, len(grams)),...  6.73 us
    pallas_call x1, Pallas kernels, pack(): pl.pallas_call(functools.partial(pack_kernel, plan), out_shape=plan.shape...  1.47 us
  transfers between devices with their start and end apart: 14, of which 8 were waited for; matrix products, arithmetic and copies ran while one was open for 0% of the time, Pallas kernels for 7%

profile of v6, /device:TPU:0, one launch (start us, length us, event | category | flops | bytes accessed | tf_op | source)
XLA Modules:
  0.0 64.9 jit_solution(16157260406521781063)
XLA Ops:
  0.7 1.5 %pack_windows.1 = (bf16[1392,128]{1,0:T(8,128)(2,1)S(1)}, bf16[864,128]{1,0:T(8,128)(2,1)S(1)}, bf16[864,128]{1,0:T(8,128)(2,1)S(1)}, bf16[1392,128]{1,0:T(8,128)(2,1)S(1)}, bf16[1392,128]{1,0:T(8,128)(2,1)S(1)}) custom-call(s32[1]{0:T(128)} %bitcast.band_ref, s32[1]{0:T(128)S(6)} %copy.11.count_ref, s32[1,5]{1,0:T(1,128)} %station_hbm.1, ...), custom_call_target="tpu_custom_call" | custom-call | bytes 4194304 | tf_op jit(solution)/shard_map/pack_windows/pallas_call | solution.py:141
  2.1 4.1 %collective-permute-start.1 = (bf16[1392,128]{1,0:T(8,128)(2,1)S(1)}, bf16[1392,128]{1,0:T(8,128)(2,1)S(1)}, u32[]{:S(2)}, u32[]{:S(2)}) collective-permute-start(bf16[1392,128]{1,0:T(8,128)(2,1)S(1)} %get-tuple-element.15), channel_id=1, source_target_pairs={{0,4},{1,5},{2,6},{3,7},{4,0},{5,1},{6,2},{7,3},{8,12},{9,13},{10,... | collective-permute-start | bytes 1069064 | tf_op jit(solution)/shard_map/ppermute | solution.py:23
  6.3 1.3 %collective-permute-start = (bf16[1392,128]{1,0:T(8,128)(2,1)S(1)}, bf16[1392,128]{1,0:T(8,128)(2,1)S(1)}, u32[]{:S(2)}, u32[]{:S(2)}) collective-permute-start(bf16[1392,128]{1,0:T(8,128)(2,1)S(1)} %get-tuple-element.14), channel_id=1, source_target_pairs={{0,6},{1,7},{2,4},{3,5},{4,2},{5,3},{6,0},{7,1},{8,14},{9,15},{10,... | collective-permute-start | bytes 1069064 | tf_op jit(solution)/shard_map/ppermute | solution.py:23
  7.8 1.3 %collective-permute-start.3 = (bf16[864,128]{1,0:T(8,128)(2,1)S(1)}, bf16[864,128]{1,0:T(8,128)(2,1)S(1)}, u32[]{:S(2)}, u32[]{:S(2)}) collective-permute-start(bf16[864,128]{1,0:T(8,128)(2,1)S(1)} %get-tuple-element.17), channel_id=1, source_target_pairs={{0,3},{1,2},{2,1},{3,0},{4,7},{5,6},{6,5},{7,4},{8,11},{9,10},{10,... | collective-permute-start | bytes 663560 | tf_op jit(solution)/shard_map/ppermute | solution.py:23
  9.2 21.5 %collective-permute-done.1.rest_0_ = bf16[1392,128]{1,0:T(8,128)(2,1)S(1)} collective-permute-done((bf16[1392,128]{1,0:T(8,128)(2,1)S(1)}, bf16[1392,128]{1,0:T(8,128)(2,1)S(1)}, u32[]{:S(2)}, u32[]{:S(2)}) %collective-permute-start.1) | collective-permute-done | bytes 356384 | tf_op jit(solution)/shard_map/ppermute | solution.py:23
  30.7 1.4 %field.4.rest_2_ = f32[8,544,128]{2,1,0:T(8,128)S(1)} custom-call(s32[1]{0:T(128)} %bitcast.band_ref, bf16[1392,128]{1,0:T(8,128)(2,1)S(1)} %get-tuple-element.18.rest_0_, bf16[1392,128]{1,0:T(8,128)(2,1)S(1)} %collective-permute-done.4.rest_1_), custom_call_target="tpu_custom_call" | custom-call | flops 1048576 | bytes 65536 | tf_op jit(solution)/shard_map/field/pallas_call | solution.py:246
  32.2 1.2 %collective-permute-done.3.rest_1_ = bf16[864,128]{1,0:T(8,128)(2,1)S(1)} collective-permute-done((bf16[864,128]{1,0:T(8,128)(2,1)S(1)}, bf16[864,128]{1,0:T(8,128)(2,1)S(1)}, u32[]{:S(2)}, u32[]{:S(2)}) %collective-permute-start.3) | collective-permute-done | bytes 221216 | tf_op jit(solution)/shard_map/ppermute | solution.py:23
  33.3 1.3 %field.5.rest_1_ = f32[8,544,128]{2,1,0:T(8,128)S(1)} custom-call(s32[1]{0:T(128)} %bitcast.band_ref, bf16[864,128]{1,0:T(8,128)(2,1)S(1)} %collective-permute-done.2.rest_0_, bf16[864,128]{1,0:T(8,128)(2,1)S(1)} %collective-permute-done.3.rest_1_, f32[8,544,128]{2,1,0:T(8,128)S(1)} %field.4.rest_2_), custom_call_target="tpu_custom_call", output_to_operand_aliasing={{}: (3, {})} | custom-call | flops 1048576 | bytes 65536 | tf_op jit(solution)/shard_map/field/pallas_call | solution.py:246
  34.6 0.9 %field.6.rest_2_ = f32[8,544,128]{2,1,0:T(8,128)S(1)} custom-call(s32[1]{0:T(128)} %bitcast.band_ref, bf16[1392,128]{1,0:T(8,128)(2,1)S(1)} %collective-permute-done.1.rest_0_, f32[8,544,128]{2,1,0:T(8,128)S(1)} %field.5.rest_1_), custom_call_target="tpu_custom_call", output_to_operand_aliasing={{}: (2, {})} | custom-call | flops 1048576 | bytes 65536 | tf_op jit(solution)/shard_map/field/pallas_call | solution.py:246
  35.5 0.6 collective-permute-start.5
  36.1 1.3 %field.7.rest_1_ = f32[8,544,128]{2,1,0:T(8,128)S(1)} custom-call(s32[1]{0:T(128)} %bitcast.band_ref, bf16[1392,128]{1,0:T(8,128)(2,1)S(1)} %collective-permute-done.rest_0_, bf16[1392,128]{1,0:T(8,128)(2,1)S(1)} %collective-permute-done.6.rest_1_, f32[8,544,128]{2,1,0:T(8,128)S(1)} %field.6.rest_2_), custom_call_target="tpu_custom_call", output_to_operand_aliasing={{}: (3, {})} | custom-call | flops 1048576 | bytes 65536 | tf_op jit(solution)/shard_map/field/pallas_call | solution.py:246
  37.4 2.1 %field_and_gram.1 = (bf16[8,544,256]{2,1,0:T(8,128)(2,1)S(1)}, f32[80,128]{1,0:T(8,128)S(1)}) custom-call(s32[1]{0:T(128)} %bitcast.band_ref, bf16[1392,128]{1,0:T(8,128)(2,1)S(1)} %collective-permute-done.5.rest_0_, f32[8,544,128]{2,1,0:T(8,128)S(1)} %field.7.rest_1_), custom_call_target="tpu_custom_call" | custom-call | flops 1048576 | bytes 65536 | tf_op jit(solution)/shard_map/field_and_gram/pallas_call | solution.py:246
  39.9 0.9 %collective-permute-done.7 = f32[80,128]{1,0:T(8,128)S(1)} collective-permute-done((f32[80,128]{1,0:T(8,128)S(1)}, f32[80,128]{1,0:T(8,128)S(1)}, u32[]{:S(2)}, u32[]{:S(2)}) %collective-permute-start.7) | collective-permute-done | bytes 40992 | tf_op jit(solution)/shard_map/ppermute | solution.py:23
  40.8 2.5 %collective-permute-start.10 = (f32[80,128]{1,0:T(8,128)S(1)}, f32[80,128]{1,0:T(8,128)S(1)}, u32[]{:S(2)}, u32[]{:S(2)}) collective-permute-start(f32[80,128]{1,0:T(8,128)S(1)} %add.12), channel_id=1, source_target_pairs={{0,24},{8,16},{16,8},{24,0},{1,25},{9,17},{17,9},{25,1},{2,26},{10... | collective-permute-start | bytes 122888 | tf_op jit(solution)/shard_map/ppermute | solution.py:23
  43.3 0.5 collective-permute-start.8
  44.3 1.4 %collective-permute-done.10 = f32[80,128]{1,0:T(8,128)S(1)} collective-permute-done((f32[80,128]{1,0:T(8,128)S(1)}, f32[80,128]{1,0:T(8,128)S(1)}, u32[]{:S(2)}, u32[]{:S(2)}) %collective-permute-start.10) | collective-permute-done | bytes 40992 | tf_op jit(solution)/shard_map/ppermute | solution.py:23
  45.7 1.6 %collective-permute-done.8 = f32[80,128]{1,0:T(8,128)S(1)} collective-permute-done((f32[80,128]{1,0:T(8,128)S(1)}, f32[80,128]{1,0:T(8,128)S(1)}, u32[]{:S(2)}, u32[]{:S(2)}) %collective-permute-start.8) | collective-permute-done | bytes 40992 | tf_op jit(solution)/shard_map/ppermute | solution.py:23
  47.3 0.5 collective-permute-done.9
  47.8 2.6 %collective-permute-start.11 = (f32[80,128]{1,0:T(8,128)S(1)}, f32[80,128]{1,0:T(8,128)S(1)}, u32[]{:S(2)}, u32[]{:S(2)}) collective-permute-start(f32[80,128]{1,0:T(8,128)S(1)} %add_add_fusion.rest_0_), channel_id=1, source_target_pairs={{0,2},{1,3},{2,0},{3,1},{4,6},{5,7},{6,4},{7,5},{8,10},{9,11},{10,... | collective-permute-start | bytes 122888 | tf_op jit(solution)/shard_map/ppermute | solution.py:23
  50.4 2.0 %collective-permute-start.12 = (f32[80,128]{1,0:T(8,128)S(1)}, f32[80,128]{1,0:T(8,128)S(1)}, u32[]{:S(2)}, u32[]{:S(2)}) collective-permute-start(f32[80,128]{1,0:T(8,128)S(1)} %add_add_fusion.rest_0_), channel_id=1, source_target_pairs={{0,4},{1,5},{2,6},{3,7},{4,0},{5,1},{6,2},{7,3},{8,12},{9,13},{10,... | collective-permute-start | bytes 122888 | tf_op jit(solution)/shard_map/ppermute | solution.py:23
  52.4 1.4 %collective-permute-start.13 = (f32[80,128]{1,0:T(8,128)S(1)}, f32[80,128]{1,0:T(8,128)S(1)}, u32[]{:S(2)}, u32[]{:S(2)}) collective-permute-start(f32[80,128]{1,0:T(8,128)S(1)} %add_add_fusion.rest_0_), channel_id=1, source_target_pairs={{0,6},{1,7},{2,4},{3,5},{4,2},{5,3},{6,0},{7,1},{8,14},{9,15},{10,... | collective-permute-start | bytes 122888 | tf_op jit(solution)/shard_map/ppermute | solution.py:23
  53.8 2.0 %collective-permute-done.12.rest_2_ = f32[80,128]{1,0:T(8,128)S(1)} collective-permute-done((f32[80,128]{1,0:T(8,128)S(1)}, f32[80,128]{1,0:T(8,128)S(1)}, u32[]{:S(2)}, u32[]{:S(2)}) %collective-permute-start.12) | collective-permute-done | bytes 40992 | tf_op jit(solution)/shard_map/ppermute | solution.py:23
  55.7 2.5 %collective-permute-done.13.rest_3_ = f32[80,128]{1,0:T(8,128)S(1)} collective-permute-done((f32[80,128]{1,0:T(8,128)S(1)}, f32[80,128]{1,0:T(8,128)S(1)}, u32[]{:S(2)}, u32[]{:S(2)}) %collective-permute-start.13) | collective-permute-done | bytes 40992 | tf_op jit(solution)/shard_map/ppermute | solution.py:23
  58.2 6.7 %factor_and_basis.1 = f32[4320,128]{1,0:T(8,128)} custom-call(f32[80,128]{1,0:T(8,128)S(1)} %add_add_fusion.rest_0_, f32[80,128]{1,0:T(8,128)S(1)} %collective-permute-done.11.rest_1_, f32[80,128]{1,0:T(8,128)S(1)} %collective-permute-done.12.rest_2_, f32[80,128]{1,0:T(8,128)S(1)} %collective-permute-done.13.rest_3_, ...), custom_call_target="tpu_custom_call" | custom-call | tf_op jit(solution)/shard_map/factor_and_basis/pallas_call | solution.py:361
  (13 shorter events, 1.1 us)
Async XLA Ops:
  2.1 28.6 %collective-permute-start.1 = (bf16[1392,128]{1,0:T(8,128)(2,1)S(1)}, bf16[1392,128]{1,0:T(8,128)(2,1)S(1)}, u32[]{:S(2)}, u32[]{:S(2)}) collective-permute-start(bf16[1392,128]{1,0:T(8,128)(2,1)S(1)} %get-tuple-element.15), channel_id=1, source_target_pairs={{0,4},{1,5},{2,6},{3,7},{4,0},{5,1},{6,2},{7,3},{8,12},{9,13},{10,... | collective-permute-start | bytes 1069064 | tf_op jit(solution)/shard_map/ppermute | solution.py:23
  6.3 24.5 %collective-permute-start.4 = (bf16[1392,128]{1,0:T(8,128)(2,1)S(1)}, bf16[1392,128]{1,0:T(8,128)(2,1)S(1)}, u32[]{:S(2)}, u32[]{:S(2)}) collective-permute-start(bf16[1392,128]{1,0:T(8,128)(2,1)S(1)} %get-tuple-element.18.rest_0_), channel_id=1, source_target_pairs={{0,1},{1,0},{2,3},{3,2},{4,5},{5,4},{6,7},{7,6},{8,9},{9,8},{10,11... | collective-permute-start | bytes 1069064 | tf_op jit(solution)/shard_map/ppermute | solution.py:23
  6.3 29.2 %collective-permute-start = (bf16[1392,128]{1,0:T(8,128)(2,1)S(1)}, bf16[1392,128]{1,0:T(8,128)(2,1)S(1)}, u32[]{:S(2)}, u32[]{:S(2)}) collective-permute-start(bf16[1392,128]{1,0:T(8,128)(2,1)S(1)} %get-tuple-element.14), channel_id=1, source_target_pairs={{0,6},{1,7},{2,4},{3,5},{4,2},{5,3},{6,0},{7,1},{8,14},{9,15},{10,... | collective-permute-start | bytes 1069064 | tf_op jit(solution)/shard_map/ppermute | solution.py:23
  7.6 24.5 %collective-permute-start.2 = (bf16[864,128]{1,0:T(8,128)(2,1)S(1)}, bf16[864,128]{1,0:T(8,128)(2,1)S(1)}, u32[]{:S(2)}, u32[]{:S(2)}) collective-permute-start(bf16[864,128]{1,0:T(8,128)(2,1)S(1)} %get-tuple-element.16), channel_id=1, source_target_pairs={{0,2},{1,3},{2,0},{3,1},{4,6},{5,7},{6,4},{7,5},{8,10},{9,11},{10,... | collective-permute-start | bytes 663560 | tf_op jit(solution)/shard_map/ppermute | solution.py:23
  7.8 25.5 %collective-permute-start.3 = (bf16[864,128]{1,0:T(8,128)(2,1)S(1)}, bf16[864,128]{1,0:T(8,128)(2,1)S(1)}, u32[]{:S(2)}, u32[]{:S(2)}) collective-permute-start(bf16[864,128]{1,0:T(8,128)(2,1)S(1)} %get-tuple-element.17), channel_id=1, source_target_pairs={{0,3},{1,2},{2,1},{3,0},{4,7},{5,6},{6,5},{7,4},{8,11},{9,10},{10,... | collective-permute-start | bytes 663560 | tf_op jit(solution)/shard_map/ppermute | solution.py:23
  30.7 5.3 %collective-permute-start.6 = (bf16[1392,128]{1,0:T(8,128)(2,1)S(1)}, bf16[1392,128]{1,0:T(8,128)(2,1)S(1)}, u32[]{:S(2)}, u32[]{:S(2)}) collective-permute-start(bf16[1392,128]{1,0:T(8,128)(2,1)S(1)} %collective-permute-done.1.rest_0_), channel_id=1, source_target_pairs={{0,1},{1,0},{2,3},{3,2},{4,5},{5,4},{6,7},{7,6},{8,9},{9,8},{10,11... | collective-permute-start | bytes 1069064 | tf_op jit(solution)/shard_map/ppermute | solution.py:23
  35.5 1.9 %collective-permute-start.5 = (bf16[1392,128]{1,0:T(8,128)(2,1)S(1)}, bf16[1392,128]{1,0:T(8,128)(2,1)S(1)}, u32[]{:S(2)}, u32[]{:S(2)}) collective-permute-start(bf16[1392,128]{1,0:T(8,128)(2,1)S(1)} %collective-permute-done.rest_0_), channel_id=1, source_target_pairs={{0,1},{1,0},{2,3},{3,2},{4,5},{5,4},{6,7},{7,6},{8,9},{9,8},{10,11... | collective-permute-start | bytes 1069064 | tf_op jit(solution)/shard_map/ppermute | solution.py:23
  39.5 1.3 %collective-permute-start.7 = (f32[80,128]{1,0:T(8,128)S(1)}, f32[80,128]{1,0:T(8,128)S(1)}, u32[]{:S(2)}, u32[]{:S(2)}) collective-permute-start(f32[80,128]{1,0:T(8,128)S(1)} %get-tuple-element.21), channel_id=1, source_target_pairs={{0,1},{1,0},{2,3},{3,2},{4,5},{5,4},{6,7},{7,6},{8,9},{9,8},{10,11... | collective-permute-start | bytes 122888 | tf_op jit(solution)/shard_map/ppermute | solution.py:23
  40.8 4.9 %collective-permute-start.10 = (f32[80,128]{1,0:T(8,128)S(1)}, f32[80,128]{1,0:T(8,128)S(1)}, u32[]{:S(2)}, u32[]{:S(2)}) collective-permute-start(f32[80,128]{1,0:T(8,128)S(1)} %add.12), channel_id=1, source_target_pairs={{0,24},{8,16},{16,8},{24,0},{1,25},{9,17},{17,9},{25,1},{2,26},{10... | collective-permute-start | bytes 122888 | tf_op jit(solution)/shard_map/ppermute | solution.py:23
  43.3 4.0 %collective-permute-start.8 = (f32[80,128]{1,0:T(8,128)S(1)}, f32[80,128]{1,0:T(8,128)S(1)}, u32[]{:S(2)}, u32[]{:S(2)}) collective-permute-start(f32[80,128]{1,0:T(8,128)S(1)} %add.12), channel_id=1, source_target_pairs={{0,8},{8,0},{16,24},{24,16},{1,9},{9,1},{17,25},{25,17},{2,10},{10... | collective-permute-start | bytes 122888 | tf_op jit(solution)/shard_map/ppermute | solution.py:23
  43.8 4.0 %collective-permute-start.9 = (f32[80,128]{1,0:T(8,128)S(1)}, f32[80,128]{1,0:T(8,128)S(1)}, u32[]{:S(2)}, u32[]{:S(2)}) collective-permute-start(f32[80,128]{1,0:T(8,128)S(1)} %add.12), channel_id=1, source_target_pairs={{0,16},{8,24},{16,0},{24,8},{1,17},{9,25},{17,1},{25,9},{2,18},{10... | collective-permute-start | bytes 122888 | tf_op jit(solution)/shard_map/ppermute | solution.py:23
  47.8 6.0 %collective-permute-start.11 = (f32[80,128]{1,0:T(8,128)S(1)}, f32[80,128]{1,0:T(8,128)S(1)}, u32[]{:S(2)}, u32[]{:S(2)}) collective-permute-start(f32[80,128]{1,0:T(8,128)S(1)} %add_add_fusion.rest_0_), channel_id=1, source_target_pairs={{0,2},{1,3},{2,0},{3,1},{4,6},{5,7},{6,4},{7,5},{8,10},{9,11},{10,... | collective-permute-start | bytes 122888 | tf_op jit(solution)/shard_map/ppermute | solution.py:23
  50.4 5.3 %collective-permute-start.12 = (f32[80,128]{1,0:T(8,128)S(1)}, f32[80,128]{1,0:T(8,128)S(1)}, u32[]{:S(2)}, u32[]{:S(2)}) collective-permute-start(f32[80,128]{1,0:T(8,128)S(1)} %add_add_fusion.rest_0_), channel_id=1, source_target_pairs={{0,4},{1,5},{2,6},{3,7},{4,0},{5,1},{6,2},{7,3},{8,12},{9,13},{10,... | collective-permute-start | bytes 122888 | tf_op jit(solution)/shard_map/ppermute | solution.py:23
  52.4 5.8 %collective-permute-start.13 = (f32[80,128]{1,0:T(8,128)S(1)}, f32[80,128]{1,0:T(8,128)S(1)}, u32[]{:S(2)}, u32[]{:S(2)}) collective-permute-start(f32[80,128]{1,0:T(8,128)S(1)} %add_add_fusion.rest_0_), channel_id=1, source_target_pairs={{0,6},{1,7},{2,4},{3,5},{4,2},{5,3},{6,0},{7,1},{8,14},{9,15},{10,... | collective-permute-start | bytes 122888 | tf_op jit(solution)/shard_map/ppermute | solution.py:23

commit v7 on v6

--- a/solution.py
+++ b/solution.py
@@ -324,9 +324,8 @@
 
 
 def basis_kernel(plan, scale, addends, *rest):
-    packed = rest[0][...]
-    for other in rest[1:addends]:
-        packed = packed + other[...]
+    own, one, two, three = (ref[...] for ref in rest[:addends])
+    packed = (own + one) + (two + three)
     split_ref, out_hbm, left, right, held, sems = rest[addends:]
     invert_factor(unfolded(packed), left, right)
     weight = right[...] * scale
@@ -372,7 +371,8 @@
 
 
 def sum_four(value, axis, bit):
-    return value + sum(swapped(value, axis, k << bit) for k in (1, 2, 3))
+    one, two, three = (swapped(value, axis, k << bit) for k in (1, 2, 3))
+    return (value + one) + (two + three)
 
 
 def sum_over(value, axis, bits):

time: 65.1 us -> 65.1 us (level)
  no operation moved by 1% of the time
where the time goes in v7:
time: 65.1 us; the launch traced here: 64.9 us
  waiting for transfers between devices  31.5 us (48%)
  starting transfers between devices  17.5 us (27%)
  Pallas kernels  15.2 us (23%)
  between operations  0.7 us (1%)
    ppermute x14, waiting for transfers between devices, swapped(): return lax.ppermute(value, axis, pairs)  31.5 us
    ppermute x14, starting transfers between devices, swapped(): return lax.ppermute(value, axis, pairs)  17.5 us
    pallas_call x5, Pallas kernels, add_rows(): pl.pallas_call(functools.partial(field_kernel, plan, first, last, count),...  6.98 us
    pallas_call x1, Pallas kernels, make_basis(): pl.pallas_call(functools.partial(basis_kernel, plan, scale, len(grams)),...  6.75 us
    pallas_call x1, Pallas kernels, pack(): pl.pallas_call(functools.partial(pack_kernel, plan), out_shape=plan.shape...  1.47 us
  transfers between devices with their start and end apart: 14, of which 8 were waited for; matrix products, arithmetic and copies ran while one was open for 0% of the time, Pallas kernels for 7%

profile of v7, /device:TPU:0, one launch (start us, length us, event | category | flops | bytes accessed | tf_op | source)
XLA Modules:
  0.0 64.9 jit_solution(18291541851425345068)
XLA Ops:
  0.7 1.5 %pack_windows.1 = (bf16[1392,128]{1,0:T(8,128)(2,1)S(1)}, bf16[864,128]{1,0:T(8,128)(2,1)S(1)}, bf16[864,128]{1,0:T(8,128)(2,1)S(1)}, bf16[1392,128]{1,0:T(8,128)(2,1)S(1)}, bf16[1392,128]{1,0:T(8,128)(2,1)S(1)}) custom-call(s32[1]{0:T(128)} %bitcast.band_ref, s32[1]{0:T(128)S(6)} %copy.11.count_ref, s32[1,5]{1,0:T(1,128)} %station_hbm.1, ...), custom_call_target="tpu_custom_call" | custom-call | bytes 4194304 | tf_op jit(solution)/shard_map/pack_windows/pallas_call | solution.py:141
  2.1 4.1 %collective-permute-start.1 = (bf16[1392,128]{1,0:T(8,128)(2,1)S(1)}, bf16[1392,128]{1,0:T(8,128)(2,1)S(1)}, u32[]{:S(2)}, u32[]{:S(2)}) collective-permute-start(bf16[1392,128]{1,0:T(8,128)(2,1)S(1)} %get-tuple-element.15), channel_id=1, source_target_pairs={{0,4},{1,5},{2,6},{3,7},{4,0},{5,1},{6,2},{7,3},{8,12},{9,13},{10,... | collective-permute-start | bytes 1069064 | tf_op jit(solution)/shard_map/ppermute | solution.py:23
  6.3 1.3 %collective-permute-start = (bf16[1392,128]{1,0:T(8,128)(2,1)S(1)}, bf16[1392,128]{1,0:T(8,128)(2,1)S(1)}, u32[]{:S(2)}, u32[]{:S(2)}) collective-permute-start(bf16[1392,128]{1,0:T(8,128)(2,1)S(1)} %get-tuple-element.14), channel_id=1, source_target_pairs={{0,6},{1,7},{2,4},{3,5},{4,2},{5,3},{6,0},{7,1},{8,14},{9,15},{10,... | collective-permute-start | bytes 1069064 | tf_op jit(solution)/shard_map/ppermute | solution.py:23
  7.8 1.3 %collective-permute-start.3 = (bf16[864,128]{1,0:T(8,128)(2,1)S(1)}, bf16[864,128]{1,0:T(8,128)(2,1)S(1)}, u32[]{:S(2)}, u32[]{:S(2)}) collective-permute-start(bf16[864,128]{1,0:T(8,128)(2,1)S(1)} %get-tuple-element.17), channel_id=1, source_target_pairs={{0,3},{1,2},{2,1},{3,0},{4,7},{5,6},{6,5},{7,4},{8,11},{9,10},{10,... | collective-permute-start | bytes 663560 | tf_op jit(solution)/shard_map/ppermute | solution.py:23
  9.2 21.5 %collective-permute-done.1.rest_0_ = bf16[1392,128]{1,0:T(8,128)(2,1)S(1)} collective-permute-done((bf16[1392,128]{1,0:T(8,128)(2,1)S(1)}, bf16[1392,128]{1,0:T(8,128)(2,1)S(1)}, u32[]{:S(2)}, u32[]{:S(2)}) %collective-permute-start.1) | collective-permute-done | bytes 356384 | tf_op jit(solution)/shard_map/ppermute | solution.py:23
  30.7 1.4 %field.4.rest_2_ = f32[8,544,128]{2,1,0:T(8,128)S(1)} custom-call(s32[1]{0:T(128)} %bitcast.band_ref, bf16[1392,128]{1,0:T(8,128)(2,1)S(1)} %get-tuple-element.18.rest_0_, bf16[1392,128]{1,0:T(8,128)(2,1)S(1)} %collective-permute-done.4.rest_1_), custom_call_target="tpu_custom_call" | custom-call | flops 1048576 | bytes 65536 | tf_op jit(solution)/shard_map/field/pallas_call | solution.py:246
  32.2 1.2 %collective-permute-done.3.rest_1_ = bf16[864,128]{1,0:T(8,128)(2,1)S(1)} collective-permute-done((bf16[864,128]{1,0:T(8,128)(2,1)S(1)}, bf16[864,128]{1,0:T(8,128)(2,1)S(1)}, u32[]{:S(2)}, u32[]{:S(2)}) %collective-permute-start.3) | collective-permute-done | bytes 221216 | tf_op jit(solution)/shard_map/ppermute | solution.py:23
  33.3 1.3 %field.5.rest_1_ = f32[8,544,128]{2,1,0:T(8,128)S(1)} custom-call(s32[1]{0:T(128)} %bitcast.band_ref, bf16[864,128]{1,0:T(8,128)(2,1)S(1)} %collective-permute-done.2.rest_0_, bf16[864,128]{1,0:T(8,128)(2,1)S(1)} %collective-permute-done.3.rest_1_, f32[8,544,128]{2,1,0:T(8,128)S(1)} %field.4.rest_2_), custom_call_target="tpu_custom_call", output_to_operand_aliasing={{}: (3, {})} | custom-call | flops 1048576 | bytes 65536 | tf_op jit(solution)/shard_map/field/pallas_call | solution.py:246
  34.6 0.9 %field.6.rest_2_ = f32[8,544,128]{2,1,0:T(8,128)S(1)} custom-call(s32[1]{0:T(128)} %bitcast.band_ref, bf16[1392,128]{1,0:T(8,128)(2,1)S(1)} %collective-permute-done.1.rest_0_, f32[8,544,128]{2,1,0:T(8,128)S(1)} %field.5.rest_1_), custom_call_target="tpu_custom_call", output_to_operand_aliasing={{}: (2, {})} | custom-call | flops 1048576 | bytes 65536 | tf_op jit(solution)/shard_map/field/pallas_call | solution.py:246
  35.5 0.6 collective-permute-start.5
  36.1 1.3 %field.7.rest_1_ = f32[8,544,128]{2,1,0:T(8,128)S(1)} custom-call(s32[1]{0:T(128)} %bitcast.band_ref, bf16[1392,128]{1,0:T(8,128)(2,1)S(1)} %collective-permute-done.rest_0_, bf16[1392,128]{1,0:T(8,128)(2,1)S(1)} %collective-permute-done.6.rest_1_, f32[8,544,128]{2,1,0:T(8,128)S(1)} %field.6.rest_2_), custom_call_target="tpu_custom_call", output_to_operand_aliasing={{}: (3, {})} | custom-call | flops 1048576 | bytes 65536 | tf_op jit(solution)/shard_map/field/pallas_call | solution.py:246
  37.4 2.1 %field_and_gram.1 = (bf16[8,544,256]{2,1,0:T(8,128)(2,1)S(1)}, f32[80,128]{1,0:T(8,128)S(1)}) custom-call(s32[1]{0:T(128)} %bitcast.band_ref, bf16[1392,128]{1,0:T(8,128)(2,1)S(1)} %collective-permute-done.5.rest_0_, f32[8,544,128]{2,1,0:T(8,128)S(1)} %field.7.rest_1_), custom_call_target="tpu_custom_call" | custom-call | flops 1048576 | bytes 65536 | tf_op jit(solution)/shard_map/field_and_gram/pallas_call | solution.py:246
  39.9 0.9 %collective-permute-done.7 = f32[80,128]{1,0:T(8,128)S(1)} collective-permute-done((f32[80,128]{1,0:T(8,128)S(1)}, f32[80,128]{1,0:T(8,128)S(1)}, u32[]{:S(2)}, u32[]{:S(2)}) %collective-permute-start.7) | collective-permute-done | bytes 40992 | tf_op jit(solution)/shard_map/ppermute | solution.py:23
  40.8 1.5 %collective-permute-start.9 = (f32[80,128]{1,0:T(8,128)S(1)}, f32[80,128]{1,0:T(8,128)S(1)}, u32[]{:S(2)}, u32[]{:S(2)}) collective-permute-start(f32[80,128]{1,0:T(8,128)S(1)} %add.12), channel_id=1, source_target_pairs={{0,16},{8,24},{16,0},{24,8},{1,17},{9,25},{17,1},{25,9},{2,18},{10... | collective-permute-start | bytes 122888 | tf_op jit(solution)/shard_map/ppermute | solution.py:23
  42.3 1.4 %collective-permute-start.10 = (f32[80,128]{1,0:T(8,128)S(1)}, f32[80,128]{1,0:T(8,128)S(1)}, u32[]{:S(2)}, u32[]{:S(2)}) collective-permute-start(f32[80,128]{1,0:T(8,128)S(1)} %add.12), channel_id=1, source_target_pairs={{0,24},{8,16},{16,8},{24,0},{1,25},{9,17},{17,9},{25,1},{2,26},{10... | collective-permute-start | bytes 122888 | tf_op jit(solution)/shard_map/ppermute | solution.py:23
  43.8 0.5 collective-permute-start.8
  44.3 0.5 collective-permute-done.9
  44.8 2.6 %collective-permute-done.10 = f32[80,128]{1,0:T(8,128)S(1)} collective-permute-done((f32[80,128]{1,0:T(8,128)S(1)}, f32[80,128]{1,0:T(8,128)S(1)}, u32[]{:S(2)}, u32[]{:S(2)}) %collective-permute-start.10) | collective-permute-done | bytes 40992 | tf_op jit(solution)/shard_map/ppermute | solution.py:23
  47.8 2.6 %collective-permute-start.11 = (f32[80,128]{1,0:T(8,128)S(1)}, f32[80,128]{1,0:T(8,128)S(1)}, u32[]{:S(2)}, u32[]{:S(2)}) collective-permute-start(f32[80,128]{1,0:T(8,128)S(1)} %add_add_fusion.rest_0_), channel_id=1, source_target_pairs={{0,2},{1,3},{2,0},{3,1},{4,6},{5,7},{6,4},{7,5},{8,10},{9,11},{10,... | collective-permute-start | bytes 122888 | tf_op jit(solution)/shard_map/ppermute | solution.py:23
  50.4 2.0 %collective-permute-start.12 = (f32[80,128]{1,0:T(8,128)S(1)}, f32[80,128]{1,0:T(8,128)S(1)}, u32[]{:S(2)}, u32[]{:S(2)}) collective-permute-start(f32[80,128]{1,0:T(8,128)S(1)} %add_add_fusion.rest_0_), channel_id=1, source_target_pairs={{0,4},{1,5},{2,6},{3,7},{4,0},{5,1},{6,2},{7,3},{8,12},{9,13},{10,... | collective-permute-start | bytes 122888 | tf_op jit(solution)/shard_map/ppermute | solution.py:23
  52.3 1.4 %collective-permute-start.13 = (f32[80,128]{1,0:T(8,128)S(1)}, f32[80,128]{1,0:T(8,128)S(1)}, u32[]{:S(2)}, u32[]{:S(2)}) collective-permute-start(f32[80,128]{1,0:T(8,128)S(1)} %add_add_fusion.rest_0_), channel_id=1, source_target_pairs={{0,6},{1,7},{2,4},{3,5},{4,2},{5,3},{6,0},{7,1},{8,14},{9,15},{10,... | collective-permute-start | bytes 122888 | tf_op jit(solution)/shard_map/ppermute | solution.py:23
  53.7 1.9 %collective-permute-done.12.rest_2_ = f32[80,128]{1,0:T(8,128)S(1)} collective-permute-done((f32[80,128]{1,0:T(8,128)S(1)}, f32[80,128]{1,0:T(8,128)S(1)}, u32[]{:S(2)}, u32[]{:S(2)}) %collective-permute-start.12) | collective-permute-done | bytes 40992 | tf_op jit(solution)/shard_map/ppermute | solution.py:23
  55.6 2.5 %collective-permute-done.13.rest_3_ = f32[80,128]{1,0:T(8,128)S(1)} collective-permute-done((f32[80,128]{1,0:T(8,128)S(1)}, f32[80,128]{1,0:T(8,128)S(1)}, u32[]{:S(2)}, u32[]{:S(2)}) %collective-permute-start.13) | collective-permute-done | bytes 40992 | tf_op jit(solution)/shard_map/ppermute | solution.py:23
  58.2 6.8 %factor_and_basis.1 = f32[4320,128]{1,0:T(8,128)} custom-call(f32[80,128]{1,0:T(8,128)S(1)} %add_add_fusion.rest_0_, f32[80,128]{1,0:T(8,128)S(1)} %collective-permute-done.11.rest_1_, f32[80,128]{1,0:T(8,128)S(1)} %collective-permute-done.12.rest_2_, f32[80,128]{1,0:T(8,128)S(1)} %collective-permute-done.13.rest_3_, ...), custom_call_target="tpu_custom_call" | custom-call | tf_op jit(solution)/shard_map/factor_and_basis/pallas_call | solution.py:360
  (13 shorter events, 1.0 us)
Async XLA Ops:
  2.1 28.6 %collective-permute-start.1 = (bf16[1392,128]{1,0:T(8,128)(2,1)S(1)}, bf16[1392,128]{1,0:T(8,128)(2,1)S(1)}, u32[]{:S(2)}, u32[]{:S(2)}) collective-permute-start(bf16[1392,128]{1,0:T(8,128)(2,1)S(1)} %get-tuple-element.15), channel_id=1, source_target_pairs={{0,4},{1,5},{2,6},{3,7},{4,0},{5,1},{6,2},{7,3},{8,12},{9,13},{10,... | collective-permute-start | bytes 1069064 | tf_op jit(solution)/shard_map/ppermute | solution.py:23
  6.3 24.5 %collective-permute-start.4 = (bf16[1392,128]{1,0:T(8,128)(2,1)S(1)}, bf16[1392,128]{1,0:T(8,128)(2,1)S(1)}, u32[]{:S(2)}, u32[]{:S(2)}) collective-permute-start(bf16[1392,128]{1,0:T(8,128)(2,1)S(1)} %get-tuple-element.18.rest_0_), channel_id=1, source_target_pairs={{0,1},{1,0},{2,3},{3,2},{4,5},{5,4},{6,7},{7,6},{8,9},{9,8},{10,11... | collective-permute-start | bytes 1069064 | tf_op jit(solution)/shard_map/ppermute | solution.py:23
  6.3 29.2 %collective-permute-start = (bf16[1392,128]{1,0:T(8,128)(2,1)S(1)}, bf16[1392,128]{1,0:T(8,128)(2,1)S(1)}, u32[]{:S(2)}, u32[]{:S(2)}) collective-permute-start(bf16[1392,128]{1,0:T(8,128)(2,1)S(1)} %get-tuple-element.14), channel_id=1, source_target_pairs={{0,6},{1,7},{2,4},{3,5},{4,2},{5,3},{6,0},{7,1},{8,14},{9,15},{10,... | collective-permute-start | bytes 1069064 | tf_op jit(solution)/shard_map/ppermute | solution.py:23
  7.6 24.5 %collective-permute-start.2 = (bf16[864,128]{1,0:T(8,128)(2,1)S(1)}, bf16[864,128]{1,0:T(8,128)(2,1)S(1)}, u32[]{:S(2)}, u32[]{:S(2)}) collective-permute-start(bf16[864,128]{1,0:T(8,128)(2,1)S(1)} %get-tuple-element.16), channel_id=1, source_target_pairs={{0,2},{1,3},{2,0},{3,1},{4,6},{5,7},{6,4},{7,5},{8,10},{9,11},{10,... | collective-permute-start | bytes 663560 | tf_op jit(solution)/shard_map/ppermute | solution.py:23
  7.8 25.5 %collective-permute-start.3 = (bf16[864,128]{1,0:T(8,128)(2,1)S(1)}, bf16[864,128]{1,0:T(8,128)(2,1)S(1)}, u32[]{:S(2)}, u32[]{:S(2)}) collective-permute-start(bf16[864,128]{1,0:T(8,128)(2,1)S(1)} %get-tuple-element.17), channel_id=1, source_target_pairs={{0,3},{1,2},{2,1},{3,0},{4,7},{5,6},{6,5},{7,4},{8,11},{9,10},{10,... | collective-permute-start | bytes 663560 | tf_op jit(solution)/shard_map/ppermute | solution.py:23
  30.7 5.3 %collective-permute-start.6 = (bf16[1392,128]{1,0:T(8,128)(2,1)S(1)}, bf16[1392,128]{1,0:T(8,128)(2,1)S(1)}, u32[]{:S(2)}, u32[]{:S(2)}) collective-permute-start(bf16[1392,128]{1,0:T(8,128)(2,1)S(1)} %collective-permute-done.1.rest_0_), channel_id=1, source_target_pairs={{0,1},{1,0},{2,3},{3,2},{4,5},{5,4},{6,7},{7,6},{8,9},{9,8},{10,11... | collective-permute-start | bytes 1069064 | tf_op jit(solution)/shard_map/ppermute | solution.py:23
  35.5 1.9 %collective-permute-start.5 = (bf16[1392,128]{1,0:T(8,128)(2,1)S(1)}, bf16[1392,128]{1,0:T(8,128)(2,1)S(1)}, u32[]{:S(2)}, u32[]{:S(2)}) collective-permute-start(bf16[1392,128]{1,0:T(8,128)(2,1)S(1)} %collective-permute-done.rest_0_), channel_id=1, source_target_pairs={{0,1},{1,0},{2,3},{3,2},{4,5},{5,4},{6,7},{7,6},{8,9},{9,8},{10,11... | collective-permute-start | bytes 1069064 | tf_op jit(solution)/shard_map/ppermute | solution.py:23
  39.5 1.3 %collective-permute-start.7 = (f32[80,128]{1,0:T(8,128)S(1)}, f32[80,128]{1,0:T(8,128)S(1)}, u32[]{:S(2)}, u32[]{:S(2)}) collective-permute-start(f32[80,128]{1,0:T(8,128)S(1)} %get-tuple-element.21), channel_id=1, source_target_pairs={{0,1},{1,0},{2,3},{3,2},{4,5},{5,4},{6,7},{7,6},{8,9},{9,8},{10,11... | collective-permute-start | bytes 122888 | tf_op jit(solution)/shard_map/ppermute | solution.py:23
  40.8 4.0 %collective-permute-start.9 = (f32[80,128]{1,0:T(8,128)S(1)}, f32[80,128]{1,0:T(8,128)S(1)}, u32[]{:S(2)}, u32[]{:S(2)}) collective-permute-start(f32[80,128]{1,0:T(8,128)S(1)} %add.12), channel_id=1, source_target_pairs={{0,16},{8,24},{16,0},{24,8},{1,17},{9,25},{17,1},{25,9},{2,18},{10... | collective-permute-start | bytes 122888 | tf_op jit(solution)/shard_map/ppermute | solution.py:23
  42.3 5.0 %collective-permute-start.10 = (f32[80,128]{1,0:T(8,128)S(1)}, f32[80,128]{1,0:T(8,128)S(1)}, u32[]{:S(2)}, u32[]{:S(2)}) collective-permute-start(f32[80,128]{1,0:T(8,128)S(1)} %add.12), channel_id=1, source_target_pairs={{0,24},{8,16},{16,8},{24,0},{1,25},{9,17},{17,9},{25,1},{2,26},{10... | collective-permute-start | bytes 122888 | tf_op jit(solution)/shard_map/ppermute | solution.py:23
  43.8 4.0 %collective-permute-start.8 = (f32[80,128]{1,0:T(8,128)S(1)}, f32[80,128]{1,0:T(8,128)S(1)}, u32[]{:S(2)}, u32[]{:S(2)}) collective-permute-start(f32[80,128]{1,0:T(8,128)S(1)} %add.12), channel_id=1, source_target_pairs={{0,8},{8,0},{16,24},{24,16},{1,9},{9,1},{17,25},{25,17},{2,10},{10... | collective-permute-start | bytes 122888 | tf_op jit(solution)/shard_map/ppermute | solution.py:23
  47.8 6.0 %collective-permute-start.11 = (f32[80,128]{1,0:T(8,128)S(1)}, f32[80,128]{1,0:T(8,128)S(1)}, u32[]{:S(2)}, u32[]{:S(2)}) collective-permute-start(f32[80,128]{1,0:T(8,128)S(1)} %add_add_fusion.rest_0_), channel_id=1, source_target_pairs={{0,2},{1,3},{2,0},{3,1},{4,6},{5,7},{6,4},{7,5},{8,10},{9,11},{10,... | collective-permute-start | bytes 122888 | tf_op jit(solution)/shard_map/ppermute | solution.py:23
  50.4 5.3 %collective-permute-start.12 = (f32[80,128]{1,0:T(8,128)S(1)}, f32[80,128]{1,0:T(8,128)S(1)}, u32[]{:S(2)}, u32[]{:S(2)}) collective-permute-start(f32[80,128]{1,0:T(8,128)S(1)} %add_add_fusion.rest_0_), channel_id=1, source_target_pairs={{0,4},{1,5},{2,6},{3,7},{4,0},{5,1},{6,2},{7,3},{8,12},{9,13},{10,... | collective-permute-start | bytes 122888 | tf_op jit(solution)/shard_map/ppermute | solution.py:23
  52.3 5.8 %collective-permute-start.13 = (f32[80,128]{1,0:T(8,128)S(1)}, f32[80,128]{1,0:T(8,128)S(1)}, u32[]{:S(2)}, u32[]{:S(2)}) collective-permute-start(f32[80,128]{1,0:T(8,128)S(1)} %add_add_fusion.rest_0_), channel_id=1, source_target_pairs={{0,6},{1,7},{2,4},{3,5},{4,2},{5,3},{6,0},{7,1},{8,14},{9,15},{10,... | collective-permute-start | bytes 122888 | tf_op jit(solution)/shard_map/ppermute | solution.py:23

commit v8 on v7

--- a/solution.py
+++ b/solution.py
@@ -52,12 +52,12 @@
     def size(self, near):
         return self.sub if near else self.window
 
-    def shapes(self):
-        return [jax.ShapeDtypeStruct((self.size(near) + self.extra, LANES), jnp.bfloat16) for _, near in self.sends]
-
-
-def pack_kernel(plan, band_ref, count_ref, station_hbm, taps_hbm, probes_hbm, *rest):
-    peers = len(plan.sends)
+    def shapes(self, sends):
+        return [jax.ShapeDtypeStruct((self.size(near) + self.extra, LANES), jnp.bfloat16) for _, near in sends]
+
+
+def pack_kernel(plan, sends, band_ref, count_ref, station_hbm, taps_hbm, probes_hbm, *rest):
+    peers = len(sends)
     messages = rest[:peers]
     station_ref, taps_ref, rows_f32, in_sems, out_sems = rest[peers:]
     loads = [(station_hbm, station_ref), (taps_hbm, taps_ref)]
@@ -66,7 +66,7 @@
         copy.start()
 
     def windows(peer, act):
-        mask, near = plan.sends[peer]
+        mask, near = sends[peer]
         size = plan.size(near)
         other = band_ref[0] ^ mask
         if not near:
@@ -125,7 +125,7 @@
     rows_f32[pl.ds(plan.slots * plan.tap_rows, 1), :] = names
     rows_bf = rows_f32[...].astype(jnp.bfloat16)
     for peer in order:
-        messages[peer][pl.ds(plan.size(plan.sends[peer][1]), plan.extra), :] = rows_bf
+        messages[peer][pl.ds(plan.size(sends[peer][1]), plan.extra), :] = rows_bf
     for peer in order:
         windows(peer, lambda copy: copy.wait())
 
@@ -134,13 +134,13 @@
     return pltpu.with_memory_space_constraint(value, pltpu.HBM)
 
 
-def pack(plan, band, probes, taps, station, count):
-    peers = len(plan.sends)
+def pack(plan, sends, band, probes, taps, station, count):
+    peers = len(sends)
     hbm = pl.BlockSpec(memory_space=pltpu.HBM)
     smem = pl.BlockSpec(memory_space=pltpu.SMEM)
     return pl.pallas_call(
-        functools.partial(pack_kernel, plan),
-        out_shape=plan.shapes(),
+        functools.partial(pack_kernel, plan, sends),
+        out_shape=plan.shapes(sends),
         in_specs=[smem] * 2 + [hbm] * 3,
         out_specs=[pl.BlockSpec(memory_space=pltpu.VMEM)] * peers,
         scratch_shapes=[
@@ -396,9 +396,10 @@
     band_size, grp_size = lax.axis_size("band"), lax.axis_size("grp")
     plan = Plan(length, taps, slots, band_size)
     band = lax.axis_index("band").astype(jnp.int32).reshape(1)
-    messages = pack(
-        plan, band, probes.reshape(length, probe_count), kernel.reshape(slots, taps), pair_station, pair_count
-    )
+    operands = probes.reshape(length, probe_count), kernel.reshape(slots, taps), pair_station, pair_count
+    close = [send for send in plan.sends if send[0] < 4]
+    messages = pack(plan, plan.sends[len(close) :], band, *operands)
+    messages = pack(plan, close, band, *operands) + messages
     arrived = [
         value if mask == 0 else swapped(value, "band", mask)
         for value, (mask, near) in zip(messages, plan.sends)

time: 65.1 us -> 65.7 us (level)
  starting transfers between devices: 17.5 us -> 16.2 us
  Pallas kernels: 15.2 us -> 16.2 us
  waiting for transfers between devices: 31.5 us -> 32.4 us
    ppermute x14, starting transfers between devices: 17.5 us -> 16.2 us  [swapped(): return lax.ppermute(value, axis, pairs)]
    pallas_call x1 -> x2, Pallas kernels: 1.47 us -> 2.46 us  [pack(): pl.pallas_call(functools.partial(pack_kernel, plan, sends), out_shape=pla...]
    ppermute x14, waiting for transfers between devices: 31.5 us -> 32.4 us  [swapped(): return lax.ppermute(value, axis, pairs)]
  transfers between devices with their start and end apart: 14 -> 14, of which waited for: 8 -> 8; matrix products, arithmetic and copies ran while one was open for 0% -> 0% of each run, Pallas kernels for 7% -> 9%
where the time goes in v8:
time: 65.7 us; the launch traced here: 65.5 us
  waiting for transfers between devices  32.4 us (49%)
  Pallas kernels  16.2 us (25%)
  starting transfers between devices  16.2 us (25%)
  between operations  0.72 us (1%)
    ppermute x14, waiting for transfers between devices, swapped(): return lax.ppermute(value, axis, pairs)  32.4 us
    ppermute x14, starting transfers between devices, swapped(): return lax.ppermute(value, axis, pairs)  16.2 us
    pallas_call x5, Pallas kernels, add_rows(): pl.pallas_call(functools.partial(field_kernel, plan, first, last, count),...  6.98 us
    pallas_call x1, Pallas kernels, make_basis(): pl.pallas_call(functools.partial(basis_kernel, plan, scale, len(grams)),...  6.75 us
    pallas_call x2, Pallas kernels, pack(): pl.pallas_call(functools.partial(pack_kernel, plan, sends), out_shape=pla...  2.46 us
  transfers between devices with their start and end apart: 14, of which 8 were waited for; matrix products, arithmetic and copies ran while one was open for 0% of the time, Pallas kernels for 9%

profile of v8, /device:TPU:0, one launch (start us, length us, event | category | flops | bytes accessed | tf_op | source)
XLA Modules:
  0.0 65.5 jit_solution(10432946207871148919)
XLA Ops:
  0.7 1.2 %pack_windows.2 = (bf16[1392,128]{1,0:T(8,128)(2,1)S(1)}, bf16[1392,128]{1,0:T(8,128)(2,1)S(1)}) custom-call(s32[1]{0:T(128)} %bitcast.band_ref, s32[1]{0:T(128)S(6)} %copy.11.count_ref, s32[1,5]{1,0:T(1,128)} %station_hbm.3, bf16[5,289]{1,0:T(8,128)(2,1)} %bitcast.8, bf16[4320,128]{1,0:T(8,128)(2,1)} %bitcast.6), custom_call_target="tpu_custom_call" | custom-call | bytes 4194304 | tf_op jit(solution)/shard_map/pack_windows/pallas_call | solution.py:141
  1.8 4.1 %collective-permute-start.1 = (bf16[1392,128]{1,0:T(8,128)(2,1)S(1)}, bf16[1392,128]{1,0:T(8,128)(2,1)S(1)}, u32[]{:S(2)}, u32[]{:S(2)}) collective-permute-start(bf16[1392,128]{1,0:T(8,128)(2,1)S(1)} %get-tuple-element.15), channel_id=1, source_target_pairs={{0,4},{1,5},{2,6},{3,7},{4,0},{5,1},{6,2},{7,3},{8,12},{9,13},{10,... | collective-permute-start | bytes 1069064 | tf_op jit(solution)/shard_map/ppermute | solution.py:23
  5.9 1.3 %pack_windows.3 = (bf16[1392,128]{1,0:T(8,128)(2,1)S(1)}, bf16[864,128]{1,0:T(8,128)(2,1)S(1)}, bf16[864,128]{1,0:T(8,128)(2,1)S(1)}) custom-call(s32[1]{0:T(128)} %bitcast.band_ref, s32[1]{0:T(128)S(6)} %copy.11.count_ref, s32[1,5]{1,0:T(1,128)} %station_hbm.3, bf16[5,289]{1,0:T(8,128)(2,1)} %bitcast.9, bf16[4320,128]{1,0:T(8,128)(2,1)} %bitcast.7), custom_call_target="tpu_custom_call" | custom-call | bytes 4194304 | tf_op jit(solution)/shard_map/pack_windows/pallas_call | solution.py:141
  7.3 1.4 %collective-permute-start = (bf16[1392,128]{1,0:T(8,128)(2,1)S(1)}, bf16[1392,128]{1,0:T(8,128)(2,1)S(1)}, u32[]{:S(2)}, u32[]{:S(2)}) collective-permute-start(bf16[1392,128]{1,0:T(8,128)(2,1)S(1)} %get-tuple-element.14), channel_id=1, source_target_pairs={{0,6},{1,7},{2,4},{3,5},{4,2},{5,3},{6,0},{7,1},{8,14},{9,15},{10,... | collective-permute-start | bytes 1069064 | tf_op jit(solution)/shard_map/ppermute | solution.py:23
  9.0 1.2 %collective-permute-start.3 = (bf16[864,128]{1,0:T(8,128)(2,1)S(1)}, bf16[864,128]{1,0:T(8,128)(2,1)S(1)}, u32[]{:S(2)}, u32[]{:S(2)}) collective-permute-start(bf16[864,128]{1,0:T(8,128)(2,1)S(1)} %get-tuple-element.17), channel_id=1, source_target_pairs={{0,3},{1,2},{2,1},{3,0},{4,7},{5,6},{6,5},{7,4},{8,11},{9,10},{10,... | collective-permute-start | bytes 663560 | tf_op jit(solution)/shard_map/ppermute | solution.py:23
  10.2 20.2 %collective-permute-done.1.rest_0_ = bf16[1392,128]{1,0:T(8,128)(2,1)S(1)} collective-permute-done((bf16[1392,128]{1,0:T(8,128)(2,1)S(1)}, bf16[1392,128]{1,0:T(8,128)(2,1)S(1)}, u32[]{:S(2)}, u32[]{:S(2)}) %collective-permute-start.1) | collective-permute-done | bytes 356384 | tf_op jit(solution)/shard_map/ppermute | solution.py:23
  30.4 1.4 %field.4.rest_2_ = f32[8,544,128]{2,1,0:T(8,128)S(1)} custom-call(s32[1]{0:T(128)} %bitcast.band_ref, bf16[1392,128]{1,0:T(8,128)(2,1)S(1)} %get-tuple-element.18.rest_0_, bf16[1392,128]{1,0:T(8,128)(2,1)S(1)} %collective-permute-done.4.rest_1_), custom_call_target="tpu_custom_call" | custom-call | flops 1048576 | bytes 65536 | tf_op jit(solution)/shard_map/field/pallas_call | solution.py:246
  31.8 2.4 %collective-permute-done.3.rest_1_ = bf16[864,128]{1,0:T(8,128)(2,1)S(1)} collective-permute-done((bf16[864,128]{1,0:T(8,128)(2,1)S(1)}, bf16[864,128]{1,0:T(8,128)(2,1)S(1)}, u32[]{:S(2)}, u32[]{:S(2)}) %collective-permute-start.3) | collective-permute-done | bytes 221216 | tf_op jit(solution)/shard_map/ppermute | solution.py:23
  34.3 1.3 %field.5.rest_1_ = f32[8,544,128]{2,1,0:T(8,128)S(1)} custom-call(s32[1]{0:T(128)} %bitcast.band_ref, bf16[864,128]{1,0:T(8,128)(2,1)S(1)} %collective-permute-done.2.rest_0_, bf16[864,128]{1,0:T(8,128)(2,1)S(1)} %collective-permute-done.3.rest_1_, f32[8,544,128]{2,1,0:T(8,128)S(1)} %field.4.rest_2_), custom_call_target="tpu_custom_call", output_to_operand_aliasing={{}: (3, {})} | custom-call | flops 1048576 | bytes 65536 | tf_op jit(solution)/shard_map/field/pallas_call | solution.py:246
  35.6 0.9 %field.6.rest_2_ = f32[8,544,128]{2,1,0:T(8,128)S(1)} custom-call(s32[1]{0:T(128)} %bitcast.band_ref, bf16[1392,128]{1,0:T(8,128)(2,1)S(1)} %collective-permute-done.1.rest_0_, f32[8,544,128]{2,1,0:T(8,128)S(1)} %field.5.rest_1_), custom_call_target="tpu_custom_call", output_to_operand_aliasing={{}: (2, {})} | custom-call | flops 1048576 | bytes 65536 | tf_op jit(solution)/shard_map/field/pallas_call | solution.py:246
  36.4 0.7 %collective-permute-start.5 = (bf16[1392,128]{1,0:T(8,128)(2,1)S(1)}, bf16[1392,128]{1,0:T(8,128)(2,1)S(1)}, u32[]{:S(2)}, u32[]{:S(2)}) collective-permute-start(bf16[1392,128]{1,0:T(8,128)(2,1)S(1)} %collective-permute-done.rest_0_), channel_id=1, source_target_pairs={{0,1},{1,0},{2,3},{3,2},{4,5},{5,4},{6,7},{7,6},{8,9},{9,8},{10,11... | collective-permute-start | bytes 1069064 | tf_op jit(solution)/shard_map/ppermute | solution.py:23
  37.1 1.3 %field.7.rest_1_ = f32[8,544,128]{2,1,0:T(8,128)S(1)} custom-call(s32[1]{0:T(128)} %bitcast.band_ref, bf16[1392,128]{1,0:T(8,128)(2,1)S(1)} %collective-permute-done.rest_0_, bf16[1392,128]{1,0:T(8,128)(2,1)S(1)} %collective-permute-done.6.rest_1_, f32[8,544,128]{2,1,0:T(8,128)S(1)} %field.6.rest_2_), custom_call_target="tpu_custom_call", output_to_operand_aliasing={{}: (3, {})} | custom-call | flops 1048576 | bytes 65536 | tf_op jit(solution)/shard_map/field/pallas_call | solution.py:246
  38.4 2.1 %field_and_gram.1 = (bf16[8,544,256]{2,1,0:T(8,128)(2,1)S(1)}, f32[80,128]{1,0:T(8,128)S(1)}) custom-call(s32[1]{0:T(128)} %bitcast.band_ref, bf16[1392,128]{1,0:T(8,128)(2,1)S(1)} %collective-permute-done.5.rest_0_, f32[8,544,128]{2,1,0:T(8,128)S(1)} %field.7.rest_1_), custom_call_target="tpu_custom_call" | custom-call | flops 1048576 | bytes 65536 | tf_op jit(solution)/shard_map/field_and_gram/pallas_call | solution.py:246
  40.9 0.9 %collective-permute-done.7 = f32[80,128]{1,0:T(8,128)S(1)} collective-permute-done((f32[80,128]{1,0:T(8,128)S(1)}, f32[80,128]{1,0:T(8,128)S(1)}, u32[]{:S(2)}, u32[]{:S(2)}) %collective-permute-start.7) | collective-permute-done | bytes 40992 | tf_op jit(solution)/shard_map/ppermute | solution.py:23
  41.8 2.5 %collective-permute-start.10 = (f32[80,128]{1,0:T(8,128)S(1)}, f32[80,128]{1,0:T(8,128)S(1)}, u32[]{:S(2)}, u32[]{:S(2)}) collective-permute-start(f32[80,128]{1,0:T(8,128)S(1)} %add.12), channel_id=1, source_target_pairs={{0,24},{8,16},{16,8},{24,0},{1,25},{9,17},{17,9},{25,1},{2,26},{10... | collective-permute-start | bytes 122888 | tf_op jit(solution)/shard_map/ppermute | solution.py:23
  44.3 0.5 collective-permute-start.8
  45.3 1.4 %collective-permute-done.10 = f32[80,128]{1,0:T(8,128)S(1)} collective-permute-done((f32[80,128]{1,0:T(8,128)S(1)}, f32[80,128]{1,0:T(8,128)S(1)}, u32[]{:S(2)}, u32[]{:S(2)}) %collective-permute-start.10) | collective-permute-done | bytes 40992 | tf_op jit(solution)/shard_map/ppermute | solution.py:23
  46.7 1.6 %collective-permute-done.8 = f32[80,128]{1,0:T(8,128)S(1)} collective-permute-done((f32[80,128]{1,0:T(8,128)S(1)}, f32[80,128]{1,0:T(8,128)S(1)}, u32[]{:S(2)}, u32[]{:S(2)}) %collective-permute-start.8) | collective-permute-done | bytes 40992 | tf_op jit(solution)/shard_map/ppermute | solution.py:23
  48.3 0.5 collective-permute-done.9
  48.9 1.2 %collective-permute-start.11 = (f32[80,128]{1,0:T(8,128)S(1)}, f32[80,128]{1,0:T(8,128)S(1)}, u32[]{:S(2)}, u32[]{:S(2)}) collective-permute-start(f32[80,128]{1,0:T(8,128)S(1)} %add_add_fusion.rest_0_), channel_id=1, source_target_pairs={{0,2},{1,3},{2,0},{3,1},{4,6},{5,7},{6,4},{7,5},{8,10},{9,11},{10,... | collective-permute-start | bytes 122888 | tf_op jit(solution)/shard_map/ppermute | solution.py:23
  50.1 2.9 %collective-permute-start.12 = (f32[80,128]{1,0:T(8,128)S(1)}, f32[80,128]{1,0:T(8,128)S(1)}, u32[]{:S(2)}, u32[]{:S(2)}) collective-permute-start(f32[80,128]{1,0:T(8,128)S(1)} %add_add_fusion.rest_0_), channel_id=1, source_target_pairs={{0,4},{1,5},{2,6},{3,7},{4,0},{5,1},{6,2},{7,3},{8,12},{9,13},{10,... | collective-permute-start | bytes 122888 | tf_op jit(solution)/shard_map/ppermute | solution.py:23
  53.5 1.5 %collective-permute-done.12.rest_2_ = f32[80,128]{1,0:T(8,128)S(1)} collective-permute-done((f32[80,128]{1,0:T(8,128)S(1)}, f32[80,128]{1,0:T(8,128)S(1)}, u32[]{:S(2)}, u32[]{:S(2)}) %collective-permute-start.12) | collective-permute-done | bytes 40992 | tf_op jit(solution)/shard_map/ppermute | solution.py:23
  55.0 3.8 %collective-permute-done.13.rest_3_ = f32[80,128]{1,0:T(8,128)S(1)} collective-permute-done((f32[80,128]{1,0:T(8,128)S(1)}, f32[80,128]{1,0:T(8,128)S(1)}, u32[]{:S(2)}, u32[]{:S(2)}) %collective-permute-start.13) | collective-permute-done | bytes 40992 | tf_op jit(solution)/shard_map/ppermute | solution.py:23
  58.8 6.7 %factor_and_basis.1 = f32[4320,128]{1,0:T(8,128)} custom-call(f32[80,128]{1,0:T(8,128)S(1)} %add_add_fusion.rest_0_, f32[80,128]{1,0:T(8,128)S(1)} %collective-permute-done.11.rest_1_, f32[80,128]{1,0:T(8,128)S(1)} %collective-permute-done.12.rest_2_, f32[80,128]{1,0:T(8,128)S(1)} %collective-permute-done.13.rest_3_, ...), custom_call_target="tpu_custom_call" | custom-call | tf_op jit(solution)/shard_map/factor_and_basis/pallas_call | solution.py:360
  (14 shorter events, 1.8 us)
Async XLA Ops:
  1.8 28.6 %collective-permute-start.1 = (bf16[1392,128]{1,0:T(8,128)(2,1)S(1)}, bf16[1392,128]{1,0:T(8,128)(2,1)S(1)}, u32[]{:S(2)}, u32[]{:S(2)}) collective-permute-start(bf16[1392,128]{1,0:T(8,128)(2,1)S(1)} %get-tuple-element.15), channel_id=1, source_target_pairs={{0,4},{1,5},{2,6},{3,7},{4,0},{5,1},{6,2},{7,3},{8,12},{9,13},{10,... | collective-permute-start | bytes 1069064 | tf_op jit(solution)/shard_map/ppermute | solution.py:23
  7.2 23.2 %collective-permute-start.4 = (bf16[1392,128]{1,0:T(8,128)(2,1)S(1)}, bf16[1392,128]{1,0:T(8,128)(2,1)S(1)}, u32[]{:S(2)}, u32[]{:S(2)}) collective-permute-start(bf16[1392,128]{1,0:T(8,128)(2,1)S(1)} %get-tuple-element.18.rest_0_), channel_id=1, source_target_pairs={{0,1},{1,0},{2,3},{3,2},{4,5},{5,4},{6,7},{7,6},{8,9},{9,8},{10,11... | collective-permute-start | bytes 1069064 | tf_op jit(solution)/shard_map/ppermute | solution.py:23
  7.3 29.1 %collective-permute-start = (bf16[1392,128]{1,0:T(8,128)(2,1)S(1)}, bf16[1392,128]{1,0:T(8,128)(2,1)S(1)}, u32[]{:S(2)}, u32[]{:S(2)}) collective-permute-start(bf16[1392,128]{1,0:T(8,128)(2,1)S(1)} %get-tuple-element.14), channel_id=1, source_target_pairs={{0,6},{1,7},{2,4},{3,5},{4,2},{5,3},{6,0},{7,1},{8,14},{9,15},{10,... | collective-permute-start | bytes 1069064 | tf_op jit(solution)/shard_map/ppermute | solution.py:23
  8.7 23.1 %collective-permute-start.2 = (bf16[864,128]{1,0:T(8,128)(2,1)S(1)}, bf16[864,128]{1,0:T(8,128)(2,1)S(1)}, u32[]{:S(2)}, u32[]{:S(2)}) collective-permute-start(bf16[864,128]{1,0:T(8,128)(2,1)S(1)} %get-tuple-element.16), channel_id=1, source_target_pairs={{0,2},{1,3},{2,0},{3,1},{4,6},{5,7},{6,4},{7,5},{8,10},{9,11},{10,... | collective-permute-start | bytes 663560 | tf_op jit(solution)/shard_map/ppermute | solution.py:23
  9.0 25.2 %collective-permute-start.3 = (bf16[864,128]{1,0:T(8,128)(2,1)S(1)}, bf16[864,128]{1,0:T(8,128)(2,1)S(1)}, u32[]{:S(2)}, u32[]{:S(2)}) collective-permute-start(bf16[864,128]{1,0:T(8,128)(2,1)S(1)} %get-tuple-element.17), channel_id=1, source_target_pairs={{0,3},{1,2},{2,1},{3,0},{4,7},{5,6},{6,5},{7,4},{8,11},{9,10},{10,... | collective-permute-start | bytes 663560 | tf_op jit(solution)/shard_map/ppermute | solution.py:23
  30.4 6.7 %collective-permute-start.6 = (bf16[1392,128]{1,0:T(8,128)(2,1)S(1)}, bf16[1392,128]{1,0:T(8,128)(2,1)S(1)}, u32[]{:S(2)}, u32[]{:S(2)}) collective-permute-start(bf16[1392,128]{1,0:T(8,128)(2,1)S(1)} %collective-permute-done.1.rest_0_), channel_id=1, source_target_pairs={{0,1},{1,0},{2,3},{3,2},{4,5},{5,4},{6,7},{7,6},{8,9},{9,8},{10,11... | collective-permute-start | bytes 1069064 | tf_op jit(solution)/shard_map/ppermute | solution.py:23
  36.4 2.0 %collective-permute-start.5 = (bf16[1392,128]{1,0:T(8,128)(2,1)S(1)}, bf16[1392,128]{1,0:T(8,128)(2,1)S(1)}, u32[]{:S(2)}, u32[]{:S(2)}) collective-permute-start(bf16[1392,128]{1,0:T(8,128)(2,1)S(1)} %collective-permute-done.rest_0_), channel_id=1, source_target_pairs={{0,1},{1,0},{2,3},{3,2},{4,5},{5,4},{6,7},{7,6},{8,9},{9,8},{10,11... | collective-permute-start | bytes 1069064 | tf_op jit(solution)/shard_map/ppermute | solution.py:23
  40.5 1.3 %collective-permute-start.7 = (f32[80,128]{1,0:T(8,128)S(1)}, f32[80,128]{1,0:T(8,128)S(1)}, u32[]{:S(2)}, u32[]{:S(2)}) collective-permute-start(f32[80,128]{1,0:T(8,128)S(1)} %get-tuple-element.21), channel_id=1, source_target_pairs={{0,1},{1,0},{2,3},{3,2},{4,5},{5,4},{6,7},{7,6},{8,9},{9,8},{10,11... | collective-permute-start | bytes 122888 | tf_op jit(solution)/shard_map/ppermute | solution.py:23
  41.8 4.9 %collective-permute-start.10 = (f32[80,128]{1,0:T(8,128)S(1)}, f32[80,128]{1,0:T(8,128)S(1)}, u32[]{:S(2)}, u32[]{:S(2)}) collective-permute-start(f32[80,128]{1,0:T(8,128)S(1)} %add.12), channel_id=1, source_target_pairs={{0,24},{8,16},{16,8},{24,0},{1,25},{9,17},{17,9},{25,1},{2,26},{10... | collective-permute-start | bytes 122888 | tf_op jit(solution)/shard_map/ppermute | solution.py:23
  44.3 4.0 %collective-permute-start.8 = (f32[80,128]{1,0:T(8,128)S(1)}, f32[80,128]{1,0:T(8,128)S(1)}, u32[]{:S(2)}, u32[]{:S(2)}) collective-permute-start(f32[80,128]{1,0:T(8,128)S(1)} %add.12), channel_id=1, source_target_pairs={{0,8},{8,0},{16,24},{24,16},{1,9},{9,1},{17,25},{25,17},{2,10},{10... | collective-permute-start | bytes 122888 | tf_op jit(solution)/shard_map/ppermute | solution.py:23
  44.9 4.0 %collective-permute-start.9 = (f32[80,128]{1,0:T(8,128)S(1)}, f32[80,128]{1,0:T(8,128)S(1)}, u32[]{:S(2)}, u32[]{:S(2)}) collective-permute-start(f32[80,128]{1,0:T(8,128)S(1)} %add.12), channel_id=1, source_target_pairs={{0,16},{8,24},{16,0},{24,8},{1,17},{9,25},{17,1},{25,9},{2,18},{10... | collective-permute-start | bytes 122888 | tf_op jit(solution)/shard_map/ppermute | solution.py:23
  48.9 4.6 %collective-permute-start.11 = (f32[80,128]{1,0:T(8,128)S(1)}, f32[80,128]{1,0:T(8,128)S(1)}, u32[]{:S(2)}, u32[]{:S(2)}) collective-permute-start(f32[80,128]{1,0:T(8,128)S(1)} %add_add_fusion.rest_0_), channel_id=1, source_target_pairs={{0,2},{1,3},{2,0},{3,1},{4,6},{5,7},{6,4},{7,5},{8,10},{9,11},{10,... | collective-permute-start | bytes 122888 | tf_op jit(solution)/shard_map/ppermute | solution.py:23
  50.1 4.9 %collective-permute-start.12 = (f32[80,128]{1,0:T(8,128)S(1)}, f32[80,128]{1,0:T(8,128)S(1)}, u32[]{:S(2)}, u32[]{:S(2)}) collective-permute-start(f32[80,128]{1,0:T(8,128)S(1)} %add_add_fusion.rest_0_), channel_id=1, source_target_pairs={{0,4},{1,5},{2,6},{3,7},{4,0},{5,1},{6,2},{7,3},{8,12},{9,13},{10,... | collective-permute-start | bytes 122888 | tf_op jit(solution)/shard_map/ppermute | solution.py:23
  53.0 5.8 %collective-permute-start.13 = (f32[80,128]{1,0:T(8,128)S(1)}, f32[80,128]{1,0:T(8,128)S(1)}, u32[]{:S(2)}, u32[]{:S(2)}) collective-permute-start(f32[80,128]{1,0:T(8,128)S(1)} %add_add_fusion.rest_0_), channel_id=1, source_target_pairs={{0,6},{1,7},{2,4},{3,5},{4,2},{5,3},{6,0},{7,1},{8,14},{9,15},{10,... | collective-permute-start | bytes 122888 | tf_op jit(solution)/shard_map/ppermute | solution.py:23

commit v9 on v7

--- a/solution.py
+++ b/solution.py
@@ -9,7 +9,7 @@
 
 LANES = 128
 TILE = 16
-BLOCK = 32
+BLOCK = 48
 PANEL = 16
 CHUNK = 272
 

time: 65.1 us -> 65.2 us (level)
  no operation moved by 1% of the time
where the time goes in v9:
time: 65.2 us; the launch traced here: 65.1 us
  waiting for transfers between devices  31.5 us (48%)
  starting transfers between devices  17.5 us (27%)
  Pallas kernels  15.3 us (23%)
  between operations  0.72 us (1%)
    ppermute x14, waiting for transfers between devices, swapped(): return lax.ppermute(value, axis, pairs)  31.5 us
    ppermute x14, starting transfers between devices, swapped(): return lax.ppermute(value, axis, pairs)  17.5 us
    pallas_call x5, Pallas kernels, add_rows(): pl.pallas_call(functools.partial(field_kernel, plan, first, last, count),...  7.1 us
    pallas_call x1, Pallas kernels, make_basis(): pl.pallas_call(functools.partial(basis_kernel, plan, scale, len(grams)),...  6.75 us
    pallas_call x1, Pallas kernels, pack(): pl.pallas_call(functools.partial(pack_kernel, plan), out_shape=plan.shape...  1.47 us
  transfers between devices with their start and end apart: 14, of which 8 were waited for; matrix products, arithmetic and copies ran while one was open for 0% of the time, Pallas kernels for 7%

profile of v9, /device:TPU:0, one launch (start us, length us, event | category | flops | bytes accessed | tf_op | source)
XLA Modules:
  0.0 65.1 jit_solution(3784767818262402576)
XLA Ops:
  0.7 1.5 %pack_windows.1 = (bf16[1392,128]{1,0:T(8,128)(2,1)S(1)}, bf16[864,128]{1,0:T(8,128)(2,1)S(1)}, bf16[864,128]{1,0:T(8,128)(2,1)S(1)}, bf16[1392,128]{1,0:T(8,128)(2,1)S(1)}, bf16[1392,128]{1,0:T(8,128)(2,1)S(1)}) custom-call(s32[1]{0:T(128)} %bitcast.band_ref, s32[1]{0:T(128)S(6)} %copy.11.count_ref, s32[1,5]{1,0:T(1,128)} %station_hbm.1, ...), custom_call_target="tpu_custom_call" | custom-call | bytes 4194304 | tf_op jit(solution)/shard_map/pack_windows/pallas_call | solution.py:141
  2.1 4.1 %collective-permute-start.1 = (bf16[1392,128]{1,0:T(8,128)(2,1)S(1)}, bf16[1392,128]{1,0:T(8,128)(2,1)S(1)}, u32[]{:S(2)}, u32[]{:S(2)}) collective-permute-start(bf16[1392,128]{1,0:T(8,128)(2,1)S(1)} %get-tuple-element.15), channel_id=1, source_target_pairs={{0,4},{1,5},{2,6},{3,7},{4,0},{5,1},{6,2},{7,3},{8,12},{9,13},{10,... | collective-permute-start | bytes 1069064 | tf_op jit(solution)/shard_map/ppermute | solution.py:23
  6.3 1.3 %collective-permute-start = (bf16[1392,128]{1,0:T(8,128)(2,1)S(1)}, bf16[1392,128]{1,0:T(8,128)(2,1)S(1)}, u32[]{:S(2)}, u32[]{:S(2)}) collective-permute-start(bf16[1392,128]{1,0:T(8,128)(2,1)S(1)} %get-tuple-element.14), channel_id=1, source_target_pairs={{0,6},{1,7},{2,4},{3,5},{4,2},{5,3},{6,0},{7,1},{8,14},{9,15},{10,... | collective-permute-start | bytes 1069064 | tf_op jit(solution)/shard_map/ppermute | solution.py:23
  7.8 1.3 %collective-permute-start.3 = (bf16[864,128]{1,0:T(8,128)(2,1)S(1)}, bf16[864,128]{1,0:T(8,128)(2,1)S(1)}, u32[]{:S(2)}, u32[]{:S(2)}) collective-permute-start(bf16[864,128]{1,0:T(8,128)(2,1)S(1)} %get-tuple-element.17), channel_id=1, source_target_pairs={{0,3},{1,2},{2,1},{3,0},{4,7},{5,6},{6,5},{7,4},{8,11},{9,10},{10,... | collective-permute-start | bytes 663560 | tf_op jit(solution)/shard_map/ppermute | solution.py:23
  9.2 21.5 %collective-permute-done.1.rest_0_ = bf16[1392,128]{1,0:T(8,128)(2,1)S(1)} collective-permute-done((bf16[1392,128]{1,0:T(8,128)(2,1)S(1)}, bf16[1392,128]{1,0:T(8,128)(2,1)S(1)}, u32[]{:S(2)}, u32[]{:S(2)}) %collective-permute-start.1) | collective-permute-done | bytes 356384 | tf_op jit(solution)/shard_map/ppermute | solution.py:23
  30.7 1.4 %field.4.rest_2_ = f32[8,544,128]{2,1,0:T(8,128)S(1)} custom-call(s32[1]{0:T(128)} %bitcast.band_ref, bf16[1392,128]{1,0:T(8,128)(2,1)S(1)} %get-tuple-element.18.rest_0_, bf16[1392,128]{1,0:T(8,128)(2,1)S(1)} %collective-permute-done.4.rest_1_), custom_call_target="tpu_custom_call" | custom-call | flops 1048576 | bytes 65536 | tf_op jit(solution)/shard_map/field/pallas_call | solution.py:246
  32.2 1.1 %collective-permute-done.3.rest_1_ = bf16[864,128]{1,0:T(8,128)(2,1)S(1)} collective-permute-done((bf16[864,128]{1,0:T(8,128)(2,1)S(1)}, bf16[864,128]{1,0:T(8,128)(2,1)S(1)}, u32[]{:S(2)}, u32[]{:S(2)}) %collective-permute-start.3) | collective-permute-done | bytes 221216 | tf_op jit(solution)/shard_map/ppermute | solution.py:23
  33.3 1.3 %field.5.rest_1_ = f32[8,544,128]{2,1,0:T(8,128)S(1)} custom-call(s32[1]{0:T(128)} %bitcast.band_ref, bf16[864,128]{1,0:T(8,128)(2,1)S(1)} %collective-permute-done.2.rest_0_, bf16[864,128]{1,0:T(8,128)(2,1)S(1)} %collective-permute-done.3.rest_1_, f32[8,544,128]{2,1,0:T(8,128)S(1)} %field.4.rest_2_), custom_call_target="tpu_custom_call", output_to_operand_aliasing={{}: (3, {})} | custom-call | flops 1048576 | bytes 65536 | tf_op jit(solution)/shard_map/field/pallas_call | solution.py:246
  34.6 0.8 %field.6.rest_2_ = f32[8,544,128]{2,1,0:T(8,128)S(1)} custom-call(s32[1]{0:T(128)} %bitcast.band_ref, bf16[1392,128]{1,0:T(8,128)(2,1)S(1)} %collective-permute-done.1.rest_0_, f32[8,544,128]{2,1,0:T(8,128)S(1)} %field.5.rest_1_), custom_call_target="tpu_custom_call", output_to_operand_aliasing={{}: (2, {})} | custom-call | flops 1048576 | bytes 65536 | tf_op jit(solution)/shard_map/field/pallas_call | solution.py:246
  35.4 0.6 collective-permute-start.5
  36.0 1.3 %field.7.rest_1_ = f32[8,544,128]{2,1,0:T(8,128)S(1)} custom-call(s32[1]{0:T(128)} %bitcast.band_ref, bf16[1392,128]{1,0:T(8,128)(2,1)S(1)} %collective-permute-done.rest_0_, bf16[1392,128]{1,0:T(8,128)(2,1)S(1)} %collective-permute-done.6.rest_1_, f32[8,544,128]{2,1,0:T(8,128)S(1)} %field.6.rest_2_), custom_call_target="tpu_custom_call", output_to_operand_aliasing={{}: (3, {})} | custom-call | flops 1048576 | bytes 65536 | tf_op jit(solution)/shard_map/field/pallas_call | solution.py:246
  37.3 2.3 %field_and_gram.1 = (bf16[8,544,256]{2,1,0:T(8,128)(2,1)S(1)}, f32[80,128]{1,0:T(8,128)S(1)}) custom-call(s32[1]{0:T(128)} %bitcast.band_ref, bf16[1392,128]{1,0:T(8,128)(2,1)S(1)} %collective-permute-done.5.rest_0_, f32[8,544,128]{2,1,0:T(8,128)S(1)} %field.7.rest_1_), custom_call_target="tpu_custom_call" | custom-call | flops 1048576 | bytes 65536 | tf_op jit(solution)/shard_map/field_and_gram/pallas_call | solution.py:246
  40.0 0.9 %collective-permute-done.7 = f32[80,128]{1,0:T(8,128)S(1)} collective-permute-done((f32[80,128]{1,0:T(8,128)S(1)}, f32[80,128]{1,0:T(8,128)S(1)}, u32[]{:S(2)}, u32[]{:S(2)}) %collective-permute-start.7) | collective-permute-done | bytes 40992 | tf_op jit(solution)/shard_map/ppermute | solution.py:23
  40.9 1.5 %collective-permute-start.9 = (f32[80,128]{1,0:T(8,128)S(1)}, f32[80,128]{1,0:T(8,128)S(1)}, u32[]{:S(2)}, u32[]{:S(2)}) collective-permute-start(f32[80,128]{1,0:T(8,128)S(1)} %add.12), channel_id=1, source_target_pairs={{0,16},{8,24},{16,0},{24,8},{1,17},{9,25},{17,1},{25,9},{2,18},{10... | collective-permute-start | bytes 122888 | tf_op jit(solution)/shard_map/ppermute | solution.py:23
  42.4 1.4 %collective-permute-start.10 = (f32[80,128]{1,0:T(8,128)S(1)}, f32[80,128]{1,0:T(8,128)S(1)}, u32[]{:S(2)}, u32[]{:S(2)}) collective-permute-start(f32[80,128]{1,0:T(8,128)S(1)} %add.12), channel_id=1, source_target_pairs={{0,24},{8,16},{16,8},{24,0},{1,25},{9,17},{17,9},{25,1},{2,26},{10... | collective-permute-start | bytes 122888 | tf_op jit(solution)/shard_map/ppermute | solution.py:23
  43.9 0.5 collective-permute-start.8
  44.4 0.5 collective-permute-done.9
  44.9 2.6 %collective-permute-done.10 = f32[80,128]{1,0:T(8,128)S(1)} collective-permute-done((f32[80,128]{1,0:T(8,128)S(1)}, f32[80,128]{1,0:T(8,128)S(1)}, u32[]{:S(2)}, u32[]{:S(2)}) %collective-permute-start.10) | collective-permute-done | bytes 40992 | tf_op jit(solution)/shard_map/ppermute | solution.py:23
  47.9 2.6 %collective-permute-start.11 = (f32[80,128]{1,0:T(8,128)S(1)}, f32[80,128]{1,0:T(8,128)S(1)}, u32[]{:S(2)}, u32[]{:S(2)}) collective-permute-start(f32[80,128]{1,0:T(8,128)S(1)} %add_add_fusion.rest_0_), channel_id=1, source_target_pairs={{0,2},{1,3},{2,0},{3,1},{4,6},{5,7},{6,4},{7,5},{8,10},{9,11},{10,... | collective-permute-start | bytes 122888 | tf_op jit(solution)/shard_map/ppermute | solution.py:23
  50.5 2.0 %collective-permute-start.12 = (f32[80,128]{1,0:T(8,128)S(1)}, f32[80,128]{1,0:T(8,128)S(1)}, u32[]{:S(2)}, u32[]{:S(2)}) collective-permute-start(f32[80,128]{1,0:T(8,128)S(1)} %add_add_fusion.rest_0_), channel_id=1, source_target_pairs={{0,4},{1,5},{2,6},{3,7},{4,0},{5,1},{6,2},{7,3},{8,12},{9,13},{10,... | collective-permute-start | bytes 122888 | tf_op jit(solution)/shard_map/ppermute | solution.py:23
  52.5 1.4 %collective-permute-start.13 = (f32[80,128]{1,0:T(8,128)S(1)}, f32[80,128]{1,0:T(8,128)S(1)}, u32[]{:S(2)}, u32[]{:S(2)}) collective-permute-start(f32[80,128]{1,0:T(8,128)S(1)} %add_add_fusion.rest_0_), channel_id=1, source_target_pairs={{0,6},{1,7},{2,4},{3,5},{4,2},{5,3},{6,0},{7,1},{8,14},{9,15},{10,... | collective-permute-start | bytes 122888 | tf_op jit(solution)/shard_map/ppermute | solution.py:23
  53.9 1.9 %collective-permute-done.12.rest_2_ = f32[80,128]{1,0:T(8,128)S(1)} collective-permute-done((f32[80,128]{1,0:T(8,128)S(1)}, f32[80,128]{1,0:T(8,128)S(1)}, u32[]{:S(2)}, u32[]{:S(2)}) %collective-permute-start.12) | collective-permute-done | bytes 40992 | tf_op jit(solution)/shard_map/ppermute | solution.py:23
  55.8 2.5 %collective-permute-done.13.rest_3_ = f32[80,128]{1,0:T(8,128)S(1)} collective-permute-done((f32[80,128]{1,0:T(8,128)S(1)}, f32[80,128]{1,0:T(8,128)S(1)}, u32[]{:S(2)}, u32[]{:S(2)}) %collective-permute-start.13) | collective-permute-done | bytes 40992 | tf_op jit(solution)/shard_map/ppermute | solution.py:23
  58.3 6.8 %factor_and_basis.1 = f32[4320,128]{1,0:T(8,128)} custom-call(f32[80,128]{1,0:T(8,128)S(1)} %add_add_fusion.rest_0_, f32[80,128]{1,0:T(8,128)S(1)} %collective-permute-done.11.rest_1_, f32[80,128]{1,0:T(8,128)S(1)} %collective-permute-done.12.rest_2_, f32[80,128]{1,0:T(8,128)S(1)} %collective-permute-done.13.rest_3_, ...), custom_call_target="tpu_custom_call" | custom-call | tf_op jit(solution)/shard_map/factor_and_basis/pallas_call | solution.py:360
  (13 shorter events, 1.0 us)
Async XLA Ops:
  2.1 28.6 %collective-permute-start.1 = (bf16[1392,128]{1,0:T(8,128)(2,1)S(1)}, bf16[1392,128]{1,0:T(8,128)(2,1)S(1)}, u32[]{:S(2)}, u32[]{:S(2)}) collective-permute-start(bf16[1392,128]{1,0:T(8,128)(2,1)S(1)} %get-tuple-element.15), channel_id=1, source_target_pairs={{0,4},{1,5},{2,6},{3,7},{4,0},{5,1},{6,2},{7,3},{8,12},{9,13},{10,... | collective-permute-start | bytes 1069064 | tf_op jit(solution)/shard_map/ppermute | solution.py:23
  6.3 24.5 %collective-permute-start.4 = (bf16[1392,128]{1,0:T(8,128)(2,1)S(1)}, bf16[1392,128]{1,0:T(8,128)(2,1)S(1)}, u32[]{:S(2)}, u32[]{:S(2)}) collective-permute-start(bf16[1392,128]{1,0:T(8,128)(2,1)S(1)} %get-tuple-element.18.rest_0_), channel_id=1, source_target_pairs={{0,1},{1,0},{2,3},{3,2},{4,5},{5,4},{6,7},{7,6},{8,9},{9,8},{10,11... | collective-permute-start | bytes 1069064 | tf_op jit(solution)/shard_map/ppermute | solution.py:23
  6.3 29.2 %collective-permute-start = (bf16[1392,128]{1,0:T(8,128)(2,1)S(1)}, bf16[1392,128]{1,0:T(8,128)(2,1)S(1)}, u32[]{:S(2)}, u32[]{:S(2)}) collective-permute-start(bf16[1392,128]{1,0:T(8,128)(2,1)S(1)} %get-tuple-element.14), channel_id=1, source_target_pairs={{0,6},{1,7},{2,4},{3,5},{4,2},{5,3},{6,0},{7,1},{8,14},{9,15},{10,... | collective-permute-start | bytes 1069064 | tf_op jit(solution)/shard_map/ppermute | solution.py:23
  7.6 24.6 %collective-permute-start.2 = (bf16[864,128]{1,0:T(8,128)(2,1)S(1)}, bf16[864,128]{1,0:T(8,128)(2,1)S(1)}, u32[]{:S(2)}, u32[]{:S(2)}) collective-permute-start(bf16[864,128]{1,0:T(8,128)(2,1)S(1)} %get-tuple-element.16), channel_id=1, source_target_pairs={{0,2},{1,3},{2,0},{3,1},{4,6},{5,7},{6,4},{7,5},{8,10},{9,11},{10,... | collective-permute-start | bytes 663560 | tf_op jit(solution)/shard_map/ppermute | solution.py:23
  7.8 25.5 %collective-permute-start.3 = (bf16[864,128]{1,0:T(8,128)(2,1)S(1)}, bf16[864,128]{1,0:T(8,128)(2,1)S(1)}, u32[]{:S(2)}, u32[]{:S(2)}) collective-permute-start(bf16[864,128]{1,0:T(8,128)(2,1)S(1)} %get-tuple-element.17), channel_id=1, source_target_pairs={{0,3},{1,2},{2,1},{3,0},{4,7},{5,6},{6,5},{7,4},{8,11},{9,10},{10,... | collective-permute-start | bytes 663560 | tf_op jit(solution)/shard_map/ppermute | solution.py:23
  30.7 5.3 %collective-permute-start.6 = (bf16[1392,128]{1,0:T(8,128)(2,1)S(1)}, bf16[1392,128]{1,0:T(8,128)(2,1)S(1)}, u32[]{:S(2)}, u32[]{:S(2)}) collective-permute-start(bf16[1392,128]{1,0:T(8,128)(2,1)S(1)} %collective-permute-done.1.rest_0_), channel_id=1, source_target_pairs={{0,1},{1,0},{2,3},{3,2},{4,5},{5,4},{6,7},{7,6},{8,9},{9,8},{10,11... | collective-permute-start | bytes 1069064 | tf_op jit(solution)/shard_map/ppermute | solution.py:23
  35.4 1.9 %collective-permute-start.5 = (bf16[1392,128]{1,0:T(8,128)(2,1)S(1)}, bf16[1392,128]{1,0:T(8,128)(2,1)S(1)}, u32[]{:S(2)}, u32[]{:S(2)}) collective-permute-start(bf16[1392,128]{1,0:T(8,128)(2,1)S(1)} %collective-permute-done.rest_0_), channel_id=1, source_target_pairs={{0,1},{1,0},{2,3},{3,2},{4,5},{5,4},{6,7},{7,6},{8,9},{9,8},{10,11... | collective-permute-start | bytes 1069064 | tf_op jit(solution)/shard_map/ppermute | solution.py:23
  39.6 1.3 %collective-permute-start.7 = (f32[80,128]{1,0:T(8,128)S(1)}, f32[80,128]{1,0:T(8,128)S(1)}, u32[]{:S(2)}, u32[]{:S(2)}) collective-permute-start(f32[80,128]{1,0:T(8,128)S(1)} %get-tuple-element.21), channel_id=1, source_target_pairs={{0,1},{1,0},{2,3},{3,2},{4,5},{5,4},{6,7},{7,6},{8,9},{9,8},{10,11... | collective-permute-start | bytes 122888 | tf_op jit(solution)/shard_map/ppermute | solution.py:23
  40.9 4.0 %collective-permute-start.9 = (f32[80,128]{1,0:T(8,128)S(1)}, f32[80,128]{1,0:T(8,128)S(1)}, u32[]{:S(2)}, u32[]{:S(2)}) collective-permute-start(f32[80,128]{1,0:T(8,128)S(1)} %add.12), channel_id=1, source_target_pairs={{0,16},{8,24},{16,0},{24,8},{1,17},{9,25},{17,1},{25,9},{2,18},{10... | collective-permute-start | bytes 122888 | tf_op jit(solution)/shard_map/ppermute | solution.py:23
  42.4 5.0 %collective-permute-start.10 = (f32[80,128]{1,0:T(8,128)S(1)}, f32[80,128]{1,0:T(8,128)S(1)}, u32[]{:S(2)}, u32[]{:S(2)}) collective-permute-start(f32[80,128]{1,0:T(8,128)S(1)} %add.12), channel_id=1, source_target_pairs={{0,24},{8,16},{16,8},{24,0},{1,25},{9,17},{17,9},{25,1},{2,26},{10... | collective-permute-start | bytes 122888 | tf_op jit(solution)/shard_map/ppermute | solution.py:23
  43.9 4.0 %collective-permute-start.8 = (f32[80,128]{1,0:T(8,128)S(1)}, f32[80,128]{1,0:T(8,128)S(1)}, u32[]{:S(2)}, u32[]{:S(2)}) collective-permute-start(f32[80,128]{1,0:T(8,128)S(1)} %add.12), channel_id=1, source_target_pairs={{0,8},{8,0},{16,24},{24,16},{1,9},{9,1},{17,25},{25,17},{2,10},{10... | collective-permute-start | bytes 122888 | tf_op jit(solution)/shard_map/ppermute | solution.py:23
  47.9 6.0 %collective-permute-start.11 = (f32[80,128]{1,0:T(8,128)S(1)}, f32[80,128]{1,0:T(8,128)S(1)}, u32[]{:S(2)}, u32[]{:S(2)}) collective-permute-start(f32[80,128]{1,0:T(8,128)S(1)} %add_add_fusion.rest_0_), channel_id=1, source_target_pairs={{0,2},{1,3},{2,0},{3,1},{4,6},{5,7},{6,4},{7,5},{8,10},{9,11},{10,... | collective-permute-start | bytes 122888 | tf_op jit(solution)/shard_map/ppermute | solution.py:23
  50.5 5.3 %collective-permute-start.12 = (f32[80,128]{1,0:T(8,128)S(1)}, f32[80,128]{1,0:T(8,128)S(1)}, u32[]{:S(2)}, u32[]{:S(2)}) collective-permute-start(f32[80,128]{1,0:T(8,128)S(1)} %add_add_fusion.rest_0_), channel_id=1, source_target_pairs={{0,4},{1,5},{2,6},{3,7},{4,0},{5,1},{6,2},{7,3},{8,12},{9,13},{10,... | collective-permute-start | bytes 122888 | tf_op jit(solution)/shard_map/ppermute | solution.py:23
  52.5 5.8 %collective-permute-start.13 = (f32[80,128]{1,0:T(8,128)S(1)}, f32[80,128]{1,0:T(8,128)S(1)}, u32[]{:S(2)}, u32[]{:S(2)}) collective-permute-start(f32[80,128]{1,0:T(8,128)S(1)} %add_add_fusion.rest_0_), channel_id=1, source_target_pairs={{0,6},{1,7},{2,4},{3,5},{4,2},{5,3},{6,0},{7,1},{8,14},{9,15},{10,... | collective-permute-start | bytes 122888 | tf_op jit(solution)/shard_map/ppermute | solution.py:23
